TPU v7x, 32 devices: a whole 2x2x4 slice. The times are simulated.
32 devices in a mesh: ctx: 16 (over z, x, core), head: 2 (over y).
Axes of the slice: x: 2, y: 2, z: 4, core: 2. Of those that a mesh axis runs over, the one named last changes fastest.
Arguments:
- query: bfloat16 [2, 8192, 1024], P(None, 'ctx', 'head'), may hold values from -12 to 12
- key_in: bfloat16 [2, 8192, 1024], P(None, 'ctx', 'head'), may hold values from -12 to 12
- value: bfloat16 [2, 8192, 1024], P(None, 'ctx', 'head'), may hold values from -6 to 6
- rates: float32 [2, 2, 8192], P(None, 'head', 'ctx'), may hold values from 0.03 to 0.3
- w_in: bfloat16 [2, 512, 512], P('head'), may hold values from -50 to 50
- w_gate: bfloat16 [2, 512, 512], P('head'), may hold values from -50 to 50
- w_out: bfloat16 [2, 512, 512], P('head'), may hold values from -50 to 50
- norm_gain: float32 [2, 512], P('head'), may hold values from 0.1 to 1.9
- proj_weight: bfloat16 [1024, 5120], P('head'), may hold values from -0.25 to 0.25
Outputs:
- mixed: bfloat16 [2, 8192, 5120], P(None, 'ctx', 'head')
- new_in: bfloat16 [2, 512, 512], P('head')
- new_gate: bfloat16 [2, 512, 512], P('head')
- new_out: bfloat16 [2, 512, 512], P('head')
All inputs are finite; a program needn't handle non-finite values.
Results may differ from a plain program's by a relative error of at most 0.015.
Values may be sent and summed in bfloat16 or wider, within the bound.
No kernel may reach another device: no remote copies, remote signals or barrier semaphores. Data moves between devices by JAX's collectives and lax.ppermute only.
A program may use at most 128 MiB of HBM per device.

v0:
```python
import jax
import jax.numpy as jnp
from jax import lax
from jax.sharding import PartitionSpec as P

DH = 512
HID = 512
GROUPS = 2
WINDOW = 1024


def with_halo(value, sides, width):
    for axis, dim in sides:
        peers, length = (lax.axis_size(axis), value.shape[dim])
        up = [(i, (i + 1) % peers) for i in range(peers - 1)]
        down = [(j, i) for i, j in up]
        last = lax.slice_in_dim(value, length - width, length, axis=dim)
        initial = lax.slice_in_dim(value, 0, width, axis=dim)
        before = lax.ppermute(last, axis, up)
        after = lax.ppermute(initial, axis, down)
        value = jnp.concatenate([before, value, after], axis=dim)
    return value


def silu_pair(inputs):
    sigmoid = jax.nn.sigmoid(inputs)
    return (inputs * sigmoid, sigmoid * (1.0 + inputs * (1.0 - sigmoid)))


def local_window(query_rows, extended, first_row, total_rows):
    tok_rows = query_rows.shape[0]
    half_window = WINDOW // 2
    block = min(512, tok_rows)
    key_rows = extended[0]
    value_rows = extended[1]
    row_ids = jnp.arange(block, dtype=jnp.int32)[:, None]
    col_ids = jnp.arange(block + WINDOW, dtype=jnp.int32)[None, :]

    def one_block(block_idx):
        offset = block_idx * block
        scores = jnp.dot(query_rows, key_rows.T, preferred_element_type=jnp.float32) * DH ** (-0.5)
        key_glob = first_row + offset + col_ids - half_window
        valid = (
            (col_ids - row_ids >= 0)
            & (col_ids - row_ids < WINDOW)
            & (key_glob >= 0)
            & (key_glob < total_rows)
        )
        scores = jnp.where(valid, scores, -1e30)
        largest = jnp.max(scores, axis=1, keepdims=True)
        expo = jnp.exp(scores - largest)
        probs = expo / jnp.sum(expo, axis=1, keepdims=True)
        return jnp.dot(probs.astype(jnp.bfloat16), value_rows, preferred_element_type=jnp.float32)

    outputs = lax.map(one_block, jnp.arange(tok_rows // block, dtype=jnp.int32))
    return outputs.reshape(tok_rows, query_rows.shape[1])


def column_scale(before, square_sums):
    kept = jnp.sqrt(jnp.sum(before * before, axis=0, keepdims=True))
    return kept / jnp.sqrt(square_sums[None, :] + 1e-06)


def local(query, key_in, value, rates, w_in, w_gate, w_out, norm_gain, proj_weight):
    tok_rows = query.shape[1]
    ctx_count = lax.axis_size("ctx")
    total_rows = tok_rows * ctx_count
    first_row = lax.axis_index("ctx") * tok_rows
    half_window = WINDOW // 2
    scale_in = DH ** (-0.5)
    scale_out = HID ** (-0.5)
    state = (
        w_in[0].astype(jnp.float32),
        w_gate[0].astype(jnp.float32),
        w_out[0].astype(jnp.float32),
    )
    gain_row = norm_gain[0]
    stacked = jnp.stack((key_in, value), axis=0)
    mixed_list = []
    for group_idx in range(GROUPS):
        query_rows = query[group_idx]
        key_rows = key_in[group_idx]
        value_rows = value[group_idx]
        rate_row = rates[group_idx, 0]
        extended = with_halo(stacked[:, group_idx], (("ctx", 1),), half_window)
        window = local_window(query_rows, extended, first_row, total_rows)
        bf_in = state[0].astype(jnp.bfloat16)
        bf_gate = state[1].astype(jnp.bfloat16)
        bf_out = state[2].astype(jnp.bfloat16)
        first_pre = jnp.dot(query_rows, bf_in, preferred_element_type=jnp.float32) * scale_in
        gate_pre = jnp.dot(query_rows, bf_gate, preferred_element_type=jnp.float32) * scale_in
        first_act, unused = silu_pair(first_pre)
        hidden_q = (first_act * gate_pre).astype(jnp.bfloat16)
        ttt_out = jnp.dot(hidden_q, bf_out, preferred_element_type=jnp.float32) * scale_out
        normed = (
            ttt_out
            * lax.rsqrt(jnp.mean(ttt_out * ttt_out, axis=1, keepdims=True) + 1e-06)
            * gain_row[None, :]
        )
        head_out = (normed + window).astype(jnp.bfloat16)
        key_first = jnp.dot(key_rows, bf_in, preferred_element_type=jnp.float32) * scale_in
        key_gate = jnp.dot(key_rows, bf_gate, preferred_element_type=jnp.float32) * scale_in
        key_act, key_slope = silu_pair(key_first)
        hidden_k = (key_act * key_gate).astype(jnp.bfloat16)
        scaled = (rate_row[:, None] * value_rows.astype(jnp.float32)).astype(jnp.bfloat16)
        grad_out = -scale_out * jnp.dot(hidden_k.T, scaled, preferred_element_type=jnp.float32)
        back = -scale_out * jnp.dot(scaled, bf_out.T, preferred_element_type=jnp.float32)
        delta_in = (back * key_gate * key_slope).astype(jnp.bfloat16)
        delta_gate = (back * key_act).astype(jnp.bfloat16)
        grad_in = scale_in * jnp.dot(key_rows.T, delta_in, preferred_element_type=jnp.float32)
        grad_gate = scale_in * jnp.dot(key_rows.T, delta_gate, preferred_element_type=jnp.float32)
        terms = jnp.dot(head_out, proj_weight, preferred_element_type=jnp.float32)
        mixed_rows = lax.psum_scatter(
            terms.astype(jnp.bfloat16), "head", scatter_dimension=1, tiled=True
        )
        mixed_list.append(mixed_rows)
        grads = lax.psum((grad_in, grad_gate, grad_out), "ctx")
        next_state = []
        for before, summed in zip(state, grads):
            changed = before - summed
            next_state.append(changed * column_scale(before, jnp.sum(changed * changed, axis=0)))
        state = tuple(next_state)
    mixed = jnp.stack(mixed_list, axis=0)
    return (
        mixed,
        state[0][None].astype(jnp.bfloat16),
        state[1][None].astype(jnp.bfloat16),
        state[2][None].astype(jnp.bfloat16),
    )


def solution(mesh):
    return jax.shard_map(
        local,
        mesh=mesh,
        in_specs=(
            P(None, "ctx", "head"),
            P(None, "ctx", "head"),
            P(None, "ctx", "head"),
            P(None, "head", "ctx"),
            P("head", None, None),
            P("head", None, None),
            P("head", None, None),
            P("head", None),
            P("head", None),
        ),
        out_specs=(
            P(None, "ctx", "head"),
            P("head", None, None),
            P("head", None, None),
            P("head", None, None),
        ),
        check_vma=False,
    )
```

profile of v0, /device:TPU:14, one launch (start us, length us, event | category | flops | bytes accessed | tf_op | source)
XLA Modules:
  0.0 298.4 jit_solution(915545992891596372)
XLA Ops:
  8.1 3.3 %fusion.38 = (bf16[2,512,512]{2,1,0:T(8,128)(2,1)}, bf16[2,512,512]{2,1,0:T(8,128)(2,1)}) fusion(bf16[1,2,512,512]{3,2,1,0:T(8,128)(2,1)} %bitcast.161, bf16[1,2,512,512]{3,2,1,0:T(8,128)(2,1)} %bitcast.164), kind=kLoop, calls=%fused_computation.80 | loop fusion | flops 1048576 | bytes 4194304 | tf_op jit(solution)/shard_map/squeeze | solution.py:85
  11.3 2.0 collective-permute-start
  13.4 3.6 %collective-permute-start.1 = (bf16[2,512,512]{2,1,0:T(8,128)(2,1)}, bf16[2,512,512]{2,1,0:T(8,128)(2,1)}, u32[]{:S(2)}, u32[]{:S(2)}) collective-permute-start(bf16[2,512,512]{2,1,0:T(8,128)(2,1)} %get-tuple-element.74), channel_id=1, source_target_pairs={{2,0},{4,2},{6,4},{8,6},{10,8},{12,10},{14,12},{16,14},{18,16},{20... | collective-permute-start | bytes 3145736 | tf_op jit(solution)/shard_map/ppermute | solution.py:20
  31.1 2.2 fusion.30
  33.9 13.3 %collective-permute-done = bf16[2,512,512]{2,1,0:T(8,128)(2,1)} collective-permute-done((bf16[2,512,512]{2,1,0:T(8,128)(2,1)}, bf16[2,512,512]{2,1,0:T(8,128)(2,1)}, u32[]{:S(2)}, u32[]{:S(2)}) %collective-permute-start) | collective-permute-done | bytes 1048608 | tf_op jit(solution)/shard_map/ppermute | solution.py:19
  47.2 2.0 pad_maximum_fusion.1
  50.9 3.5 %fusion.128 = (f32[512]{0:T(512)S(1)}, f32[512,1536]{0,1:T(8,128)}) fusion(bf16[2,512,512]{2,1,0:T(8,128)(2,1)S(1)} %copy-done.13, bf16[2,1536,512]{2,1,0:T(8,128)(2,1)S(1)} %pad_maximum_fusion.1, pred[1536]{0:T(1024)(128)(4,1)S(1)} %get-tuple-element.85, pred[1536]{0:T(1024)(128)(4,1)S(1)} %get-tuple-element.86), kind=kOutput, calls=%fused_computation.197 | convolution fusion | flops 812383744 | bytes 5249024 | tf_op jit(solution)/shard_map/while/body/eval_jaxpr/dot_general | solution.py:41
  54.3 75.2 %all-reduce.7.cloned.1.call-done = (f32[512,512]{0,1:T(8,128)}, f32[512,512]{0,1:T(8,128)}, f32[512,512]{0,1:T(8,128)}) async-done(((f32[512,512]{0,1:T(8,128)}, f32[512,512]{0,1:T(8,128)}, f32[512,512]{0,1:T(8,128)}), (f32[512,512]{0,1:T(8,128)}, f32[512,512]{0,1:T(8,128)}, f32[512,512]{0,1:T(8,128)})) %all-reduce.7.cloned.1.call-update) | async-done | bytes 3145744 | tf_op jit(solution)/shard_map/psum | solution.py:117
  129.6 2.5 multiply_reduce_fusion.7
  139.5 2.4 fusion.9
  141.9 10.8 %convolution_convert_fusion.1 = bf16[512,5120]{1,0:T(8,128)(2,1)} fusion(bf16[512,5120]{1,0:T(8,128)(2,1)} %param.17, bf16[2,1536,512]{2,1,0:T(8,128)(2,1)} %copy-done.7, f32[512,1536]{0,1:T(8,128)} %get-tuple-element.84, f32[512]{0:T(512)S(1)} %fusion.9, f32[512]{0:T(512)S(1)} %get-tuple-element.83, f32[512,512]{0,1:T(8,128)} %copy-done.6, ...), kind=kOutput, calls=%fused_computation.1 | convolution fusion | flops 3495690240 | bytes 16261120 | tf_op jit(solution)/shard_map/dot_general | solution.py:112
  152.8 2.1 collective-permute-start.2
  154.8 3.6 %collective-permute-start.3 = (bf16[2,512,512]{2,1,0:T(8,128)(2,1)}, bf16[2,512,512]{2,1,0:T(8,128)(2,1)S(1)}, u32[]{:S(2)}, u32[]{:S(2)}) collective-permute-start(bf16[2,512,512]{2,1,0:T(8,128)(2,1)} %get-tuple-element.75), channel_id=1, source_target_pairs={{2,0},{4,2},{6,4},{8,6},{10,8},{12,10},{14,12},{16,14},{18,16},{20... | collective-permute-start | bytes 3145736 | tf_op jit(solution)/shard_map/ppermute | solution.py:20
  158.5 24.9 %collective-permute-done.2 = bf16[2,512,512]{2,1,0:T(8,128)(2,1)S(1)} collective-permute-done((bf16[2,512,512]{2,1,0:T(8,128)(2,1)}, bf16[2,512,512]{2,1,0:T(8,128)(2,1)S(1)}, u32[]{:S(2)}, u32[]{:S(2)}) %collective-permute-start.2) | collective-permute-done | bytes 1048608 | tf_op jit(solution)/shard_map/ppermute | solution.py:19
  190.1 3.3 %fusion.29 = f32[512,512]{0,1:T(8,128)} fusion(f32[512,512]{0,1:T(8,128)} %fusion.20, bf16[2,512,512]{2,1,0:T(8,128)(2,1)} %param.9, f32[512,512]{0,1:T(8,128)S(1)} %get-tuple-element.89, f32[512]{0:T(512)S(1)} %rsqrt_multiply_fusion.5, f32[512,512]{0,1:T(8,128)S(1)} %get-tuple-element.69, f32[512]{0:T(512)S(1)} %rsqrt_multiply_fusion.4), kind=kOutput, calls=%fused_computation.71 | convolution fusion | flops 539754496 | bytes 4722688 | tf_op jit(solution)/shard_map/dot_general | solution.py:94
  193.4 2.5 copy.25
  197.4 10.7 %convolution_convert_fusion = bf16[512,5120]{1,0:T(8,128)(2,1)} fusion(bf16[512,5120]{1,0:T(8,128)(2,1)} %param.17, bf16[2,1536,512]{2,1,0:T(8,128)(2,1)} %copy-done.8, f32[512,1536]{0,1:T(8,128)} %copy-done.9, f32[512]{0:T(512)S(1)} %fusion.10, f32[512]{0:T(512)S(1)} %get-tuple-element.81, f32[512,512]{0,1:T(8,128)} %fusion.29, ...), kind=kOutput, calls=%fused_computation | convolution fusion | flops 3495690240 | bytes 16261120 | tf_op jit(solution)/shard_map/dot_general | solution.py:112
  208.1 37.6 %all-reduce.5.cloned.1.call-done = (f32[512,512]{0,1:T(8,128)}, f32[512,512]{0,1:T(8,128)}, f32[512,512]{0,1:T(8,128)}) async-done(((f32[512,512]{0,1:T(8,128)}, f32[512,512]{0,1:T(8,128)}, f32[512,512]{0,1:T(8,128)}), (f32[512,512]{0,1:T(8,128)}, f32[512,512]{0,1:T(8,128)}, f32[512,512]{0,1:T(8,128)})) %all-reduce.5.cloned.1.call-update) | async-done | bytes 3145744 | tf_op jit(solution)/shard_map/psum | solution.py:117
  247.3 2.2 fusion.55
  249.6 2.0 copy.30
  253.3 2.2 fusion.54
  255.6 2.0 copy.29
  259.2 26.3 %reduce-scatter.5.cloned.1.call-done = bf16[512,2560]{1,0:T(8,128)(2,1)} async-done(((bf16[512,5120]{1,0:T(8,128)(2,1)}), bf16[512,2560]{1,0:T(8,128)(2,1)}) %reduce-scatter.5.cloned.1.call-update) | async-done | bytes 2621456 | tf_op jit(solution)/shard_map/reduce_scatter | solution.py:113
  285.6 5.4 %pad_maximum_fusion = bf16[2,512,2560]{2,1,0:T(8,128)(2,1)} fusion(bf16[1,512,2560]{2,1,0:T(8,128)(2,1)} %bitcast.163, bf16[1,512,2560]{2,1,0:T(8,128)(2,1)} %bitcast.162), kind=kLoop, calls=%fused_computation.2 | loop fusion | flops 2621440 | bytes 10485760 | tf_op jit(solution)/shard_map/stack | solution.py:123
  (97 shorter events, 36.7 us)
Async XLA Ops:
  8.0 9.1 %copy-start = (bf16[2,512,512]{2,1,0:T(8,128)(2,1)S(1)}, bf16[2,512,512]{2,1,0:T(8,128)(2,1)}, u32[]{:S(2)}) copy-start(bf16[2,512,512]{2,1,0:T(8,128)(2,1)} %param.10) | copy-start | bytes 3145732
  8.0 9.0 %copy-start.20 = (f32[2,1,512]{2,1,0:T(1,128)S(1)}, f32[2,1,512]{2,1,0:T(1,128)}, u32[]{:S(2)}) copy-start(f32[2,1,512]{2,1,0:T(1,128)} %param.12) | copy-start | bytes 12292
  8.0 9.1 %copy-start.4 = (bf16[1,512,512]{2,1,0:T(8,128)(2,1)S(1)}, bf16[1,512,512]{2,1,0:T(8,128)(2,1)}, u32[]{:S(2)}) copy-start(bf16[1,512,512]{2,1,0:T(8,128)(2,1)} %param.13) | copy-start | bytes 1572868
  8.0 121.5 %all-reduce.7.cloned.1.call-start = ((), (), s32[]{:S(2)}) async-start(), calls=%async_computation.5 | async-start | bytes 6291456 | tf_op jit(solution)/shard_map/psum | solution.py:117
  8.1 9.5 %copy-start.3 = (bf16[1,512,512]{2,1,0:T(8,128)(2,1)S(1)}, bf16[1,512,512]{2,1,0:T(8,128)(2,1)}, u32[]{:S(2)}) copy-start(bf16[1,512,512]{2,1,0:T(8,128)(2,1)} %param.14) | copy-start | bytes 1572868
  11.3 6.7 %copy-start.10 = (bf16[2,512,512]{2,1,0:T(8,128)(2,1)S(1)}, bf16[2,512,512]{2,1,0:T(8,128)(2,1)}, u32[]{:S(2)}) copy-start(bf16[2,512,512]{2,1,0:T(8,128)(2,1)} %param.11) | copy-start | bytes 3145732
  11.3 6.8 %copy-start.15 = (bf16[1,512,512]{2,1,0:T(8,128)(2,1)S(1)}, bf16[1,512,512]{2,1,0:T(8,128)(2,1)}, u32[]{:S(2)}) copy-start(bf16[1,512,512]{2,1,0:T(8,128)(2,1)} %param.15) | copy-start | bytes 1572868
  11.3 35.9 %collective-permute-start = (bf16[2,512,512]{2,1,0:T(8,128)(2,1)}, bf16[2,512,512]{2,1,0:T(8,128)(2,1)}, u32[]{:S(2)}, u32[]{:S(2)}) collective-permute-start(bf16[2,512,512]{2,1,0:T(8,128)(2,1)} %get-tuple-element.74), channel_id=1, source_target_pairs={{0,2},{2,4},{4,6},{6,8},{8,10},{10,12},{12,14},{14,16},{16,18},{18... | collective-permute-start | bytes 3145736 | tf_op jit(solution)/shard_map/ppermute | solution.py:19
  13.4 33.8 %collective-permute-start.1 = (bf16[2,512,512]{2,1,0:T(8,128)(2,1)}, bf16[2,512,512]{2,1,0:T(8,128)(2,1)}, u32[]{:S(2)}, u32[]{:S(2)}) collective-permute-start(bf16[2,512,512]{2,1,0:T(8,128)(2,1)} %get-tuple-element.74), channel_id=1, source_target_pairs={{2,0},{4,2},{6,4},{8,6},{10,8},{12,10},{14,12},{16,14},{18,16},{20... | collective-permute-start | bytes 3145736 | tf_op jit(solution)/shard_map/ppermute | solution.py:20
  23.4 3.1 %copy-start.12 = (bf16[2,512,512]{2,1,0:T(8,128)(2,1)S(1)}, bf16[2,512,512]{2,1,0:T(8,128)(2,1)}, u32[]{:S(2)}) copy-start(bf16[2,512,512]{2,1,0:T(8,128)(2,1)} %param.9) | copy-start | bytes 3145732
  23.4 222.3 %all-reduce.5.cloned.1.call-start = ((), (), s32[]{:S(2)}) async-start(), calls=%async_computation.4 | async-start | bytes 6291456 | tf_op jit(solution)/shard_map/psum | solution.py:117
  27.0 4.1 %copy-start.17 = (bf16[1,512,512]{2,1,0:T(8,128)(2,1)S(1)}, bf16[1,512,512]{2,1,0:T(8,128)(2,1)}, u32[]{:S(2)}) copy-start(bf16[1,512,512]{2,1,0:T(8,128)(2,1)} %param.15) | copy-start | bytes 1572868
  33.3 15.9 %copy-start.6 = (f32[512,512]{0,1:T(8,128)}, f32[512,512]{0,1:T(8,128)S(1)}, u32[]{:S(2)}) copy-start(f32[512,512]{0,1:T(8,128)S(1)} %fusion.30) | copy-start | bytes 3145732
  33.9 17.0 %copy-start.13 = (bf16[2,512,512]{2,1,0:T(8,128)(2,1)S(1)}, bf16[2,512,512]{2,1,0:T(8,128)(2,1)}, u32[]{:S(2)}) copy-start(bf16[2,512,512]{2,1,0:T(8,128)(2,1)} %param.9) | copy-start | bytes 3145732
  54.3 77.8 %copy-start.1 = (bf16[2,512,512]{2,1,0:T(8,128)(2,1)S(1)}, bf16[2,512,512]{2,1,0:T(8,128)(2,1)}, u32[]{:S(2)}) copy-start(bf16[2,512,512]{2,1,0:T(8,128)(2,1)} %param.10) | copy-start | bytes 3145732
  129.6 3.0 %copy-start.18 = (bf16[1,512,512]{1,2,0:T(8,128)(2,1)S(1)}, bf16[1,512,512]{1,2,0:T(8,128)(2,1)}, u32[]{:S(2)}) copy-start(bf16[1,512,512]{1,2,0:T(8,128)(2,1)} %copy.13) | copy-start | bytes 1572868
  129.6 3.0 %copy-start.19 = (f32[512,512]{0,1:T(8,128)S(1)}, f32[512,512]{0,1:T(8,128)}, u32[]{:S(2)}) copy-start(f32[512,512]{0,1:T(8,128)} %get-tuple-element.65) | copy-start | bytes 3145732
  139.2 2.6 copy-start.21
  139.3 120.0 %reduce-scatter.3.cloned.1.call-start = ((), (), s32[]{:S(2)}) async-start(), calls=%async_computation.2 | async-start | bytes 7864320 | tf_op jit(solution)/shard_map/reduce_scatter | solution.py:113
  152.7 132.9 %reduce-scatter.5.cloned.1.call-start = ((), (), s32[]{:S(2)}) async-start(), calls=%async_computation.3 | async-start | bytes 7864320 | tf_op jit(solution)/shard_map/reduce_scatter | solution.py:113
  152.8 32.0 %copy-start.14 = (bf16[2,512,512]{2,1,0:T(8,128)(2,1)S(1)}, bf16[2,512,512]{2,1,0:T(8,128)(2,1)}, u32[]{:S(2)}) copy-start(bf16[2,512,512]{2,1,0:T(8,128)(2,1)} %param.9) | copy-start | bytes 3145732
  152.8 30.6 %collective-permute-start.2 = (bf16[2,512,512]{2,1,0:T(8,128)(2,1)}, bf16[2,512,512]{2,1,0:T(8,128)(2,1)S(1)}, u32[]{:S(2)}, u32[]{:S(2)}) collective-permute-start(bf16[2,512,512]{2,1,0:T(8,128)(2,1)} %get-tuple-element.75), channel_id=1, source_target_pairs={{0,2},{2,4},{4,6},{6,8},{8,10},{10,12},{12,14},{14,16},{16,18},{18... | collective-permute-start | bytes 3145736 | tf_op jit(solution)/shard_map/ppermute | solution.py:19
  154.8 28.5 %collective-permute-start.3 = (bf16[2,512,512]{2,1,0:T(8,128)(2,1)}, bf16[2,512,512]{2,1,0:T(8,128)(2,1)S(1)}, u32[]{:S(2)}, u32[]{:S(2)}) collective-permute-start(bf16[2,512,512]{2,1,0:T(8,128)(2,1)} %get-tuple-element.75), channel_id=1, source_target_pairs={{2,0},{4,2},{6,4},{8,6},{10,8},{12,10},{14,12},{16,14},{18,16},{20... | collective-permute-start | bytes 3145736 | tf_op jit(solution)/shard_map/ppermute | solution.py:20
  251.6 6.0 %copy-start.5 = (f32[512,512]{0,1:T(8,128)S(1)}, f32[512,512]{0,1:T(8,128)}, u32[]{:S(2)}) copy-start(f32[512,512]{0,1:T(8,128)} %get-tuple-element.54) | copy-start | bytes 3145732
  (6 other events, 8.7 us)
Sparse Core Ops, SparseCore 0:
  23.6 105.9 all-reduce.6
  139.4 106.2 all-reduce.4
Sparse Core Ops, SparseCore 1:
  152.8 64.2 reduce-scatter.2
  219.8 65.7 reduce-scatter.4
where the time goes:
time: 302 us; the launch traced here: 298 us
  waiting for transfers between devices  177 us (59%)
  matrix products  46.1 us (15%)
  other arithmetic  29.2 us (10%)
  local copies, waits for them, and re-layouts  18 us (6%)
  between operations  15.9 us (5%)
  starting transfers between devices  11.7 us (4%)
    psum x2, waiting for transfers between devices, local(): grads = lax.psum((grad_in, grad_gate, grad_out), 'ctx')  113 us
    ppermute x2, waiting for transfers between devices, with_halo(): before = lax.ppermute(last, axis, up)  38.2 us
    reduce_scatter x2, waiting for transfers between devices, local(): lax.psum_scatter(terms.astype(jnp.bfloat16), 'head', scatter_dimension=1,...  26.3 us
    dot_general x2, matrix products, local(): terms = jnp.dot(head_out, proj_weight, preferred_element_type=jnp.float32)  21.5 us
    unnamed x50, local copies, waits for them, and re-layouts  12.5 us
    ppermute x2, starting transfers between devices, with_halo(): after = lax.ppermute(initial, axis, down)  7.29 us
  transfers between devices with their start and end apart: 8, of which 5 were waited for; matrix products, arithmetic and copies ran while one was open for 24% of the time, Pallas kernels for 0%

commit v1 on v0

v1 whole, which is shorter than its diff:
```python
import functools

import jax
import jax.numpy as jnp
from jax import lax
from jax.experimental import pallas as pl
from jax.experimental.pallas import tpu as pltpu
from jax.sharding import PartitionSpec as P

GROUPS = 2
WINDOW = 1024
F32 = jnp.float32
BF16 = jnp.bfloat16
NN = (((1,), (0,)), ((), ()))
NT = (((1,), (1,)), ((), ()))
TN = (((0,), (0,)), ((), ()))


def dot(lhs, rhs, dims):
    return lax.dot_general(lhs, rhs, dims, preferred_element_type=F32)


def whole(shape):
    zeros = (0,) * len(shape)
    return pl.BlockSpec(shape, lambda i, *refs: zeros)


def of_group(group, shape):
    block = (group,) + (0,) * len(shape)
    return pl.BlockSpec((None,) + shape, lambda i, *refs: block)


ANY = pl.BlockSpec(memory_space=pl.ANY)


def key_side(core, keys, values, rate_col, weights, group, gathered):
    tokens, width = keys.shape[1:]
    hidden = width
    rows = 3 * hidden
    half = rows // 2
    step = min(256, tokens)
    scale = width ** (-0.5)
    first = NT if gathered else NN
    second = NN if gathered else NT

    def kernel(core_ref, k_ref, v_ref, rate_ref, *refs):
        if gathered:
            mine, other, send_ref, keep_ref, w_ref, hk, sc, d1, d3, grad, sems = refs
            c = core_ref[0]
            copies = (
                pltpu.make_async_copy(mine, w_ref.at[pl.ds(c * half, half)], sems.at[0]),
                pltpu.make_async_copy(other, w_ref.at[pl.ds((1 - c) * half, half)], sems.at[1]),
            )
            for copy in copies:
                copy.start()
            for copy in copies:
                copy.wait()
            w1, w3, w2 = (w_ref.at[pl.ds(n * hidden, hidden)] for n in range(3))
        else:
            w1, w3, w2, send_ref, keep_ref, hk, sc, d1, d3, grad = refs
            c = core_ref[0]

        def forward(n, carry):
            at = pl.ds(n * step, step)
            k = k_ref[at]
            f1 = dot(k, w1[...], first) * scale
            f3 = dot(k, w3[...], first) * scale
            scaled = (rate_ref[at] * v_ref[at].astype(F32)).astype(BF16)
            sc[at] = scaled
            back = dot(scaled, w2[...], second) * (-scale)
            sig = jax.nn.sigmoid(f1)
            act = f1 * sig
            slope = sig * (1.0 + f1 * (1.0 - sig))
            hk[at] = (act * f3).astype(BF16)
            d1[at] = (back * f3 * slope).astype(BF16)
            d3[at] = (back * act).astype(BF16)
            return carry

        lax.fori_loop(0, tokens // step, forward, 0)
        for n, (lhs, rhs, by) in enumerate(((d1, k_ref, scale), (d3, k_ref, scale), (sc, hk, -scale))):
            grad[pl.ds(n * hidden, hidden)] = dot(lhs[...], rhs[...], TN) * by
        send_ref[...] = grad[pl.ds(pl.multiple_of((1 - c) * half, 16), half)].astype(BF16)
        keep_ref[...] = grad[pl.ds(pl.multiple_of(c * half, 16), half)]

    act_scratch = [pltpu.VMEM((tokens, hidden), BF16) for _ in range(4)]
    scratch = act_scratch + [pltpu.VMEM((rows, width), F32)]
    if gathered:
        w_specs = [ANY, ANY]
        scratch = [pltpu.VMEM((rows, width), BF16)] + scratch + [pltpu.SemaphoreType.DMA((2,))]
    else:
        w_specs = [of_group(0, (hidden, width))] * 3
    return pl.pallas_call(
        kernel,
        grid_spec=pltpu.PrefetchScalarGridSpec(
            num_scalar_prefetch=1,
            grid=(1,),
            in_specs=[
                of_group(group, (tokens, width)),
                of_group(group, (tokens, width)),
                of_group(group, (tokens, 1)),
                *w_specs,
            ],
            out_specs=[whole((half, width)), whole((half, width))],
            scratch_shapes=scratch,
        ),
        out_shape=[
            jax.ShapeDtypeStruct((half, width), BF16),
            jax.ShapeDtypeStruct((half, width), F32),
        ],
        name="key_side",
    )(core, keys, values, rate_col, *weights)


def window_side(bounds, query, keys, values, before_k, before_v, after_k, after_v, group):
    tokens, width = query.shape[1:]
    reach = WINDOW // 2
    total = tokens + WINDOW
    step = min(256, tokens)
    span = step + WINDOW
    scale = width ** (-0.5)

    def kernel(bounds_ref, q_ref, k_ref, v_ref, bk, bv, ak, av, out_ref, k_all, v_all, sems):
        at = (pl.ds(0, reach), pl.ds(reach, tokens), pl.ds(reach + tokens, reach))
        parts = []
        for n, (source, target, place) in enumerate(
            (
                (bk.at[group], k_all, at[0]),
                (k_ref.at[group], k_all, at[1]),
                (ak.at[group], k_all, at[2]),
                (bv.at[group], v_all, at[0]),
                (v_ref.at[group], v_all, at[1]),
                (av.at[group], v_all, at[2]),
            )
        ):
            parts.append(pltpu.make_async_copy(source, target.at[place], sems.at[n]))
        for part in parts:
            part.start()
        for part in parts:
            part.wait()
        lowest, highest = bounds_ref[0], bounds_ref[1]

        def block(n, carry):
            start = n * step
            q = q_ref[pl.ds(start, step)]
            scores = dot(q, k_all[pl.ds(start, span)], NT) * scale
            row = lax.broadcasted_iota(jnp.int32, (step, span), 0)
            col = lax.broadcasted_iota(jnp.int32, (step, span), 1)
            valid = (
                (col >= row)
                & (col < row + WINDOW)
                & (col >= lowest - start)
                & (col < highest - start)
            )
            scores = jnp.where(valid, scores, -1e30)
            largest = jnp.max(scores, axis=1, keepdims=True)
            expo = jnp.exp(scores - largest)
            norm = jnp.sum(expo, axis=1, keepdims=True)
            mixed = dot(expo.astype(BF16), v_all[pl.ds(start, span)], NN)
            out_ref[pl.ds(start, step)] = mixed / norm
            return carry

        lax.fori_loop(0, tokens // step, block, 0)

    return pl.pallas_call(
        kernel,
        grid_spec=pltpu.PrefetchScalarGridSpec(
            num_scalar_prefetch=1,
            grid=(1,),
            in_specs=[of_group(group, (tokens, width))] + [ANY] * 6,
            out_specs=whole((tokens, width)),
            scratch_shapes=[
                pltpu.VMEM((total, width), BF16),
                pltpu.VMEM((total, width), BF16),
                pltpu.SemaphoreType.DMA((6,)),
            ],
        ),
        out_shape=jax.ShapeDtypeStruct((tokens, width), F32),
        name="window_side",
    )(bounds, query, keys, values, before_k, before_v, after_k, after_v)


def query_side(core, query, gain, window, weights, group, gathered):
    tokens, width = query.shape[1:]
    hidden = width
    rows = 3 * hidden
    half = rows // 2
    step = min(256, tokens)
    scale = width ** (-0.5)
    first = NT if gathered else NN

    def kernel(core_ref, q_ref, gain_ref, window_ref, *refs):
        if gathered:
            mine, other, out_ref, w_ref, sems = refs
            c = core_ref[0]
            copies = (
                pltpu.make_async_copy(mine, w_ref.at[pl.ds(c * half, half)], sems.at[0]),
                pltpu.make_async_copy(other, w_ref.at[pl.ds((1 - c) * half, half)], sems.at[1]),
            )
            for copy in copies:
                copy.start()
            for copy in copies:
                copy.wait()
            w1, w3, w2 = (w_ref.at[pl.ds(n * hidden, hidden)] for n in range(3))
        else:
            w1, w3, w2, out_ref = refs

        def block(n, carry):
            at = pl.ds(n * step, step)
            q = q_ref[at]
            g1 = dot(q, w1[...], first) * scale
            g3 = dot(q, w3[...], first) * scale
            hq = (g1 * jax.nn.sigmoid(g1) * g3).astype(BF16)
            ttt = dot(hq, w2[...], first) * scale
            mean = jnp.mean(ttt * ttt, axis=1, keepdims=True)
            normed = ttt * lax.rsqrt(mean + 1e-06) * gain_ref[...]
            out_ref[at] = (normed + window_ref[at]).astype(BF16)
            return carry

        lax.fori_loop(0, tokens // step, block, 0)

    if gathered:
        w_specs = [ANY, ANY]
        scratch = [pltpu.VMEM((rows, width), BF16), pltpu.SemaphoreType.DMA((2,))]
    else:
        w_specs = [of_group(0, (hidden, width))] * 3
        scratch = []
    return pl.pallas_call(
        kernel,
        grid_spec=pltpu.PrefetchScalarGridSpec(
            num_scalar_prefetch=1,
            grid=(1,),
            in_specs=[
                of_group(group, (tokens, width)),
                whole((1, width)),
                whole((tokens, width)),
                *w_specs,
            ],
            out_specs=whole((tokens, width)),
            scratch_shapes=scratch,
        ),
        out_shape=jax.ShapeDtypeStruct((tokens, width), BF16),
        name="query_side",
    )(core, query, gain, window, *weights)


def project(place, heads, mine, near, far, group, mixed):
    tokens, width = heads[0].shape
    count = len(heads)
    features = near[0].shape[1] if near else mine.shape[1]
    part = width // 2
    tile = 512 if features % 512 == 0 else 128

    def kernel(place_ref, *refs):
        head_refs, refs = refs[:count], refs[count:]
        mine_ref, refs = refs[0], refs[1:]
        near_refs, refs = refs[: count - 1], refs[count - 1 :]
        far_refs, refs = refs[: count - 1], refs[count - 1 :]
        out_ref = refs[-1]
        c = place_ref[0]
        total = dot(head_refs[0][...], mine_ref[...], NN)
        for head, one, two in zip(head_refs[1:], near_refs, far_refs):
            total += dot(head[:, pl.ds(pl.multiple_of(c * part, 128), part)], one[...], NN)
            total += dot(head[:, pl.ds(pl.multiple_of((1 - c) * part, 128), part)], two[...], NN)
        out_ref[...] = total.astype(BF16)

    blocks = features // tile
    operands = [*heads, mine, *near, *far]
    in_specs = [whole((tokens, width))] * count
    in_specs += [pl.BlockSpec((width, tile), lambda i, at: (0, at[1] * blocks + i))]
    in_specs += [pl.BlockSpec((part, tile), lambda i, at: (0, i))] * (2 * (count - 1))
    aliases = {}
    if mixed is not None:
        operands.append(mixed)
        in_specs.append(ANY)
        aliases = {len(operands): 0}
    return pl.pallas_call(
        kernel,
        grid_spec=pltpu.PrefetchScalarGridSpec(
            num_scalar_prefetch=1,
            grid=(blocks,),
            in_specs=in_specs,
            out_specs=pl.BlockSpec((None, tokens, tile), lambda i, at: (group, 0, i)),
        ),
        out_shape=jax.ShapeDtypeStruct((GROUPS, tokens, features), BF16),
        input_output_aliases=aliases,
        name="project",
    )(place, *operands)


def matrices(core, mine, other):
    half, width = mine.shape
    rows = 2 * half
    hidden = rows // 3

    def kernel(core_ref, mine_ref, other_ref, a, b, c, w_ref):
        core_at = core_ref[0]
        w_ref[pl.ds(pl.multiple_of(core_at * half, 16), half)] = mine_ref[...]
        w_ref[pl.ds(pl.multiple_of((1 - core_at) * half, 16), half)] = other_ref[...]
        for n, out in enumerate((a, b, c)):
            out[...] = w_ref[pl.ds(n * hidden, hidden)].T

    return pl.pallas_call(
        kernel,
        grid_spec=pltpu.PrefetchScalarGridSpec(
            num_scalar_prefetch=1,
            grid=(1,),
            in_specs=[whole((half, width))] * 2,
            out_specs=[of_group(0, (width, hidden))] * 3,
            scratch_shapes=[pltpu.VMEM((rows, width), BF16)],
        ),
        out_shape=[jax.ShapeDtypeStruct((1, width, hidden), BF16)] * 3,
        name="matrices",
    )(core, mine, other)


def orders(count):
    rest = list(range(1, count.bit_length() - 1))
    return rest, rest[1:] + rest[:1]


def exchange(value, count, step):
    even, odd = orders(count)
    pairs = [(i, i ^ (1 << (odd if i & 1 else even)[step])) for i in range(count)]
    return lax.ppermute(value, "ctx", pairs)


def own_bit(index, count, step):
    even, odd = orders(count)
    return jnp.where(index & 1, (index >> odd[step]) & 1, (index >> even[step]) & 1)


def reduce_rows(send, keep, index, count):
    swap = [(i, i ^ 1) for i in range(count)]
    got = lax.ppermute(send, "ctx", swap)
    total = keep + got.astype(F32)
    for step in range(len(orders(count)[0])):
        rows = total.shape[0] // 2
        bit = own_bit(index, count, step)
        out = lax.dynamic_slice_in_dim(total, (1 - bit) * rows, rows, 0).astype(BF16)
        got = exchange(out, count, step)
        total = lax.dynamic_slice_in_dim(total, bit * rows, rows, 0) + got.astype(F32)
    return total


def gather_rows(shard, index, count):
    for step in reversed(range(len(orders(count)[0]))):
        got = exchange(shard, count, step)
        bit = own_bit(index, count, step)
        shard = jnp.where(
            bit == 0,
            jnp.concatenate([shard, got], axis=0),
            jnp.concatenate([got, shard], axis=0),
        )
    swap = [(i, i ^ 1) for i in range(count)]
    return shard, lax.ppermute(shard, "ctx", swap)


def row_start(index, count, rows):
    rows //= 2
    start = (index & 1) * rows
    for step in range(len(orders(count)[0])):
        rows //= 2
        start += own_bit(index, count, step) * rows
    return start, rows


def renormed(before, summed):
    changed = before - summed
    kept = jnp.sqrt(jnp.sum(before * before, axis=1, keepdims=True))
    return changed * (kept / jnp.sqrt(jnp.sum(changed * changed, axis=1, keepdims=True) + 1e-06))


def local(query, key_in, value, rates, w_in, w_gate, w_out, norm_gain, proj_weight):
    count = lax.axis_size("ctx")
    heads = lax.axis_size("head")
    index = lax.axis_index("ctx")
    head = lax.axis_index("head")
    core = (index & 1).astype(jnp.int32)
    core_arg = core[None]
    tokens, width = query.shape[1:]
    reach = WINDOW // 2
    features = proj_weight.shape[1] // heads
    part = width // 2

    up = [(i, i + 1) for i in range(count - 1)]
    down = [(j, i) for i, j in up]
    before_k = lax.ppermute(key_in[:, tokens - reach :], "ctx", up)
    after_k = lax.ppermute(key_in[:, :reach], "ctx", down)
    before_v = lax.ppermute(value[:, tokens - reach :], "ctx", up)
    after_v = lax.ppermute(value[:, :reach], "ctx", down)
    bounds = jnp.stack(
        [
            jnp.where(index == 0, reach, 0),
            jnp.where(index == count - 1, reach + tokens, tokens + WINDOW),
        ]
    ).astype(jnp.int32)

    swap = [(i, i ^ 1) for i in range(count)]
    near = []
    far = []
    for shift in range(1, heads):
        target = (head + shift) % heads
        piece = lax.dynamic_slice(proj_weight, (core * part, target * features), (part, features))
        got = lax.ppermute(piece, "head", [(i, (i + shift) % heads) for i in range(heads)])
        near.append(got)
        far.append(lax.ppermute(got, "ctx", swap))
    place = jnp.stack([core, head.astype(jnp.int32)])

    natural = (w_in, w_gate, w_out)
    rate_col = rates.reshape(GROUPS, tokens, 1)
    state_rows = jnp.concatenate([w_in[0].T, w_gate[0].T, w_out[0].T], axis=0)
    start, rows = row_start(index, count, state_rows.shape[0])
    state = lax.dynamic_slice_in_dim(state_rows, start, rows, 0).astype(F32)

    weights = natural
    mixed = None
    for group in range(GROUPS):
        gathered = group > 0
        send, keep = key_side(core_arg, key_in, value, rate_col, weights, group, gathered)
        window = window_side(
            bounds, query, key_in, value, before_k, before_v, after_k, after_v, group
        )
        head_out = query_side(core_arg, query, norm_gain, window, weights, group, gathered)
        outs = [head_out]
        for shift in range(1, heads):
            outs.append(
                lax.ppermute(head_out, "head", [(i, (i + shift) % heads) for i in range(heads)])
            )
        mixed = project(place, outs, proj_weight, near, far, group, mixed)
        state = renormed(state, reduce_rows(send, keep, index, count))
        weights = gather_rows(state.astype(BF16), index, count)
    return (mixed, *matrices(core_arg, *weights))


def solution(mesh):
    return jax.shard_map(
        local,
        mesh=mesh,
        in_specs=(
            P(None, "ctx", "head"),
            P(None, "ctx", "head"),
            P(None, "ctx", "head"),
            P(None, "head", "ctx"),
            P("head", None, None),
            P("head", None, None),
            P("head", None, None),
            P("head", None),
            P("head", None),
        ),
        out_specs=(
            P(None, "ctx", "head"),
            P("head", None, None),
            P("head", None, None),
            P("head", None, None),
        ),
        check_vma=False,
    )
```

time: 302 us -> 212 us (0.70); the launches traced: 298 us -> 211 us
  waiting for transfers between devices: 177 us -> 106 us
  Pallas kernels: 0 us -> 54.9 us
  matrix products: 46.1 us -> 0 us
  other arithmetic: 29.2 us -> 11.1 us
  starting transfers between devices: 11.7 us -> 28.9 us
  between operations: 15.9 us -> 1.01 us
  local copies, waits for them, and re-layouts: 18 us -> 9 us
    psum x2 -> x0, waiting for transfers between devices: 113 us -> none  [local(): grads = lax.psum((grad_in, grad_gate, grad_out), 'ctx')]
    ppermute x4 -> x24, waiting for transfers between devices: 38.2 us -> 106 us  [the longest x12 83.8 us: exchange(): return lax.ppermute(value, 'ctx', pairs)]
    pallas_call x0 -> x9, Pallas kernels: none -> 54.9 us  [the longest x2 16 us: project(): pl.pallas_call(kernel, grid_spec=pltpu.PrefetchScalarGridSpec(num_scalar_...]
    dot_general x20 -> x0, matrix products: 46.1 us -> none  [the longest x2 21.5 us: local(): terms = jnp.dot(head_out, proj_weight, preferred_element_type=jnp.float32)]
    reduce_scatter x2 -> x0, waiting for transfers between devices: 26.3 us -> none  [local(): lax.psum_scatter(terms.astype(jnp.bfloat16), 'head', scatter_dimension=1,...]
    ppermute x4 -> x24, starting transfers between devices: 11.4 us -> 28.9 us  [the longest x12 15.9 us: exchange(): return lax.ppermute(value, 'ctx', pairs)]
    reduce_sum x9 -> x3, other arithmetic: 11 us -> 1.48 us  [the longest x2 1.35 us: renormed(): kept = jnp.sqrt(jnp.sum(before * before, axis=1, keepdims=True))]
    unnamed x50 -> x31, local copies, waits for them, and re-layouts: 12.5 us -> 5.63 us
  transfers between devices with their start and end apart: 8 -> 24, of which waited for: 5 -> 19; matrix products, arithmetic and copies ran while one was open for 24% -> 3% of each run, Pallas kernels for 0% -> 19%
where the time goes in v1:
time: 212 us; the launch traced here: 211 us
  waiting for transfers between devices  106 us (50%)
  Pallas kernels  54.9 us (26%)
  starting transfers between devices  28.9 us (14%)
  other arithmetic  11.1 us (5%)
  local copies, waits for them, and re-layouts  9 us (4%)
    ppermute x12, waiting for transfers between devices, exchange(): return lax.ppermute(value, 'ctx', pairs)  83.8 us
    pallas_call x2, Pallas kernels, project(): pl.pallas_call(kernel, grid_spec=pltpu.PrefetchScalarGridSpec(num_scalar_...  16 us
    ppermute x12, starting transfers between devices, exchange(): return lax.ppermute(value, 'ctx', pairs)  15.9 us
    pallas_call x2, Pallas kernels, window_side(): pl.pallas_call(kernel, grid_spec=pltpu.PrefetchScalarGridSpec(num_scalar_...  13.8 us
    pallas_call x2, Pallas kernels, key_side(): pl.pallas_call(kernel, grid_spec=pltpu.PrefetchScalarGridSpec(num_scalar_...  12.9 us
    pallas_call x2, Pallas kernels, query_side(): pl.pallas_call(kernel, grid_spec=pltpu.PrefetchScalarGridSpec(num_scalar_...  9.45 us
    ppermute x1, waiting for transfers between devices, local(): after_v = lax.ppermute(value[:, :reach], 'ctx', down)  6.78 us
    unnamed x31, local copies, waits for them, and re-layouts  5.63 us
  transfers between devices with their start and end apart: 24, of which 19 were waited for; matrix products, arithmetic and copies ran while one was open for 3% of the time, Pallas kernels for 19%

profile of v1, /device:TPU:14, one launch (start us, length us, event | category | flops | bytes accessed | tf_op | source)
XLA Modules:
  0.0 211.4 jit_solution(14992879100082650238)
XLA Ops:
  2.3 5.9 %key_side.2 = (bf16[768,512]{1,0:T(8,128)(2,1)}, f32[768,512]{1,0:T(8,128)}) custom-call(s32[1]{0:T(128)} %bitcast.core_ref, bf16[2,512,512]{2,1,0:T(8,128)(2,1)} %k_ref.7, bf16[2,512,512]{2,1,0:T(8,128)(2,1)} %v_ref.7, f32[2,512,1]{2,1,0:T(8,128)} %reshape.36.rate_ref, bf16[1,512,512]{2,1,0:T(8,128)(2,1)} %refs_0_.3, bf16[1,512,512]{2,1,0:T(8,128)(2,1)} %refs_1_.3, ...), custom_call_target="tpu_custom_call" | custom-call | tf_op jit(solution)/shard_map/key_side/pallas_call | solution.py:92
  13.1 7.3 %collective-permute-done.5 = bf16[384,512]{1,0:T(8,128)(2,1)} collective-permute-done((bf16[384,512]{1,0:T(8,128)(2,1)S(1)}, bf16[384,512]{1,0:T(8,128)(2,1)}, u32[]{:S(2)}, u32[]{:S(2)}) %collective-permute-start.5) | collective-permute-done | bytes 393248 | tf_op jit(solution)/shard_map/ppermute | solution.py:324
  22.8 5.9 %collective-permute-done.6 = bf16[192,512]{1,0:T(8,128)(2,1)S(1)} collective-permute-done((bf16[192,512]{1,0:T(8,128)(2,1)S(1)}, bf16[192,512]{1,0:T(8,128)(2,1)S(1)}, u32[]{:S(2)}, u32[]{:S(2)}) %collective-permute-start.6) | collective-permute-done | bytes 196640 | tf_op jit(solution)/shard_map/ppermute | solution.py:324
  28.9 3.2 %collective-permute-start.7 = (bf16[96,512]{1,0:T(8,128)(2,1)S(1)}, bf16[96,512]{1,0:T(8,128)(2,1)S(1)}, u32[]{:S(2)}, u32[]{:S(2)}) collective-permute-start(bf16[96,512]{1,0:T(8,128)(2,1)S(1)} %dynamic-slice_convert_fusion.5), channel_id=1, source_target_pairs={{0,16},{2,6},{4,20},{6,2},{8,24},{10,14},{12,28},{14,10},{16,0},{1... | collective-permute-start | bytes 294920 | tf_op jit(solution)/shard_map/ppermute | solution.py:324
  38.6 5.2 %collective-permute-done.8 = bf16[96,512]{1,0:T(8,128)(2,1)S(1)} collective-permute-done((bf16[96,512]{1,0:T(8,128)(2,1)S(1)}, bf16[96,512]{1,0:T(8,128)(2,1)S(1)}, u32[]{:S(2)}, u32[]{:S(2)}) %collective-permute-start.8) | collective-permute-done | bytes 98336 | tf_op jit(solution)/shard_map/ppermute | solution.py:324
  44.0 7.5 %collective-permute-done.9 = bf16[192,512]{1,0:T(8,128)(2,1)S(1)} collective-permute-done((bf16[192,512]{1,0:T(8,128)(2,1)S(1)}, bf16[192,512]{1,0:T(8,128)(2,1)S(1)}, u32[]{:S(2)}, u32[]{:S(2)}) %collective-permute-start.9) | collective-permute-done | bytes 196640 | tf_op jit(solution)/shard_map/ppermute | solution.py:324
  52.2 7.2 %collective-permute-done.10 = bf16[384,512]{1,0:T(8,128)(2,1)S(1)} collective-permute-done((bf16[384,512]{1,0:T(8,128)(2,1)S(1)}, bf16[384,512]{1,0:T(8,128)(2,1)S(1)}, u32[]{:S(2)}, u32[]{:S(2)}) %collective-permute-start.10) | collective-permute-done | bytes 393248 | tf_op jit(solution)/shard_map/ppermute | solution.py:324
  63.1 6.9 %key_side.3 = (bf16[768,512]{1,0:T(8,128)(2,1)}, f32[768,512]{1,0:T(8,128)}) custom-call(s32[1]{0:T(128)} %bitcast.core_ref, bf16[2,512,512]{2,1,0:T(8,128)(2,1)} %k_ref.7, bf16[2,512,512]{2,1,0:T(8,128)(2,1)} %v_ref.7, f32[2,512,1]{2,1,0:T(8,128)} %reshape.36.rate_ref, bf16[768,512]{1,0:T(8,128)(2,1)} %copy-done.2, bf16[768,512]{1,0:T(8,128)(2,1)} %copy-done.8), custom_call_target="tpu_custom_call" | custom-call | tf_op jit(solution)/shard_map/key_side/pallas_call | solution.py:92
  74.9 7.2 %collective-permute-done.17 = bf16[384,512]{1,0:T(8,128)(2,1)S(1)} collective-permute-done((bf16[384,512]{1,0:T(8,128)(2,1)S(1)}, bf16[384,512]{1,0:T(8,128)(2,1)S(1)}, u32[]{:S(2)}, u32[]{:S(2)}) %collective-permute-start.17) | collective-permute-done | bytes 393248 | tf_op jit(solution)/shard_map/ppermute | solution.py:324
  82.4 7.5 %collective-permute-done.18 = bf16[192,512]{1,0:T(8,128)(2,1)S(1)} collective-permute-done((bf16[192,512]{1,0:T(8,128)(2,1)S(1)}, bf16[192,512]{1,0:T(8,128)(2,1)S(1)}, u32[]{:S(2)}, u32[]{:S(2)}) %collective-permute-start.18) | collective-permute-done | bytes 196640 | tf_op jit(solution)/shard_map/ppermute | solution.py:324
  91.4 3.5 %collective-permute-start.19 = (bf16[96,512]{1,0:T(8,128)(2,1)}, bf16[96,512]{1,0:T(8,128)(2,1)S(1)}, u32[]{:S(2)}, u32[]{:S(2)}) collective-permute-start(bf16[96,512]{1,0:T(8,128)(2,1)} %dynamic-slice_convert_fusion.4), channel_id=1, source_target_pairs={{0,16},{2,6},{4,20},{6,2},{8,24},{10,14},{12,28},{14,10},{16,0},{1... | collective-permute-start | bytes 294920 | tf_op jit(solution)/shard_map/ppermute | solution.py:324
  102.9 5.3 %collective-permute-done.20 = bf16[96,512]{1,0:T(8,128)(2,1)S(1)} collective-permute-done((bf16[96,512]{1,0:T(8,128)(2,1)S(1)}, bf16[96,512]{1,0:T(8,128)(2,1)S(1)}, u32[]{:S(2)}, u32[]{:S(2)}) %collective-permute-start.20) | collective-permute-done | bytes 98336 | tf_op jit(solution)/shard_map/ppermute | solution.py:324
  110.3 3.9 %collective-permute-done.21 = bf16[192,512]{1,0:T(8,128)(2,1)S(1)} collective-permute-done((bf16[192,512]{1,0:T(8,128)(2,1)S(1)}, bf16[192,512]{1,0:T(8,128)(2,1)S(1)}, u32[]{:S(2)}, u32[]{:S(2)}) %collective-permute-start.21) | collective-permute-done | bytes 196640 | tf_op jit(solution)/shard_map/ppermute | solution.py:324
  116.8 3.6 %collective-permute-start.3 = (bf16[2,512,512]{2,1,0:T(8,128)(2,1)S(1)}, bf16[2,512,512]{2,1,0:T(8,128)(2,1)}, u32[]{:S(2)}, u32[]{:S(2)}) collective-permute-start(bf16[2,512,512]{2,1,0:T(8,128)(2,1)S(1)} %copy-done.1), channel_id=1, source_target_pairs={{2,0},{4,2},{6,4},{8,6},{10,8},{12,10},{14,12},{16,14},{18,16},{20... | collective-permute-start | bytes 3145736 | tf_op jit(solution)/shard_map/ppermute | solution.py:390
  120.5 3.1 %collective-permute-done.13.refs_3_ = bf16[256,2560]{1,0:T(8,128)(2,1)S(1)} collective-permute-done((bf16[256,2560]{1,0:T(8,128)(2,1)S(1)}, bf16[256,2560]{1,0:T(8,128)(2,1)S(1)}, u32[]{:S(2)}, u32[]{:S(2)}) %collective-permute-start.13) | collective-permute-done | bytes 1310752 | tf_op jit(solution)/shard_map/ppermute | solution.py:404
  125.7 23.5 %collective-permute-done.22 = bf16[384,512]{1,0:T(8,128)(2,1)S(1)} collective-permute-done((bf16[384,512]{1,0:T(8,128)(2,1)S(1)}, bf16[384,512]{1,0:T(8,128)(2,1)S(1)}, u32[]{:S(2)}, u32[]{:S(2)}) %collective-permute-start.22) | collective-permute-done | bytes 393248 | tf_op jit(solution)/shard_map/ppermute | solution.py:324
  153.7 6.8 %collective-permute-done.3.av = bf16[2,512,512]{2,1,0:T(8,128)(2,1)} collective-permute-done((bf16[2,512,512]{2,1,0:T(8,128)(2,1)S(1)}, bf16[2,512,512]{2,1,0:T(8,128)(2,1)}, u32[]{:S(2)}, u32[]{:S(2)}) %collective-permute-start.3) | collective-permute-done | bytes 1048608 | tf_op jit(solution)/shard_map/ppermute | solution.py:390
  160.5 4.5 %collective-permute-done.1.bv = bf16[2,512,512]{2,1,0:T(8,128)(2,1)} collective-permute-done((bf16[2,512,512]{2,1,0:T(8,128)(2,1)S(1)}, bf16[2,512,512]{2,1,0:T(8,128)(2,1)}, u32[]{:S(2)}, u32[]{:S(2)}) %collective-permute-start.1) | collective-permute-done | bytes 1048608 | tf_op jit(solution)/shard_map/ppermute | solution.py:389
  164.9 6.9 %window_side.3.window_ref = f32[512,512]{1,0:T(8,128)} custom-call(s32[2]{0:T(128)} %pad_add_fusion.1.bounds_ref, bf16[2,512,512]{2,1,0:T(8,128)(2,1)} %q_ref.7, bf16[2,512,512]{2,1,0:T(8,128)(2,1)} %k_ref.7, bf16[2,512,512]{2,1,0:T(8,128)(2,1)} %v_ref.7, bf16[2,512,512]{2,1,0:T(8,128)(2,1)} %collective-permute-done.bk, ...), custom_call_target="tpu_custom_call" | custom-call | tf_op jit(solution)/shard_map/window_side/pallas_call | solution.py:164
  171.9 4.2 %query_side.3.refs_0_ = bf16[512,512]{1,0:T(8,128)(2,1)} custom-call(s32[1]{0:T(128)} %bitcast.core_ref, bf16[2,512,512]{2,1,0:T(8,128)(2,1)} %q_ref.7, f32[1,512]{1,0:T(1,128)} %gain_ref.3, f32[512,512]{1,0:T(8,128)} %window_side.3.window_ref, bf16[1,512,512]{2,1,0:T(8,128)(2,1)} %refs_0_.3, bf16[1,512,512]{2,1,0:T(8,128)(2,1)} %refs_1_.3, ...), custom_call_target="tpu_custom_call" | custom-call | tf_op jit(solution)/shard_map/query_side/pallas_call | solution.py:227
  176.3 6.9 %window_side.2.window_ref = f32[512,512]{1,0:T(8,128)} custom-call(s32[2]{0:T(128)} %pad_add_fusion.1.bounds_ref, bf16[2,512,512]{2,1,0:T(8,128)(2,1)} %q_ref.7, bf16[2,512,512]{2,1,0:T(8,128)(2,1)} %k_ref.7, bf16[2,512,512]{2,1,0:T(8,128)(2,1)} %v_ref.7, bf16[2,512,512]{2,1,0:T(8,128)(2,1)} %collective-permute-done.bk, ...), custom_call_target="tpu_custom_call" | custom-call | tf_op jit(solution)/shard_map/window_side/pallas_call | solution.py:164
  183.2 5.2 %query_side.2.refs_0_ = bf16[512,512]{1,0:T(8,128)(2,1)} custom-call(s32[1]{0:T(128)} %bitcast.core_ref, bf16[2,512,512]{2,1,0:T(8,128)(2,1)} %q_ref.7, f32[1,512]{1,0:T(1,128)} %gain_ref.3, f32[512,512]{1,0:T(8,128)} %window_side.2.window_ref, bf16[768,512]{1,0:T(8,128)(2,1)} %copy-done.2, bf16[768,512]{1,0:T(8,128)(2,1)} %copy-done.8), custom_call_target="tpu_custom_call" | custom-call | tf_op jit(solution)/shard_map/query_side/pallas_call | solution.py:227
  191.8 8.0 %project.2.refs_5_ = bf16[2,512,2560]{2,1,0:T(8,128)(2,1)} custom-call(s32[2]{0:T(128)} %pad_add_fusion.place_ref, bf16[512,512]{1,0:T(8,128)(2,1)} %query_side.3.refs_0_, bf16[512,512]{1,0:T(8,128)(2,1)} %copy-done.12, bf16[512,5120]{1,0:T(8,128)(2,1)} %refs_2_.7, bf16[256,2560]{1,0:T(8,128)(2,1)} %copy-done.3, ...), custom_call_target="tpu_custom_call" | custom-call | tf_op jit(solution)/shard_map/project/pallas_call | solution.py:276
  200.6 8.0 %project.3 = bf16[2,512,2560]{2,1,0:T(8,128)(2,1)} custom-call(s32[2]{0:T(128)} %pad_add_fusion.place_ref, bf16[512,512]{1,0:T(8,128)(2,1)} %query_side.2.refs_0_, bf16[512,512]{1,0:T(8,128)(2,1)} %copy-done.13, bf16[512,5120]{1,0:T(8,128)(2,1)} %refs_2_.7, bf16[256,2560]{1,0:T(8,128)(2,1)} %copy-done.3, ...), custom_call_target="tpu_custom_call", output_to_operand_aliasing={{}: (6, {})} | custom-call | tf_op jit(solution)/shard_map/project/pallas_call | solution.py:276
  (94 shorter events, 52.8 us)
Async XLA Ops:
  8.3 2.5 %collective-permute-start.4 = (bf16[768,512]{1,0:T(8,128)(2,1)}, bf16[768,512]{1,0:T(8,128)(2,1)S(1)}, u32[]{:S(2)}, u32[]{:S(2)}) collective-permute-start(bf16[768,512]{1,0:T(8,128)(2,1)} %get-tuple-element.12), channel_id=1, source_target_pairs={{0,2},{2,0},{4,6},{6,4},{8,10},{10,8},{12,14},{14,12},{16,18},{18,... | collective-permute-start | bytes 2359304 | tf_op jit(solution)/shard_map/ppermute | solution.py:334
  12.5 7.9 %collective-permute-start.5 = (bf16[384,512]{1,0:T(8,128)(2,1)S(1)}, bf16[384,512]{1,0:T(8,128)(2,1)}, u32[]{:S(2)}, u32[]{:S(2)}) collective-permute-start(bf16[384,512]{1,0:T(8,128)(2,1)S(1)} %dynamic-slice_convert_fusion.1), channel_id=1, source_target_pairs={{0,4},{2,10},{4,0},{6,14},{8,12},{10,2},{12,8},{14,6},{16,20},{18,... | collective-permute-start | bytes 1179656 | tf_op jit(solution)/shard_map/ppermute | solution.py:324
  21.6 7.2 %collective-permute-start.6 = (bf16[192,512]{1,0:T(8,128)(2,1)S(1)}, bf16[192,512]{1,0:T(8,128)(2,1)S(1)}, u32[]{:S(2)}, u32[]{:S(2)}) collective-permute-start(bf16[192,512]{1,0:T(8,128)(2,1)S(1)} %dynamic-slice_convert_fusion.3), channel_id=1, source_target_pairs={{0,8},{2,18},{4,12},{6,22},{8,0},{10,26},{12,4},{14,30},{16,24},{1... | collective-permute-start | bytes 589832 | tf_op jit(solution)/shard_map/ppermute | solution.py:324
  28.9 5.8 %collective-permute-start.7 = (bf16[96,512]{1,0:T(8,128)(2,1)S(1)}, bf16[96,512]{1,0:T(8,128)(2,1)S(1)}, u32[]{:S(2)}, u32[]{:S(2)}) collective-permute-start(bf16[96,512]{1,0:T(8,128)(2,1)S(1)} %dynamic-slice_convert_fusion.5), channel_id=1, source_target_pairs={{0,16},{2,6},{4,20},{6,2},{8,24},{10,14},{12,28},{14,10},{16,0},{1... | collective-permute-start | bytes 294920 | tf_op jit(solution)/shard_map/ppermute | solution.py:324
  35.6 8.3 %collective-permute-start.8 = (bf16[96,512]{1,0:T(8,128)(2,1)S(1)}, bf16[96,512]{1,0:T(8,128)(2,1)S(1)}, u32[]{:S(2)}, u32[]{:S(2)}) collective-permute-start(bf16[96,512]{1,0:T(8,128)(2,1)S(1)} %multiply_convert_fusion.1), channel_id=1, source_target_pairs={{0,16},{2,6},{4,20},{6,2},{8,24},{10,14},{12,28},{14,10},{16,0},{1... | collective-permute-start | bytes 294920 | tf_op jit(solution)/shard_map/ppermute | solution.py:324
  43.9 7.6 %collective-permute-start.9 = (bf16[192,512]{1,0:T(8,128)(2,1)S(1)}, bf16[192,512]{1,0:T(8,128)(2,1)S(1)}, u32[]{:S(2)}, u32[]{:S(2)}) collective-permute-start(bf16[192,512]{1,0:T(8,128)(2,1)S(1)} %maximum_select_fusion.4), channel_id=1, source_target_pairs={{0,8},{2,18},{4,12},{6,22},{8,0},{10,26},{12,4},{14,30},{16,24},{1... | collective-permute-start | bytes 589832 | tf_op jit(solution)/shard_map/ppermute | solution.py:324
  51.6 7.8 %collective-permute-start.10 = (bf16[384,512]{1,0:T(8,128)(2,1)S(1)}, bf16[384,512]{1,0:T(8,128)(2,1)S(1)}, u32[]{:S(2)}, u32[]{:S(2)}) collective-permute-start(bf16[384,512]{1,0:T(8,128)(2,1)S(1)} %maximum_select_fusion.2), channel_id=1, source_target_pairs={{0,4},{2,10},{4,0},{6,14},{8,12},{10,2},{12,8},{14,6},{16,20},{18,... | collective-permute-start | bytes 1179656 | tf_op jit(solution)/shard_map/ppermute | solution.py:324
  59.7 2.4 %collective-permute-start.11 = (bf16[768,512]{1,0:T(8,128)(2,1)S(1)}, bf16[768,512]{1,0:T(8,128)(2,1)S(1)}, u32[]{:S(2)}, u32[]{:S(2)}) collective-permute-start(bf16[768,512]{1,0:T(8,128)(2,1)S(1)} %maximum_select_fusion.refs_0_), channel_id=1, source_target_pairs={{0,2},{2,0},{4,6},{6,4},{8,10},{10,8},{12,14},{14,12},{16,18},{18,... | collective-permute-start | bytes 2359304 | tf_op jit(solution)/shard_map/ppermute | solution.py:355
  70.0 2.6 %collective-permute-start.16 = (bf16[768,512]{1,0:T(8,128)(2,1)}, bf16[768,512]{1,0:T(8,128)(2,1)S(1)}, u32[]{:S(2)}, u32[]{:S(2)}) collective-permute-start(bf16[768,512]{1,0:T(8,128)(2,1)} %get-tuple-element.14), channel_id=1, source_target_pairs={{0,2},{2,0},{4,6},{6,4},{8,10},{10,8},{12,14},{14,12},{16,18},{18,... | collective-permute-start | bytes 2359304 | tf_op jit(solution)/shard_map/ppermute | solution.py:334
  74.3 7.8 %collective-permute-start.17 = (bf16[384,512]{1,0:T(8,128)(2,1)S(1)}, bf16[384,512]{1,0:T(8,128)(2,1)S(1)}, u32[]{:S(2)}, u32[]{:S(2)}) collective-permute-start(bf16[384,512]{1,0:T(8,128)(2,1)S(1)} %dynamic-slice_convert_fusion), channel_id=1, source_target_pairs={{0,4},{2,10},{4,0},{6,14},{8,12},{10,2},{12,8},{14,6},{16,20},{18,... | collective-permute-start | bytes 1179656 | tf_op jit(solution)/shard_map/ppermute | solution.py:324
  82.3 7.6 %collective-permute-start.18 = (bf16[192,512]{1,0:T(8,128)(2,1)S(1)}, bf16[192,512]{1,0:T(8,128)(2,1)S(1)}, u32[]{:S(2)}, u32[]{:S(2)}) collective-permute-start(bf16[192,512]{1,0:T(8,128)(2,1)S(1)} %dynamic-slice_convert_fusion.2), channel_id=1, source_target_pairs={{0,8},{2,18},{4,12},{6,22},{8,0},{10,26},{12,4},{14,30},{16,24},{1... | collective-permute-start | bytes 589832 | tf_op jit(solution)/shard_map/ppermute | solution.py:324
  91.4 6.3 %collective-permute-start.19 = (bf16[96,512]{1,0:T(8,128)(2,1)}, bf16[96,512]{1,0:T(8,128)(2,1)S(1)}, u32[]{:S(2)}, u32[]{:S(2)}) collective-permute-start(bf16[96,512]{1,0:T(8,128)(2,1)} %dynamic-slice_convert_fusion.4), channel_id=1, source_target_pairs={{0,16},{2,6},{4,20},{6,2},{8,24},{10,14},{12,28},{14,10},{16,0},{1... | collective-permute-start | bytes 294920 | tf_op jit(solution)/shard_map/ppermute | solution.py:324
  96.4 27.2 %collective-permute-start.13 = (bf16[256,2560]{1,0:T(8,128)(2,1)S(1)}, bf16[256,2560]{1,0:T(8,128)(2,1)S(1)}, u32[]{:S(2)}, u32[]{:S(2)}) collective-permute-start(bf16[256,2560]{1,0:T(8,128)(2,1)S(1)} %dynamic_slice.49), channel_id=1, source_target_pairs={{0,1},{1,0},{2,3},{3,2},{4,5},{5,4},{6,7},{7,6},{8,9},{9,8},{10,11... | collective-permute-start | bytes 3932168 | tf_op jit(solution)/shard_map/ppermute | solution.py:404
  99.9 8.4 %collective-permute-start.20 = (bf16[96,512]{1,0:T(8,128)(2,1)S(1)}, bf16[96,512]{1,0:T(8,128)(2,1)S(1)}, u32[]{:S(2)}, u32[]{:S(2)}) collective-permute-start(bf16[96,512]{1,0:T(8,128)(2,1)S(1)} %multiply_convert_fusion), channel_id=1, source_target_pairs={{0,16},{2,6},{4,20},{6,2},{8,24},{10,14},{12,28},{14,10},{16,0},{1... | collective-permute-start | bytes 294920 | tf_op jit(solution)/shard_map/ppermute | solution.py:324
  108.3 5.9 %collective-permute-start.21 = (bf16[192,512]{1,0:T(8,128)(2,1)S(1)}, bf16[192,512]{1,0:T(8,128)(2,1)S(1)}, u32[]{:S(2)}, u32[]{:S(2)}) collective-permute-start(bf16[192,512]{1,0:T(8,128)(2,1)S(1)} %maximum_select_fusion.5), channel_id=1, source_target_pairs={{0,8},{2,18},{4,12},{6,22},{8,0},{10,26},{12,4},{14,30},{16,24},{1... | collective-permute-start | bytes 589832 | tf_op jit(solution)/shard_map/ppermute | solution.py:324
  108.3 42.2 %collective-permute-start.2 = (bf16[2,512,512]{2,1,0:T(8,128)(2,1)S(1)}, bf16[2,512,512]{2,1,0:T(8,128)(2,1)S(1)}, u32[]{:S(2)}, u32[]{:S(2)}) collective-permute-start(bf16[2,512,512]{2,1,0:T(8,128)(2,1)S(1)} %copy-done), channel_id=1, source_target_pairs={{2,0},{4,2},{6,4},{8,6},{10,8},{12,10},{14,12},{16,14},{18,16},{20... | collective-permute-start | bytes 3145736 | tf_op jit(solution)/shard_map/ppermute | solution.py:388
  114.3 35.0 %collective-permute-start.22 = (bf16[384,512]{1,0:T(8,128)(2,1)S(1)}, bf16[384,512]{1,0:T(8,128)(2,1)S(1)}, u32[]{:S(2)}, u32[]{:S(2)}) collective-permute-start(bf16[384,512]{1,0:T(8,128)(2,1)S(1)} %maximum_select_fusion.3), channel_id=1, source_target_pairs={{0,4},{2,10},{4,0},{6,14},{8,12},{10,2},{12,8},{14,6},{16,20},{18,... | collective-permute-start | bytes 1179656 | tf_op jit(solution)/shard_map/ppermute | solution.py:324
  114.9 38.8 %collective-permute-start = (bf16[2,512,512]{2,1,0:T(8,128)(2,1)S(1)}, bf16[2,512,512]{2,1,0:T(8,128)(2,1)}, u32[]{:S(2)}, u32[]{:S(2)}) collective-permute-start(bf16[2,512,512]{2,1,0:T(8,128)(2,1)S(1)} %copy-done), channel_id=1, source_target_pairs={{0,2},{2,4},{4,6},{6,8},{8,10},{10,12},{12,14},{14,16},{16,18},{18... | collective-permute-start | bytes 3145736 | tf_op jit(solution)/shard_map/ppermute | solution.py:387
  116.8 43.7 %collective-permute-start.3 = (bf16[2,512,512]{2,1,0:T(8,128)(2,1)S(1)}, bf16[2,512,512]{2,1,0:T(8,128)(2,1)}, u32[]{:S(2)}, u32[]{:S(2)}) collective-permute-start(bf16[2,512,512]{2,1,0:T(8,128)(2,1)S(1)} %copy-done.1), channel_id=1, source_target_pairs={{2,0},{4,2},{6,4},{8,6},{10,8},{12,10},{14,12},{16,14},{18,16},{20... | collective-permute-start | bytes 3145736 | tf_op jit(solution)/shard_map/ppermute | solution.py:390
  123.6 41.3 %collective-permute-start.1 = (bf16[2,512,512]{2,1,0:T(8,128)(2,1)S(1)}, bf16[2,512,512]{2,1,0:T(8,128)(2,1)}, u32[]{:S(2)}, u32[]{:S(2)}) collective-permute-start(bf16[2,512,512]{2,1,0:T(8,128)(2,1)S(1)} %copy-done.1), channel_id=1, source_target_pairs={{0,2},{2,4},{4,6},{6,8},{8,10},{10,12},{12,14},{14,16},{16,18},{18... | collective-permute-start | bytes 3145736 | tf_op jit(solution)/shard_map/ppermute | solution.py:389
  149.3 41.7 %collective-permute-start.14 = (bf16[256,2560]{1,0:T(8,128)(2,1)S(1)}, bf16[256,2560]{1,0:T(8,128)(2,1)}, u32[]{:S(2)}, u32[]{:S(2)}) collective-permute-start(bf16[256,2560]{1,0:T(8,128)(2,1)S(1)} %collective-permute-done.13.refs_3_), channel_id=1, source_target_pairs={{0,2},{2,0},{4,6},{6,4},{8,10},{10,8},{12,14},{14,12},{16,18},{18,... | collective-permute-start | bytes 3932168 | tf_op jit(solution)/shard_map/ppermute | solution.py:406
  151.5 57.1 %collective-permute-start.23 = (bf16[768,512]{1,0:T(8,128)(2,1)}, bf16[768,512]{1,0:T(8,128)(2,1)}, u32[]{:S(2)}, u32[]{:S(2)}) collective-permute-start(bf16[768,512]{1,0:T(8,128)(2,1)} %maximum_select_fusion.1.mine_ref), channel_id=1, source_target_pairs={{0,2},{2,0},{4,6},{6,4},{8,10},{10,8},{12,14},{14,12},{16,18},{18,... | collective-permute-start | bytes 2359304 | tf_op jit(solution)/shard_map/ppermute | solution.py:355
  176.1 14.9 %collective-permute-start.15 = (bf16[512,512]{1,0:T(8,128)(2,1)}, bf16[512,512]{1,0:T(8,128)(2,1)S(1)}, u32[]{:S(2)}, u32[]{:S(2)}) collective-permute-start(bf16[512,512]{1,0:T(8,128)(2,1)} %query_side.3.refs_0_), channel_id=1, source_target_pairs={{0,1},{1,0},{2,3},{3,2},{4,5},{5,4},{6,7},{7,6},{8,9},{9,8},{10,11... | collective-permute-start | bytes 1572872 | tf_op jit(solution)/shard_map/ppermute | solution.py:427
  188.5 11.3 %collective-permute-start.12 = (bf16[512,512]{1,0:T(8,128)(2,1)}, bf16[512,512]{1,0:T(8,128)(2,1)S(1)}, u32[]{:S(2)}, u32[]{:S(2)}) collective-permute-start(bf16[512,512]{1,0:T(8,128)(2,1)} %query_side.2.refs_0_), channel_id=1, source_target_pairs={{0,1},{1,0},{2,3},{3,2},{4,5},{5,4},{6,7},{7,6},{8,9},{9,8},{10,11... | collective-permute-start | bytes 1572872 | tf_op jit(solution)/shard_map/ppermute | solution.py:427
  (14 other events, 112.3 us)

commit v2 on v1

v2 whole, which is shorter than its diff:
```python
import jax
import jax.numpy as jnp
from jax import lax
from jax.experimental import pallas as pl
from jax.experimental.pallas import tpu as pltpu
from jax.sharding import PartitionSpec as P


GROUPS = 2
WINDOW = 1024
F32 = jnp.float32
BF16 = jnp.bfloat16
NN = (((1,), (0,)), ((), ()))
NT = (((1,), (1,)), ((), ()))
TN = (((0,), (0,)), ((), ()))


def dot(lhs, rhs, dims):
    return lax.dot_general(lhs, rhs, dims, preferred_element_type=F32)


def whole(shape):
    zeros = (0,) * len(shape)
    return pl.BlockSpec(shape, lambda i, *refs: zeros)


HBM = pl.BlockSpec(memory_space=pltpu.HBM)
VMEM = pl.BlockSpec(memory_space=pltpu.VMEM)


def limit(mib):
    return pltpu.CompilerParams(vmem_limit_bytes=mib << 20)


def in_hbm(*arrays):
    return [pltpu.with_memory_space_constraint(array, pltpu.HBM) for array in arrays]


def fetch(pairs, sems):
    copies = [pltpu.make_async_copy(a, b, sems.at[n]) for n, (a, b) in enumerate(pairs)]
    for copy in copies:
        copy.start()
    return copies


def wait(copies):
    for copy in copies:
        copy.wait()


def weight_pairs(refs, target, hidden, gathered):
    if not gathered:
        return [(ref.at[0], target.at[pl.ds(n * hidden, hidden)]) for n, ref in enumerate(refs)]
    c = lax.axis_index("ctx") & 1
    half = target.shape[0] // 2
    return [
        (ref, target.at[pl.ds(pl.multiple_of(at * half, 16), half)])
        for ref, at in zip(refs, (c, 1 - c))
    ]


def key_side(keys, values, rates, weights, group, gathered):
    tokens, width = keys.shape[1:]
    hidden = width
    rows = 3 * hidden
    half = rows // 2
    step = min(256, tokens)
    scale = width ** (-0.5)
    first = NT if gathered else NN
    second = NN if gathered else NT
    count = len(weights)

    def kernel(k_in, v_in, rate_ref, *refs):
        w_in, refs = refs[:count], refs[count:]
        send_ref, keep_ref, *refs = refs
        stacks, refs = ([], refs) if gathered else (refs[:GROUPS], refs[GROUPS:])
        w_ref, k_all, v_all, hk, sc, d1, d3, grad, rate_col, sems, load_sems, stack_sems = refs
        loads = fetch(weight_pairs(w_in, w_ref, hidden, gathered), sems)
        wanted = [group] if gathered else list(range(GROUPS))
        wanted.sort(key=lambda g: g != group)
        fetched = fetch(
            [(a.at[g], b.at[g]) for g in wanted for a, b in ((k_in, k_all), (v_in, v_all))],
            load_sems,
        )
        w1, w3, w2 = (w_ref.at[pl.ds(n * hidden, hidden)] for n in range(3))
        k_ref, v_ref = k_all.at[group], v_all.at[group]
        rate_col[...] = jnp.broadcast_to(rate_ref[group], (8, tokens)).T
        wait(loads + fetched)
        stacking = fetch(
            [
                (source.at[g], stack.at[n])
                for g, stack in enumerate(stacks)
                for n, source in enumerate((k_all, v_all))
            ],
            stack_sems,
        )

        def forward(n, carry):
            at = pl.ds(n * step, step)
            k = k_ref[at]
            f1 = dot(k, w1[...], first) * scale
            f3 = dot(k, w3[...], first) * scale
            scaled = (rate_col[at, :1] * v_ref[at].astype(F32)).astype(BF16)
            sc[at] = scaled
            back = dot(scaled, w2[...], second) * (-scale)
            sig = jax.nn.sigmoid(f1)
            act = f1 * sig
            slope = sig * (1.0 + f1 * (1.0 - sig))
            hk[at] = (act * f3).astype(BF16)
            d1[at] = (back * f3 * slope).astype(BF16)
            d3[at] = (back * act).astype(BF16)
            return carry

        lax.fori_loop(0, tokens // step, forward, 0)
        for n, (lhs, rhs, by) in enumerate(((d1, k_ref, scale), (d3, k_ref, scale), (sc, hk, -scale))):
            grad[pl.ds(n * hidden, hidden)] = dot(lhs[...], rhs[...], TN) * by
        c = lax.axis_index("ctx") & 1
        send_ref[...] = grad[pl.ds(pl.multiple_of((1 - c) * half, 16), half)].astype(BF16)
        keep_ref[...] = grad[pl.ds(pl.multiple_of(c * half, 16), half)]
        wait(stacking)

    out_specs = [VMEM, VMEM]
    out_shape = [
        jax.ShapeDtypeStruct((half, width), BF16),
        jax.ShapeDtypeStruct((half, width), F32),
    ]
    if not gathered:
        out_specs += [HBM] * GROUPS
        out_shape += [jax.ShapeDtypeStruct((2, tokens, width), BF16)] * GROUPS
    return pl.pallas_call(
        kernel,
        in_specs=[HBM, HBM, VMEM] + [VMEM if gathered else HBM] * count,
        out_specs=out_specs,
        out_shape=out_shape,
        scratch_shapes=[
            pltpu.VMEM((rows, width), BF16),
            pltpu.VMEM((GROUPS, tokens, width), BF16),
            pltpu.VMEM((GROUPS, tokens, width), BF16),
            *[pltpu.VMEM((tokens, hidden), BF16) for _ in range(4)],
            pltpu.VMEM((rows, width), F32),
            pltpu.VMEM((tokens, 8), F32),
            pltpu.SemaphoreType.DMA((3,)),
            pltpu.SemaphoreType.DMA((2 * GROUPS,)),
            pltpu.SemaphoreType.DMA((2 * GROUPS,)),
        ],
        compiler_params=limit(28),
        name="key_side",
    )(*in_hbm(keys, values), rates, *(weights if gathered else in_hbm(*weights)))


def window_side(query, own, before, after, group):
    tokens, width = query.shape[1:]
    reach = WINDOW // 2
    total = tokens + WINDOW
    step = min(256, tokens)
    span = step + WINDOW
    scale = width ** (-0.5)

    def kernel(q_in, own_ref, before_ref, after_ref, out_ref, q_ref, k_all, v_all, sems):
        places = (pl.ds(reach, tokens), pl.ds(0, reach), pl.ds(reach + tokens, reach))
        pairs = [(q_in.at[group], q_ref)]
        for n, target in enumerate((k_all, v_all)):
            for source, place in zip((own_ref, before_ref, after_ref), places):
                pairs.append((source.at[n], target.at[place]))
        wait(fetch(pairs, sems))
        index = lax.axis_index("ctx")
        lowest = jnp.where(index == 0, reach, 0)
        highest = jnp.where(index == lax.axis_size("ctx") - 1, reach + tokens, total)

        def block(n, carry):
            start = n * step
            q = q_ref[pl.ds(start, step)]
            scores = dot(q, k_all[pl.ds(start, span)], NT) * scale
            row = lax.broadcasted_iota(jnp.int32, (step, span), 0)
            col = lax.broadcasted_iota(jnp.int32, (step, span), 1)
            valid = (
                (col >= row)
                & (col < row + WINDOW)
                & (col >= lowest - start)
                & (col < highest - start)
            )
            scores = jnp.where(valid, scores, -1e30)
            largest = jnp.max(scores, axis=1, keepdims=True)
            expo = jnp.exp(scores - largest)
            norm = jnp.sum(expo, axis=1, keepdims=True)
            mixed = dot(expo.astype(BF16), v_all[pl.ds(start, span)], NN)
            out_ref[pl.ds(start, step)] = mixed / norm
            return carry

        lax.fori_loop(0, tokens // step, block, 0)

    return pl.pallas_call(
        kernel,
        in_specs=[HBM] * 4,
        out_specs=VMEM,
        out_shape=jax.ShapeDtypeStruct((tokens, width), F32),
        scratch_shapes=[
            pltpu.VMEM((tokens, width), BF16),
            pltpu.VMEM((total, width), BF16),
            pltpu.VMEM((total, width), BF16),
            pltpu.SemaphoreType.DMA((7,)),
        ],
        compiler_params=limit(20),
        name="window_side",
    )(*in_hbm(query, own, before, after))


def query_side(query, gain, window, weights, group, gathered):
    tokens, width = query.shape[1:]
    hidden = width
    rows = 3 * hidden
    step = min(256, tokens)
    scale = width ** (-0.5)
    first = NT if gathered else NN
    count = len(weights)

    def kernel(q_in, gain_ref, window_ref, *refs):
        w_in, (out_ref, q_ref, w_ref, sems) = refs[:count], refs[count:]
        pairs = [(q_in.at[group], q_ref)]
        wait(fetch(pairs + weight_pairs(w_in, w_ref, hidden, gathered), sems))
        w1, w3, w2 = (w_ref.at[pl.ds(n * hidden, hidden)] for n in range(3))

        def block(n, carry):
            at = pl.ds(n * step, step)
            q = q_ref[at]
            g1 = dot(q, w1[...], first) * scale
            g3 = dot(q, w3[...], first) * scale
            hq = (g1 * jax.nn.sigmoid(g1) * g3).astype(BF16)
            ttt = dot(hq, w2[...], first) * scale
            mean = jnp.mean(ttt * ttt, axis=1, keepdims=True)
            normed = ttt * lax.rsqrt(mean + 1e-06) * gain_ref[...]
            out_ref[at] = (normed + window_ref[at]).astype(BF16)
            return carry

        lax.fori_loop(0, tokens // step, block, 0)

    return pl.pallas_call(
        kernel,
        in_specs=[HBM, VMEM, VMEM] + [VMEM if gathered else HBM] * count,
        out_specs=VMEM,
        out_shape=jax.ShapeDtypeStruct((tokens, width), BF16),
        scratch_shapes=[
            pltpu.VMEM((tokens, width), BF16),
            pltpu.VMEM((rows, width), BF16),
            pltpu.SemaphoreType.DMA((4,)),
        ],
        compiler_params=limit(14),
        name="query_side",
    )(*in_hbm(query), gain, window, *(weights if gathered else in_hbm(*weights)))


def project(place, heads, mine, near, far, group, mixed):
    tokens, width = heads[0].shape
    count = len(heads)
    features = near[0].shape[1] if near else mine.shape[1]
    part = width // 2
    tile = 512 if features % 512 == 0 else 128

    def kernel(place_ref, *refs):
        head_refs, refs = refs[:count], refs[count:]
        mine_ref, refs = refs[0], refs[1:]
        near_refs, refs = refs[: count - 1], refs[count - 1 :]
        far_refs, refs = refs[: count - 1], refs[count - 1 :]
        out_ref = refs[-1]
        c = place_ref[0]
        total = dot(head_refs[0][...], mine_ref[...], NN)
        for head, one, two in zip(head_refs[1:], near_refs, far_refs):
            total += dot(head[:, pl.ds(pl.multiple_of(c * part, 128), part)], one[...], NN)
            total += dot(head[:, pl.ds(pl.multiple_of((1 - c) * part, 128), part)], two[...], NN)
        out_ref[...] = total.astype(BF16)

    blocks = features // tile
    operands = [*heads, mine, *near, *far]
    in_specs = [whole((tokens, width))] * count
    in_specs += [pl.BlockSpec((width, tile), lambda i, at: (0, at[1] * blocks + i))]
    in_specs += [pl.BlockSpec((part, tile), lambda i, at: (0, i))] * (2 * (count - 1))
    aliases = {}
    if mixed is not None:
        operands.append(mixed)
        in_specs.append(HBM)
        aliases = {len(operands): 0}
    return pl.pallas_call(
        kernel,
        grid_spec=pltpu.PrefetchScalarGridSpec(
            num_scalar_prefetch=1,
            grid=(blocks,),
            in_specs=in_specs,
            out_specs=pl.BlockSpec((None, tokens, tile), lambda i, at: (group, 0, i)),
        ),
        out_shape=jax.ShapeDtypeStruct((GROUPS, tokens, features), BF16),
        input_output_aliases=aliases,
        compiler_params=limit(20),
        name="project",
    )(place, *operands)


def matrices(mine, other):
    half, width = mine.shape
    rows = 2 * half
    hidden = rows // 3

    def kernel(mine_ref, other_ref, a, b, c, w_ref, out_ref, sems, out_sems):
        wait(fetch(weight_pairs((mine_ref, other_ref), w_ref, hidden, True), sems))
        copies = []
        for n, out in enumerate((a, b, c)):
            out_ref[n] = w_ref[pl.ds(n * hidden, hidden)].T
            copies += fetch([(out_ref.at[n], out.at[0])], out_sems.at[pl.ds(n, 1)])
        wait(copies)

    return pl.pallas_call(
        kernel,
        in_specs=[VMEM] * 2,
        out_specs=[HBM] * 3,
        out_shape=[jax.ShapeDtypeStruct((1, width, hidden), BF16)] * 3,
        scratch_shapes=[
            pltpu.VMEM((rows, width), BF16),
            pltpu.VMEM((3, width, hidden), BF16),
            pltpu.SemaphoreType.DMA((2,)),
            pltpu.SemaphoreType.DMA((3,)),
        ],
        compiler_params=limit(10),
        name="matrices",
    )(mine, other)


def orders(count):
    rest = list(range(1, count.bit_length() - 1))
    return rest, rest[1:] + rest[:1]


def swap_pairs(count):
    return [(i, i ^ 1) for i in range(count)]


def exchange(value, count, step):
    even, odd = orders(count)
    pairs = [(i, i ^ (1 << (odd if i & 1 else even)[step])) for i in range(count)]
    return lax.ppermute(value, "ctx", pairs)


def own_bit(index, count, step):
    even, odd = orders(count)
    return jnp.where(index & 1, (index >> odd[step]) & 1, (index >> even[step]) & 1)


def piece_rows(refs, index, count, steps, flip):
    total = None
    for made, ref in enumerate(refs):
        start, rows = 0, ref.shape[0]
        for step in range(max(made - 1, 0), steps):
            rows //= 2
            bit = own_bit(index, count, step)
            start += (1 - bit if flip and step == steps - 1 else bit) * rows
        part = ref[...] if isinstance(start, int) else ref[pl.ds(pl.multiple_of(start, 16), rows)]
        total = part.astype(F32) if total is None else total + part.astype(F32)
    return total


def partial_sum(pieces, count, steps):
    rows, width = pieces[0].shape
    rows >>= steps

    def kernel(*refs):
        index = lax.axis_index("ctx")
        refs[-1][...] = piece_rows(refs[:-1], index, count, steps, True).astype(BF16)

    return pl.pallas_call(
        kernel,
        in_specs=[VMEM] * len(pieces),
        out_specs=VMEM,
        out_shape=jax.ShapeDtypeStruct((rows, width), BF16),
        compiler_params=limit(4),
        name="partial_sum",
    )(*pieces)


def renormed(before, pieces, count, steps):
    rows, width = before.shape

    def kernel(before_ref, *refs):
        index = lax.axis_index("ctx")
        old = before_ref[...]
        changed = old - piece_rows(refs[:-2], index, count, steps, False)
        kept = jnp.sqrt(jnp.sum(old * old, axis=1, keepdims=True))
        new = changed * (kept / jnp.sqrt(jnp.sum(changed * changed, axis=1, keepdims=True) + 1e-06))
        refs[-2][...] = new
        refs[-1][...] = new.astype(BF16)

    return pl.pallas_call(
        kernel,
        in_specs=[VMEM] * (1 + len(pieces)),
        out_specs=[VMEM] * 2,
        out_shape=[
            jax.ShapeDtypeStruct((rows, width), F32),
            jax.ShapeDtypeStruct((rows, width), BF16),
        ],
        compiler_params=limit(4),
        name="renormed",
    )(before, *pieces)


def next_state(before, send, keep, count):
    pieces = [keep, lax.ppermute(send, "ctx", swap_pairs(count))]
    steps = len(orders(count)[0])
    for step in range(steps):
        out = partial_sum(pieces, count, step + 1)
        pieces.append(exchange(out, count, step))
    return renormed(before, pieces, count, steps)


def gather_rows(shard, index, count):
    steps = len(orders(count)[0])
    for step in reversed(range(steps)):
        got = exchange(shard, count, step)
        bit = own_bit(index, count, step)
        shard = jnp.where(
            bit == 0,
            jnp.concatenate([shard, got], axis=0),
            jnp.concatenate([got, shard], axis=0),
        )
    return shard, lax.ppermute(shard, "ctx", swap_pairs(count))


def row_start(index, count, rows):
    rows //= 2
    start = (index & 1) * rows
    for step in range(len(orders(count)[0])):
        rows //= 2
        start += own_bit(index, count, step) * rows
    return start, rows


def layer(query, key_in, value, rates, w_in, w_gate, w_out, norm_gain, proj_weight):
    count = lax.axis_size("ctx")
    heads = lax.axis_size("head")
    index = lax.axis_index("ctx").astype(jnp.int32)
    head = lax.axis_index("head")
    core = (index & 1).astype(jnp.int32)
    tokens, width = query.shape[1:]
    reach = WINDOW // 2
    features = proj_weight.shape[1] // heads
    part = width // 2

    natural = (w_in, w_gate, w_out)
    send, keep, *stacks = key_side(key_in, value, rates, natural, 0, False)

    up = [(i, i + 1) for i in range(count - 1)]
    down = [(j, i) for i, j in up]
    before = []
    after = []
    for group in range(GROUPS):
        before.append(lax.ppermute(stacks[group][:, tokens - reach :], "ctx", up))
        after.append(lax.ppermute(stacks[group][:, :reach], "ctx", down))
    near = []
    far = []
    for shift in range(1, heads):
        target = (head + shift) % heads
        piece = lax.dynamic_slice(proj_weight, (core * part, target * features), (part, features))
        got = lax.ppermute(piece, "head", [(i, (i + shift) % heads) for i in range(heads)])
        near.append(got)
        far.append(lax.ppermute(got, "ctx", swap_pairs(count)))
    place = jnp.stack([core, head.astype(jnp.int32)])

    state_rows = jnp.concatenate([w_in[0].T, w_gate[0].T, w_out[0].T], axis=0)
    offset, rows = row_start(index, count, state_rows.shape[0])
    state = lax.dynamic_slice_in_dim(state_rows, offset, rows, 0).astype(F32)

    weights = natural
    mixed = None
    for group in range(GROUPS):
        gathered = group > 0
        if gathered:
            send, keep = key_side(key_in, value, rates, weights, group, True)
        window = window_side(query, stacks[group], before[group], after[group], group)
        head_out = query_side(query, norm_gain, window, weights, group, gathered)
        outs = [head_out]
        for shift in range(1, heads):
            outs.append(
                lax.ppermute(head_out, "head", [(i, (i + shift) % heads) for i in range(heads)])
            )
        mixed = project(place, outs, proj_weight, near, far, group, mixed)
        state, shard = next_state(state, send, keep, count)
        weights = gather_rows(shard, index, count)
    return (mixed, *matrices(*weights))


def solution(mesh):
    return jax.shard_map(
        layer,
        mesh=mesh,
        in_specs=(
            P(None, "ctx", "head"),
            P(None, "ctx", "head"),
            P(None, "ctx", "head"),
            P(None, "head", "ctx"),
            P("head", None, None),
            P("head", None, None),
            P("head", None, None),
            P("head", None),
            P("head", None),
        ),
        out_specs=(
            P(None, "ctx", "head"),
            P("head", None, None),
            P("head", None, None),
            P("head", None, None),
        ),
        check_vma=False,
    )
```

time: 212 us -> 186 us (0.88)
  Pallas kernels: 54.9 us -> 39.1 us
  waiting for transfers between devices: 106 us -> 94.9 us
  other arithmetic: 11.1 us -> 1.17 us
  starting transfers between devices: 28.9 us -> 36.2 us
    pallas_call x7 -> x15, Pallas kernels: 38.9 us -> 28.4 us  [the longest x2 10 us: key_side(): pl.pallas_call(kernel, in_specs=[HBM, HBM, VMEM] + [VMEM if gathered else...]
    ppermute x12, starting transfers between devices: 15.9 us -> 23.7 us  [exchange(): return lax.ppermute(value, 'ctx', pairs)]
    ppermute x12, waiting for transfers between devices: 83.8 us -> 76.9 us  [exchange(): return lax.ppermute(value, 'ctx', pairs)]
    pallas_call x2, Pallas kernels: 16 us -> 10.7 us  [project(): pl.pallas_call(kernel, grid_spec=pltpu.PrefetchScalarGridSpec(num_scalar_...]
    ppermute x12, waiting for transfers between devices: 22.6 us -> 18 us  [the longest x2 8.75 us: layer(): lax.ppermute(head_out, 'head', [(i, (i + shift) % heads) for i in range(h...]
    add x6 -> x0, other arithmetic: 4.63 us -> none  [the longest x2 3.32 us: reduce_rows(): total = keep + got.astype(F32)]
    unnamed x31 -> x43, local copies, waits for them, and re-layouts: 5.63 us -> 9.55 us
  transfers between devices with their start and end apart: 24 -> 24, of which waited for: 19 -> 20; matrix products, arithmetic and copies ran while one was open for 3% -> 4% of each run, Pallas kernels for 19% -> 14%
where the time goes in v2:
time: 186 us; the launch traced here: 184 us
  waiting for transfers between devices  94.9 us (51%)
  Pallas kernels  39.1 us (21%)
  starting transfers between devices  36.2 us (19%)
  local copies, waits for them, and re-layouts  11 us (6%)
    ppermute x12, waiting for transfers between devices, exchange(): return lax.ppermute(value, 'ctx', pairs)  76.9 us
    ppermute x12, starting transfers between devices, exchange(): return lax.ppermute(value, 'ctx', pairs)  23.7 us
    pallas_call x2, Pallas kernels, project(): pl.pallas_call(kernel, grid_spec=pltpu.PrefetchScalarGridSpec(num_scalar_...  10.7 us
    pallas_call x2, Pallas kernels, key_side(): pl.pallas_call(kernel, in_specs=[HBM, HBM, VMEM] + [VMEM if gathered else...  10 us
    unnamed x43, local copies, waits for them, and re-layouts  9.55 us
    ppermute x2, waiting for transfers between devices, layer(): lax.ppermute(head_out, 'head', [(i, (i + shift) % heads) for i in range(h...  8.75 us
    pallas_call x2, Pallas kernels, window_side(): pl.pallas_call(kernel, in_specs=[HBM] * 4, out_specs=VMEM, out_shape=jax....  8.73 us
    pallas_call x2, Pallas kernels, query_side(): pl.pallas_call(kernel, in_specs=[HBM, VMEM, VMEM] + [VMEM if gathered els...  6.02 us
  transfers between devices with their start and end apart: 24, of which 20 were waited for; matrix products, arithmetic and copies ran while one was open for 4% of the time, Pallas kernels for 14%

profile of v2, /device:TPU:14, one launch (start us, length us, event | category | flops | bytes accessed | tf_op | source)
XLA Modules:
  0.0 183.5 jit_solution(6514916711393514754)
XLA Ops:
  1.3 5.3 %key_side.2 = (bf16[768,512]{1,0:T(8,128)(2,1)S(1)}, f32[768,512]{1,0:T(8,128)S(1)}, bf16[2,512,512]{2,1,0:T(8,128)(2,1)S(1)}, bf16[2,512,512]{2,1,0:T(8,128)(2,1)S(1)}) custom-call(bf16[2,512,512]{2,1,0:T(8,128)(2,1)} %k_in.3, bf16[2,512,512]{2,1,0:T(8,128)(2,1)} %v_in.3, f32[2,1,512]{2,1,0:T(1,128)S(1)} %copy-done.8, bf16[1,512,512]{2,1,0:T(8,128)(2,1)} %refs_0_.3, ...), custom_call_target="tpu_custom_call" | custom-call | tf_op jit(solution)/shard_map/key_side/pallas_call | solution.py:130
  9.7 7.2 %collective-permute-done.3.refs_2_ = bf16[384,512]{1,0:T(8,128)(2,1)S(1)} collective-permute-done((bf16[384,512]{1,0:T(8,128)(2,1)S(1)}, bf16[384,512]{1,0:T(8,128)(2,1)S(1)}, u32[]{:S(2)}, u32[]{:S(2)}) %collective-permute-start.3) | collective-permute-done | bytes 393248 | tf_op jit(solution)/shard_map/ppermute | solution.py:338
  24.2 3.2 %collective-permute-start.5 = (bf16[96,512]{1,0:T(8,128)(2,1)S(1)}, bf16[96,512]{1,0:T(8,128)(2,1)S(1)}, u32[]{:S(2)}, u32[]{:S(2)}) collective-permute-start(bf16[96,512]{1,0:T(8,128)(2,1)S(1)} %partial_sum.8), channel_id=1, source_target_pairs={{0,16},{2,6},{4,20},{6,2},{8,24},{10,14},{12,28},{14,10},{16,0},{1... | collective-permute-start | bytes 294920 | tf_op jit(solution)/shard_map/ppermute | solution.py:338
  27.6 3.0 %collective-permute-done.5.refs_4_ = bf16[96,512]{1,0:T(8,128)(2,1)S(1)} collective-permute-done((bf16[96,512]{1,0:T(8,128)(2,1)S(1)}, bf16[96,512]{1,0:T(8,128)(2,1)S(1)}, u32[]{:S(2)}, u32[]{:S(2)}) %collective-permute-start.5) | collective-permute-done | bytes 98336 | tf_op jit(solution)/shard_map/ppermute | solution.py:338
  31.5 3.4 %collective-permute-start.6 = (bf16[96,512]{1,0:T(8,128)(2,1)S(1)}, bf16[96,512]{1,0:T(8,128)(2,1)S(1)}, u32[]{:S(2)}, u32[]{:S(2)}) collective-permute-start(bf16[96,512]{1,0:T(8,128)(2,1)S(1)} %get-tuple-element.19), channel_id=1, source_target_pairs={{0,16},{2,6},{4,20},{6,2},{8,24},{10,14},{12,28},{14,10},{16,0},{1... | collective-permute-start | bytes 294920 | tf_op jit(solution)/shard_map/ppermute | solution.py:338
  34.9 4.3 %collective-permute-done.6 = bf16[96,512]{1,0:T(8,128)(2,1)S(1)} collective-permute-done((bf16[96,512]{1,0:T(8,128)(2,1)S(1)}, bf16[96,512]{1,0:T(8,128)(2,1)S(1)}, u32[]{:S(2)}, u32[]{:S(2)}) %collective-permute-start.6) | collective-permute-done | bytes 98336 | tf_op jit(solution)/shard_map/ppermute | solution.py:338
  39.2 3.4 %collective-permute-start.7 = (bf16[192,512]{1,0:T(8,128)(2,1)S(1)}, bf16[192,512]{1,0:T(8,128)(2,1)S(1)}, u32[]{:S(2)}, u32[]{:S(2)}) collective-permute-start(bf16[192,512]{1,0:T(8,128)(2,1)S(1)} %maximum_select_fusion.4), channel_id=1, source_target_pairs={{0,8},{2,18},{4,12},{6,22},{8,0},{10,26},{12,4},{14,30},{16,24},{1... | collective-permute-start | bytes 589832 | tf_op jit(solution)/shard_map/ppermute | solution.py:338
  42.7 5.8 %collective-permute-done.7 = bf16[192,512]{1,0:T(8,128)(2,1)S(1)} collective-permute-done((bf16[192,512]{1,0:T(8,128)(2,1)S(1)}, bf16[192,512]{1,0:T(8,128)(2,1)S(1)}, u32[]{:S(2)}, u32[]{:S(2)}) %collective-permute-start.7) | collective-permute-done | bytes 196640 | tf_op jit(solution)/shard_map/ppermute | solution.py:338
  49.1 7.2 %collective-permute-done.8 = bf16[384,512]{1,0:T(8,128)(2,1)S(1)} collective-permute-done((bf16[384,512]{1,0:T(8,128)(2,1)S(1)}, bf16[384,512]{1,0:T(8,128)(2,1)S(1)}, u32[]{:S(2)}, u32[]{:S(2)}) %collective-permute-start.8) | collective-permute-done | bytes 393248 | tf_op jit(solution)/shard_map/ppermute | solution.py:338
  59.1 4.7 %key_side.3 = (bf16[768,512]{1,0:T(8,128)(2,1)S(1)}, f32[768,512]{1,0:T(8,128)S(1)}) custom-call(bf16[2,512,512]{2,1,0:T(8,128)(2,1)} %k_in.3, bf16[2,512,512]{2,1,0:T(8,128)(2,1)} %v_in.3, f32[2,1,512]{2,1,0:T(1,128)S(1)} %copy-done.9, bf16[768,512]{1,0:T(8,128)(2,1)S(1)} %maximum_select_fusion.refs_0_, bf16[768,512]{1,0:T(8,128)(2,1)S(1)} %collective-permute-done.9.refs_1_), custom_call_target="tpu_custom_call" | custom-call | tf_op jit(solution)/shard_map/key_side/pallas_call | solution.py:130
  69.5 5.5 %collective-permute-done.17.refs_2_ = bf16[384,512]{1,0:T(8,128)(2,1)S(1)} collective-permute-done((bf16[384,512]{1,0:T(8,128)(2,1)}, bf16[384,512]{1,0:T(8,128)(2,1)S(1)}, u32[]{:S(2)}, u32[]{:S(2)}) %collective-permute-start.17) | collective-permute-done | bytes 393248 | tf_op jit(solution)/shard_map/ppermute | solution.py:338
  77.1 5.0 %collective-permute-done.18.refs_3_ = bf16[192,512]{1,0:T(8,128)(2,1)S(1)} collective-permute-done((bf16[192,512]{1,0:T(8,128)(2,1)S(1)}, bf16[192,512]{1,0:T(8,128)(2,1)S(1)}, u32[]{:S(2)}, u32[]{:S(2)}) %collective-permute-start.18) | collective-permute-done | bytes 196640 | tf_op jit(solution)/shard_map/ppermute | solution.py:338
  88.6 3.0 %collective-permute-start.20 = (bf16[96,512]{1,0:T(8,128)(2,1)S(1)}, bf16[96,512]{1,0:T(8,128)(2,1)S(1)}, u32[]{:S(2)}, u32[]{:S(2)}) collective-permute-start(bf16[96,512]{1,0:T(8,128)(2,1)S(1)} %get-tuple-element.24), channel_id=1, source_target_pairs={{0,16},{2,6},{4,20},{6,2},{8,24},{10,14},{12,28},{14,10},{16,0},{1... | collective-permute-start | bytes 294920 | tf_op jit(solution)/shard_map/ppermute | solution.py:338
  91.6 5.3 %collective-permute-done.20 = bf16[96,512]{1,0:T(8,128)(2,1)S(1)} collective-permute-done((bf16[96,512]{1,0:T(8,128)(2,1)S(1)}, bf16[96,512]{1,0:T(8,128)(2,1)S(1)}, u32[]{:S(2)}, u32[]{:S(2)}) %collective-permute-start.20) | collective-permute-done | bytes 98336 | tf_op jit(solution)/shard_map/ppermute | solution.py:338
  97.0 3.0 %collective-permute-start.21 = (bf16[192,512]{1,0:T(8,128)(2,1)S(1)}, bf16[192,512]{1,0:T(8,128)(2,1)S(1)}, u32[]{:S(2)}, u32[]{:S(2)}) collective-permute-start(bf16[192,512]{1,0:T(8,128)(2,1)S(1)} %maximum_select_fusion.5), channel_id=1, source_target_pairs={{0,8},{2,18},{4,12},{6,22},{8,0},{10,26},{12,4},{14,30},{16,24},{1... | collective-permute-start | bytes 589832 | tf_op jit(solution)/shard_map/ppermute | solution.py:338
  106.3 3.6 %collective-permute-start.1 = (bf16[2,512,512]{2,1,0:T(8,128)(2,1)S(1)}, bf16[2,512,512]{2,1,0:T(8,128)(2,1)S(1)}, u32[]{:S(2)}, u32[]{:S(2)}) collective-permute-start(bf16[2,512,512]{2,1,0:T(8,128)(2,1)S(1)} %copy-done.3), channel_id=1, source_target_pairs={{2,0},{4,2},{6,4},{8,6},{10,8},{12,10},{14,12},{16,14},{18,16},{20... | collective-permute-start | bytes 3145736 | tf_op jit(solution)/shard_map/ppermute | solution.py:453
  112.4 28.5 %collective-permute-done.22 = bf16[384,512]{1,0:T(8,128)(2,1)S(1)} collective-permute-done((bf16[384,512]{1,0:T(8,128)(2,1)S(1)}, bf16[384,512]{1,0:T(8,128)(2,1)S(1)}, u32[]{:S(2)}, u32[]{:S(2)}) %collective-permute-start.22) | collective-permute-done | bytes 393248 | tf_op jit(solution)/shard_map/ppermute | solution.py:338
  143.3 4.4 %window_side.3.window_ref = f32[512,512]{1,0:T(8,128)S(1)} custom-call(bf16[2,512,512]{2,1,0:T(8,128)(2,1)} %q_in.7, bf16[2,512,512]{2,1,0:T(8,128)(2,1)} %copy-done.4, bf16[2,512,512]{2,1,0:T(8,128)(2,1)} %copy-done.17, bf16[2,512,512]{2,1,0:T(8,128)(2,1)} %copy-done.14), custom_call_target="tpu_custom_call" | custom-call | tf_op jit(solution)/shard_map/window_side/pallas_call | solution.py:192
  147.7 3.3 %query_side.3.refs_0_ = bf16[512,512]{1,0:T(8,128)(2,1)S(1)} custom-call(bf16[2,512,512]{2,1,0:T(8,128)(2,1)} %q_in.7, f32[1,512]{1,0:T(1,128)S(1)} %copy-done.10, f32[512,512]{1,0:T(8,128)S(1)} %window_side.3.window_ref, bf16[1,512,512]{2,1,0:T(8,128)(2,1)} %refs_0_.3, bf16[1,512,512]{2,1,0:T(8,128)(2,1)} %refs_1_.3, bf16[1,512,512]{2,1,0:T(8,128)(2,1)} %refs_2_.5), custom_call_target="tpu_custom_call" | custom-call | tf_op jit(solution)/shard_map/query_side/pallas_call | solution.py:237
  154.6 4.4 %window_side.2.window_ref = f32[512,512]{1,0:T(8,128)S(1)} custom-call(bf16[2,512,512]{2,1,0:T(8,128)(2,1)} %q_in.7, bf16[2,512,512]{2,1,0:T(8,128)(2,1)} %copy-done.2, bf16[2,512,512]{2,1,0:T(8,128)(2,1)} %copy-done.16, bf16[2,512,512]{2,1,0:T(8,128)(2,1)} %copy-done.15), custom_call_target="tpu_custom_call" | custom-call | tf_op jit(solution)/shard_map/window_side/pallas_call | solution.py:192
  162.4 3.5 %collective-permute-done.15.refs_1_ = bf16[512,512]{1,0:T(8,128)(2,1)S(1)} collective-permute-done((bf16[512,512]{1,0:T(8,128)(2,1)S(1)}, bf16[512,512]{1,0:T(8,128)(2,1)S(1)}, u32[]{:S(2)}, u32[]{:S(2)}) %collective-permute-start.15) | collective-permute-done | bytes 524320 | tf_op jit(solution)/shard_map/ppermute | solution.py:479
  165.9 5.4 %project.2.refs_5_ = bf16[2,512,2560]{2,1,0:T(8,128)(2,1)} custom-call(s32[2]{0:T(128)S(1)} %pad_add_fusion.place_ref, bf16[512,512]{1,0:T(8,128)(2,1)S(1)} %query_side.3.refs_0_, bf16[512,512]{1,0:T(8,128)(2,1)S(1)} %collective-permute-done.15.refs_1_, bf16[512,5120]{1,0:T(8,128)(2,1)S(1)} %bitcast.12, ...), custom_call_target="tpu_custom_call" | custom-call | tf_op jit(solution)/shard_map/project/pallas_call | solution.py:282
  171.3 5.2 %collective-permute-done.10.refs_1_ = bf16[512,512]{1,0:T(8,128)(2,1)S(1)} collective-permute-done((bf16[512,512]{1,0:T(8,128)(2,1)S(1)}, bf16[512,512]{1,0:T(8,128)(2,1)S(1)}, u32[]{:S(2)}, u32[]{:S(2)}) %collective-permute-start.10) | collective-permute-done | bytes 524320 | tf_op jit(solution)/shard_map/ppermute | solution.py:479
  176.5 5.3 %project.3 = bf16[2,512,2560]{2,1,0:T(8,128)(2,1)} custom-call(s32[2]{0:T(128)S(1)} %pad_add_fusion.place_ref, bf16[512,512]{1,0:T(8,128)(2,1)S(1)} %query_side.2.refs_0_, bf16[512,512]{1,0:T(8,128)(2,1)S(1)} %collective-permute-done.10.refs_1_, bf16[512,5120]{1,0:T(8,128)(2,1)S(1)} %bitcast.12, ...), custom_call_target="tpu_custom_call", output_to_operand_aliasing={{}: (6, {})} | custom-call | tf_op jit(solution)/shard_map/project/pallas_call | solution.py:282
  (94 shorter events, 49.4 us)
Async XLA Ops:
  6.7 2.4 %collective-permute-start.2 = (bf16[768,512]{1,0:T(8,128)(2,1)S(1)}, bf16[768,512]{1,0:T(8,128)(2,1)S(1)}, u32[]{:S(2)}, u32[]{:S(2)}) collective-permute-start(bf16[768,512]{1,0:T(8,128)(2,1)S(1)} %get-tuple-element.18), channel_id=1, source_target_pairs={{0,2},{2,0},{4,6},{6,4},{8,10},{10,8},{12,14},{14,12},{16,18},{18,... | collective-permute-start | bytes 2359304 | tf_op jit(solution)/shard_map/ppermute | solution.py:403
  9.1 7.8 %collective-permute-start.3 = (bf16[384,512]{1,0:T(8,128)(2,1)S(1)}, bf16[384,512]{1,0:T(8,128)(2,1)S(1)}, u32[]{:S(2)}, u32[]{:S(2)}) collective-permute-start(bf16[384,512]{1,0:T(8,128)(2,1)S(1)} %partial_sum.6), channel_id=1, source_target_pairs={{0,4},{2,10},{4,0},{6,14},{8,12},{10,2},{12,8},{14,6},{16,20},{18,... | collective-permute-start | bytes 1179656 | tf_op jit(solution)/shard_map/ppermute | solution.py:338
  17.0 7.2 %collective-permute-start.4 = (bf16[192,512]{1,0:T(8,128)(2,1)S(1)}, bf16[192,512]{1,0:T(8,128)(2,1)S(1)}, u32[]{:S(2)}, u32[]{:S(2)}) collective-permute-start(bf16[192,512]{1,0:T(8,128)(2,1)S(1)} %partial_sum.7), channel_id=1, source_target_pairs={{0,8},{2,18},{4,12},{6,22},{8,0},{10,26},{12,4},{14,30},{16,24},{1... | collective-permute-start | bytes 589832 | tf_op jit(solution)/shard_map/ppermute | solution.py:338
  24.2 6.4 %collective-permute-start.5 = (bf16[96,512]{1,0:T(8,128)(2,1)S(1)}, bf16[96,512]{1,0:T(8,128)(2,1)S(1)}, u32[]{:S(2)}, u32[]{:S(2)}) collective-permute-start(bf16[96,512]{1,0:T(8,128)(2,1)S(1)} %partial_sum.8), channel_id=1, source_target_pairs={{0,16},{2,6},{4,20},{6,2},{8,24},{10,14},{12,28},{14,10},{16,0},{1... | collective-permute-start | bytes 294920 | tf_op jit(solution)/shard_map/ppermute | solution.py:338
  31.5 7.7 %collective-permute-start.6 = (bf16[96,512]{1,0:T(8,128)(2,1)S(1)}, bf16[96,512]{1,0:T(8,128)(2,1)S(1)}, u32[]{:S(2)}, u32[]{:S(2)}) collective-permute-start(bf16[96,512]{1,0:T(8,128)(2,1)S(1)} %get-tuple-element.19), channel_id=1, source_target_pairs={{0,16},{2,6},{4,20},{6,2},{8,24},{10,14},{12,28},{14,10},{16,0},{1... | collective-permute-start | bytes 294920 | tf_op jit(solution)/shard_map/ppermute | solution.py:338
  39.2 9.2 %collective-permute-start.7 = (bf16[192,512]{1,0:T(8,128)(2,1)S(1)}, bf16[192,512]{1,0:T(8,128)(2,1)S(1)}, u32[]{:S(2)}, u32[]{:S(2)}) collective-permute-start(bf16[192,512]{1,0:T(8,128)(2,1)S(1)} %maximum_select_fusion.4), channel_id=1, source_target_pairs={{0,8},{2,18},{4,12},{6,22},{8,0},{10,26},{12,4},{14,30},{16,24},{1... | collective-permute-start | bytes 589832 | tf_op jit(solution)/shard_map/ppermute | solution.py:338
  48.5 7.8 %collective-permute-start.8 = (bf16[384,512]{1,0:T(8,128)(2,1)S(1)}, bf16[384,512]{1,0:T(8,128)(2,1)S(1)}, u32[]{:S(2)}, u32[]{:S(2)}) collective-permute-start(bf16[384,512]{1,0:T(8,128)(2,1)S(1)} %maximum_select_fusion.2), channel_id=1, source_target_pairs={{0,4},{2,10},{4,0},{6,14},{8,12},{10,2},{12,8},{14,6},{16,20},{18,... | collective-permute-start | bytes 1179656 | tf_op jit(solution)/shard_map/ppermute | solution.py:338
  56.7 2.4 %collective-permute-start.9 = (bf16[768,512]{1,0:T(8,128)(2,1)S(1)}, bf16[768,512]{1,0:T(8,128)(2,1)S(1)}, u32[]{:S(2)}, u32[]{:S(2)}) collective-permute-start(bf16[768,512]{1,0:T(8,128)(2,1)S(1)} %maximum_select_fusion.refs_0_), channel_id=1, source_target_pairs={{0,2},{2,0},{4,6},{6,4},{8,10},{10,8},{12,14},{14,12},{16,18},{18,... | collective-permute-start | bytes 2359304 | tf_op jit(solution)/shard_map/ppermute | solution.py:421
  63.8 2.4 %collective-permute-start.16 = (bf16[768,512]{1,0:T(8,128)(2,1)S(1)}, bf16[768,512]{1,0:T(8,128)(2,1)S(1)}, u32[]{:S(2)}, u32[]{:S(2)}) collective-permute-start(bf16[768,512]{1,0:T(8,128)(2,1)S(1)} %get-tuple-element.23), channel_id=1, source_target_pairs={{0,2},{2,0},{4,6},{6,4},{8,10},{10,8},{12,14},{14,12},{16,18},{18,... | collective-permute-start | bytes 2359304 | tf_op jit(solution)/shard_map/ppermute | solution.py:403
  67.0 8.0 %collective-permute-start.17 = (bf16[384,512]{1,0:T(8,128)(2,1)}, bf16[384,512]{1,0:T(8,128)(2,1)S(1)}, u32[]{:S(2)}, u32[]{:S(2)}) collective-permute-start(bf16[384,512]{1,0:T(8,128)(2,1)} %partial_sum.9), channel_id=1, source_target_pairs={{0,4},{2,10},{4,0},{6,14},{8,12},{10,2},{12,8},{14,6},{16,20},{18,... | collective-permute-start | bytes 1179656 | tf_op jit(solution)/shard_map/ppermute | solution.py:338
  68.9 41.0 %collective-permute-start.11 = (bf16[256,2560]{1,0:T(8,128)(2,1)S(1)}, bf16[256,2560]{1,0:T(8,128)(2,1)S(1)}, u32[]{:S(2)}, u32[]{:S(2)}) collective-permute-start(bf16[256,2560]{1,0:T(8,128)(2,1)S(1)} %dynamic_slice.7), channel_id=1, source_target_pairs={{0,1},{1,0},{2,3},{3,2},{4,5},{5,4},{6,7},{7,6},{8,9},{9,8},{10,11... | collective-permute-start | bytes 3932168 | tf_op jit(solution)/shard_map/ppermute | solution.py:459
  75.0 7.1 %collective-permute-start.18 = (bf16[192,512]{1,0:T(8,128)(2,1)S(1)}, bf16[192,512]{1,0:T(8,128)(2,1)S(1)}, u32[]{:S(2)}, u32[]{:S(2)}) collective-permute-start(bf16[192,512]{1,0:T(8,128)(2,1)S(1)} %partial_sum.10), channel_id=1, source_target_pairs={{0,8},{2,18},{4,12},{6,22},{8,0},{10,26},{12,4},{14,30},{16,24},{1... | collective-permute-start | bytes 589832 | tf_op jit(solution)/shard_map/ppermute | solution.py:338
  82.2 5.6 %collective-permute-start.19 = (bf16[96,512]{1,0:T(8,128)(2,1)S(1)}, bf16[96,512]{1,0:T(8,128)(2,1)S(1)}, u32[]{:S(2)}, u32[]{:S(2)}) collective-permute-start(bf16[96,512]{1,0:T(8,128)(2,1)S(1)} %partial_sum.11), channel_id=1, source_target_pairs={{0,16},{2,6},{4,20},{6,2},{8,24},{10,14},{12,28},{14,10},{16,0},{1... | collective-permute-start | bytes 294920 | tf_op jit(solution)/shard_map/ppermute | solution.py:338
  88.6 8.3 %collective-permute-start.20 = (bf16[96,512]{1,0:T(8,128)(2,1)S(1)}, bf16[96,512]{1,0:T(8,128)(2,1)S(1)}, u32[]{:S(2)}, u32[]{:S(2)}) collective-permute-start(bf16[96,512]{1,0:T(8,128)(2,1)S(1)} %get-tuple-element.24), channel_id=1, source_target_pairs={{0,16},{2,6},{4,20},{6,2},{8,24},{10,14},{12,28},{14,10},{16,0},{1... | collective-permute-start | bytes 294920 | tf_op jit(solution)/shard_map/ppermute | solution.py:338
  97.0 6.6 %collective-permute-start.21 = (bf16[192,512]{1,0:T(8,128)(2,1)S(1)}, bf16[192,512]{1,0:T(8,128)(2,1)S(1)}, u32[]{:S(2)}, u32[]{:S(2)}) collective-permute-start(bf16[192,512]{1,0:T(8,128)(2,1)S(1)} %maximum_select_fusion.5), channel_id=1, source_target_pairs={{0,8},{2,18},{4,12},{6,22},{8,0},{10,26},{12,4},{14,30},{16,24},{1... | collective-permute-start | bytes 589832 | tf_op jit(solution)/shard_map/ppermute | solution.py:338
  100.0 41.2 %collective-permute-start.14 = (bf16[2,512,512]{2,1,0:T(8,128)(2,1)S(1)}, bf16[2,512,512]{2,1,0:T(8,128)(2,1)S(1)}, u32[]{:S(2)}, u32[]{:S(2)}) collective-permute-start(bf16[2,512,512]{2,1,0:T(8,128)(2,1)S(1)} %copy-done.5), channel_id=1, source_target_pairs={{2,0},{4,2},{6,4},{8,6},{10,8},{12,10},{14,12},{16,14},{18,16},{20... | collective-permute-start | bytes 3145736 | tf_op jit(solution)/shard_map/ppermute | solution.py:453
  103.8 37.1 %collective-permute-start.22 = (bf16[384,512]{1,0:T(8,128)(2,1)S(1)}, bf16[384,512]{1,0:T(8,128)(2,1)S(1)}, u32[]{:S(2)}, u32[]{:S(2)}) collective-permute-start(bf16[384,512]{1,0:T(8,128)(2,1)S(1)} %maximum_select_fusion.3), channel_id=1, source_target_pairs={{0,4},{2,10},{4,0},{6,14},{8,12},{10,2},{12,8},{14,6},{16,20},{18,... | collective-permute-start | bytes 1179656 | tf_op jit(solution)/shard_map/ppermute | solution.py:338
  104.4 38.0 %collective-permute-start.13 = (bf16[2,512,512]{2,1,0:T(8,128)(2,1)S(1)}, bf16[2,512,512]{2,1,0:T(8,128)(2,1)S(1)}, u32[]{:S(2)}, u32[]{:S(2)}) collective-permute-start(bf16[2,512,512]{2,1,0:T(8,128)(2,1)S(1)} %copy-done.5), channel_id=1, source_target_pairs={{0,2},{2,4},{4,6},{6,8},{8,10},{10,12},{12,14},{14,16},{16,18},{18... | collective-permute-start | bytes 3145736 | tf_op jit(solution)/shard_map/ppermute | solution.py:452
  106.3 45.8 %collective-permute-start.1 = (bf16[2,512,512]{2,1,0:T(8,128)(2,1)S(1)}, bf16[2,512,512]{2,1,0:T(8,128)(2,1)S(1)}, u32[]{:S(2)}, u32[]{:S(2)}) collective-permute-start(bf16[2,512,512]{2,1,0:T(8,128)(2,1)S(1)} %copy-done.3), channel_id=1, source_target_pairs={{2,0},{4,2},{6,4},{8,6},{10,8},{12,10},{14,12},{16,14},{18,16},{20... | collective-permute-start | bytes 3145736 | tf_op jit(solution)/shard_map/ppermute | solution.py:453
  109.9 43.6 %collective-permute-start = (bf16[2,512,512]{2,1,0:T(8,128)(2,1)S(1)}, bf16[2,512,512]{2,1,0:T(8,128)(2,1)S(1)}, u32[]{:S(2)}, u32[]{:S(2)}) collective-permute-start(bf16[2,512,512]{2,1,0:T(8,128)(2,1)S(1)} %copy-done.3), channel_id=1, source_target_pairs={{0,2},{2,4},{4,6},{6,8},{8,10},{10,12},{12,14},{14,16},{16,18},{18... | collective-permute-start | bytes 3145736 | tf_op jit(solution)/shard_map/ppermute | solution.py:452
  140.9 25.0 %collective-permute-start.12 = (bf16[256,2560]{1,0:T(8,128)(2,1)S(1)}, bf16[256,2560]{1,0:T(8,128)(2,1)S(1)}, u32[]{:S(2)}, u32[]{:S(2)}) collective-permute-start(bf16[256,2560]{1,0:T(8,128)(2,1)S(1)} %collective-permute-done.11.refs_3_), channel_id=1, source_target_pairs={{0,2},{2,0},{4,6},{6,4},{8,10},{10,8},{12,14},{14,12},{16,18},{18,... | collective-permute-start | bytes 3932168 | tf_op jit(solution)/shard_map/ppermute | solution.py:461
  141.2 40.6 %collective-permute-start.23 = (bf16[768,512]{1,0:T(8,128)(2,1)S(1)}, bf16[768,512]{1,0:T(8,128)(2,1)S(1)}, u32[]{:S(2)}, u32[]{:S(2)}) collective-permute-start(bf16[768,512]{1,0:T(8,128)(2,1)S(1)} %maximum_select_fusion.1.mine_ref), channel_id=1, source_target_pairs={{0,2},{2,0},{4,6},{6,4},{8,10},{10,8},{12,14},{14,12},{16,18},{18,... | collective-permute-start | bytes 2359304 | tf_op jit(solution)/shard_map/ppermute | solution.py:421
  151.0 14.9 %collective-permute-start.15 = (bf16[512,512]{1,0:T(8,128)(2,1)S(1)}, bf16[512,512]{1,0:T(8,128)(2,1)S(1)}, u32[]{:S(2)}, u32[]{:S(2)}) collective-permute-start(bf16[512,512]{1,0:T(8,128)(2,1)S(1)} %query_side.3.refs_0_), channel_id=1, source_target_pairs={{0,1},{1,0},{2,3},{3,2},{4,5},{5,4},{6,7},{7,6},{8,9},{9,8},{10,11... | collective-permute-start | bytes 1572872 | tf_op jit(solution)/shard_map/ppermute | solution.py:479
  161.7 14.8 %collective-permute-start.10 = (bf16[512,512]{1,0:T(8,128)(2,1)S(1)}, bf16[512,512]{1,0:T(8,128)(2,1)S(1)}, u32[]{:S(2)}, u32[]{:S(2)}) collective-permute-start(bf16[512,512]{1,0:T(8,128)(2,1)S(1)} %query_side.2.refs_0_), channel_id=1, source_target_pairs={{0,1},{1,0},{2,3},{3,2},{4,5},{5,4},{6,7},{7,6},{8,9},{9,8},{10,11... | collective-permute-start | bytes 1572872 | tf_op jit(solution)/shard_map/ppermute | solution.py:479
  (20 other events, 161.3 us)

commit v3 on v2

--- a/solution.py
+++ b/solution.py
@@ -19,11 +19,6 @@
     return lax.dot_general(lhs, rhs, dims, preferred_element_type=F32)
 
 
-def whole(shape):
-    zeros = (0,) * len(shape)
-    return pl.BlockSpec(shape, lambda i, *refs: zeros)
-
-
 HBM = pl.BlockSpec(memory_space=pltpu.HBM)
 VMEM = pl.BlockSpec(memory_space=pltpu.VMEM)
 
@@ -51,7 +46,7 @@
 def weight_pairs(refs, target, hidden, gathered):
     if not gathered:
         return [(ref.at[0], target.at[pl.ds(n * hidden, hidden)]) for n, ref in enumerate(refs)]
-    c = lax.axis_index("ctx") & 1
+    c = class_of(lax.axis_index("ctx"))
     half = target.shape[0] // 2
     return [
         (ref, target.at[pl.ds(pl.multiple_of(at * half, 16), half)])
@@ -59,41 +54,22 @@
     ]
 
 
-def key_side(keys, values, rates, weights, group, gathered):
-    tokens, width = keys.shape[1:]
+def key_side(kv, rates, weights, group):
+    first_group = group == 0
+    tokens, width = kv.shape[1:]
     hidden = width
     rows = 3 * hidden
     half = rows // 2
     step = min(256, tokens)
     scale = width ** (-0.5)
-    first = NT if gathered else NN
-    second = NN if gathered else NT
+    first = NN if first_group else NT
+    second = NT if first_group else NN
     count = len(weights)
 
-    def kernel(k_in, v_in, rate_ref, *refs):
-        w_in, refs = refs[:count], refs[count:]
-        send_ref, keep_ref, *refs = refs
-        stacks, refs = ([], refs) if gathered else (refs[:GROUPS], refs[GROUPS:])
-        w_ref, k_all, v_all, hk, sc, d1, d3, grad, rate_col, sems, load_sems, stack_sems = refs
-        loads = fetch(weight_pairs(w_in, w_ref, hidden, gathered), sems)
-        wanted = [group] if gathered else list(range(GROUPS))
-        wanted.sort(key=lambda g: g != group)
-        fetched = fetch(
-            [(a.at[g], b.at[g]) for g in wanted for a, b in ((k_in, k_all), (v_in, v_all))],
-            load_sems,
-        )
+    def body(refs):
+        send_ref, keep_ref, kv, w_ref, _, hk, sc, d1, d3, grad, rate_col = refs
+        k_ref, v_ref = kv.at[0], kv.at[1]
         w1, w3, w2 = (w_ref.at[pl.ds(n * hidden, hidden)] for n in range(3))
-        k_ref, v_ref = k_all.at[group], v_all.at[group]
-        rate_col[...] = jnp.broadcast_to(rate_ref[group], (8, tokens)).T
-        wait(loads + fetched)
-        stacking = fetch(
-            [
-                (source.at[g], stack.at[n])
-                for g, stack in enumerate(stacks)
-                for n, source in enumerate((k_all, v_all))
-            ],
-            stack_sems,
-        )
 
         def forward(n, carry):
             at = pl.ds(n * step, step)
@@ -114,41 +90,69 @@
         lax.fori_loop(0, tokens // step, forward, 0)
         for n, (lhs, rhs, by) in enumerate(((d1, k_ref, scale), (d3, k_ref, scale), (sc, hk, -scale))):
             grad[pl.ds(n * hidden, hidden)] = dot(lhs[...], rhs[...], TN) * by
-        c = lax.axis_index("ctx") & 1
+        c = class_of(lax.axis_index("ctx"))
         send_ref[...] = grad[pl.ds(pl.multiple_of((1 - c) * half, 16), half)].astype(BF16)
         keep_ref[...] = grad[pl.ds(pl.multiple_of(c * half, 16), half)]
-        wait(stacking)
-
-    out_specs = [VMEM, VMEM]
+
+    def kernel(kv, rate_ref, *refs):
+        w_in, refs = refs[:count], refs[count:]
+        send_ref, keep_ref, *refs = refs
+        hk, sc, d1, d3, grad, rate_col, sems, *refs = refs
+        w_ref = w_in[0] if first_group else refs[0]
+        rate_col[...] = jnp.broadcast_to(rate_ref[group], (8, tokens)).T
+        if not first_group:
+            wait(fetch(weight_pairs(w_in, w_ref, hidden, True), sems))
+        body((send_ref, keep_ref, kv, w_ref, rate_ref, hk, sc, d1, d3, grad, rate_col))
+
     out_shape = [
         jax.ShapeDtypeStruct((half, width), BF16),
         jax.ShapeDtypeStruct((half, width), F32),
     ]
-    if not gathered:
-        out_specs += [HBM] * GROUPS
-        out_shape += [jax.ShapeDtypeStruct((2, tokens, width), BF16)] * GROUPS
-    return pl.pallas_call(
-        kernel,
-        in_specs=[HBM, HBM, VMEM] + [VMEM if gathered else HBM] * count,
-        out_specs=out_specs,
+    scratch = [pltpu.VMEM((tokens, hidden), BF16) for _ in range(4)]
+    scratch += [
+        pltpu.VMEM((rows, width), F32),
+        pltpu.VMEM((tokens, 8), F32),
+        pltpu.SemaphoreType.DMA((2,)),
+    ]
+    operands = [kv, rates, *weights]
+    in_specs = [VMEM] * len(operands)
+    if not first_group:
+        scratch.append(pltpu.VMEM((rows, width), BF16))
+    return pl.pallas_call(
+        kernel,
+        in_specs=in_specs,
+        out_specs=[VMEM] * len(out_shape),
         out_shape=out_shape,
-        scratch_shapes=[
-            pltpu.VMEM((rows, width), BF16),
-            pltpu.VMEM((GROUPS, tokens, width), BF16),
-            pltpu.VMEM((GROUPS, tokens, width), BF16),
-            *[pltpu.VMEM((tokens, hidden), BF16) for _ in range(4)],
-            pltpu.VMEM((rows, width), F32),
-            pltpu.VMEM((tokens, 8), F32),
-            pltpu.SemaphoreType.DMA((3,)),
-            pltpu.SemaphoreType.DMA((2 * GROUPS,)),
-            pltpu.SemaphoreType.DMA((2 * GROUPS,)),
-        ],
-        compiler_params=limit(28),
+        scratch_shapes=scratch,
+        compiler_params=limit(12),
         name="key_side",
-    )(*in_hbm(keys, values), rates, *(weights if gathered else in_hbm(*weights)))
-
-
-def window_side(query, own, before, after, group):
+    )(*operands)
+
+
+def side_by_side(keys, values, weights, group):
+    tokens, width = keys.shape[1:]
+    count = len(weights)
+
+    def kernel(k_in, v_in, *refs):
+        w_in, (kv, *w_ref, sems, w_sems) = refs[:count], refs[count:]
+        loads = fetch([(k_in.at[group], kv.at[0]), (v_in.at[group], kv.at[1])], sems)
+        wait(loads + (fetch(weight_pairs(w_in, w_ref[0], width, False), w_sems) if count else []))
+
+    out_shape = [jax.ShapeDtypeStruct((2, tokens, width), BF16)]
+    if count:
+        out_shape.append(jax.ShapeDtypeStruct((count * width, weights[0].shape[2]), BF16))
+    return pl.pallas_call(
+        kernel,
+        in_specs=[HBM] * (2 + count),
+        out_specs=[VMEM] * len(out_shape),
+        out_shape=out_shape,
+        scratch_shapes=[pltpu.SemaphoreType.DMA((2,)), pltpu.SemaphoreType.DMA((3,))],
+        compiler_params=limit(2),
+        name="side_by_side",
+    )(*in_hbm(keys, values, *weights))
+
+
+def window_side(query, keys, values, chip, near, far, group):
     tokens, width = query.shape[1:]
     reach = WINDOW // 2
     total = tokens + WINDOW
@@ -156,14 +160,28 @@
     span = step + WINDOW
     scale = width ** (-0.5)
 
-    def kernel(q_in, own_ref, before_ref, after_ref, out_ref, q_ref, k_all, v_all, sems):
-        places = (pl.ds(reach, tokens), pl.ds(0, reach), pl.ds(reach + tokens, reach))
+    def kernel(q_in, k_in, v_in, chip_ref, near_ref, far_ref, out_ref, q_ref, k_all, v_all, sems, far_sems):
+        index = lax.axis_index("ctx")
+        core = index & 1
+        other = class_of(index)
+        chip_at = pl.ds(pl.multiple_of((1 - core) * (reach + tokens), 128), reach)
+        far_at = pl.ds(pl.multiple_of(core * (reach + tokens), 128), reach)
         pairs = [(q_in.at[group], q_ref)]
-        for n, target in enumerate((k_all, v_all)):
-            for source, place in zip((own_ref, before_ref, after_ref), places):
-                pairs.append((source.at[n], target.at[place]))
-        wait(fetch(pairs, sems))
-        index = lax.axis_index("ctx")
+        copies = []
+        for n, (own_in, target) in enumerate(((k_in, k_all), (v_in, v_all))):
+            pairs.append((own_in.at[group], target.at[pl.ds(reach, tokens)]))
+            pairs.append((chip_ref.at[n], target.at[chip_at]))
+
+            @pl.when(other == 1)
+            def _():
+                pltpu.make_async_copy(near_ref.at[n], target.at[far_at], far_sems.at[n]).start()
+
+            @pl.when(other == 0)
+            def _():
+                pltpu.make_async_copy(far_ref.at[n], target.at[far_at], far_sems.at[n]).start()
+
+            copies.append(pltpu.make_async_copy(near_ref.at[n], target.at[far_at], far_sems.at[n]))
+        wait(fetch(pairs, sems) + copies)
         lowest = jnp.where(index == 0, reach, 0)
         highest = jnp.where(index == lax.axis_size("ctx") - 1, reach + tokens, total)
 
@@ -191,18 +209,19 @@
 
     return pl.pallas_call(
         kernel,
-        in_specs=[HBM] * 4,
+        in_specs=[HBM] * 6,
         out_specs=VMEM,
         out_shape=jax.ShapeDtypeStruct((tokens, width), F32),
         scratch_shapes=[
             pltpu.VMEM((tokens, width), BF16),
             pltpu.VMEM((total, width), BF16),
             pltpu.VMEM((total, width), BF16),
-            pltpu.SemaphoreType.DMA((7,)),
+            pltpu.SemaphoreType.DMA((5,)),
+            pltpu.SemaphoreType.DMA((2,)),
         ],
-        compiler_params=limit(20),
+        compiler_params=limit(12),
         name="window_side",
-    )(*in_hbm(query, own, before, after))
+    )(*in_hbm(query, keys, values), chip, near, far)
 
 
 def query_side(query, gain, window, weights, group, gathered):
@@ -244,54 +263,83 @@
             pltpu.VMEM((rows, width), BF16),
             pltpu.SemaphoreType.DMA((4,)),
         ],
-        compiler_params=limit(14),
+        compiler_params=limit(10),
         name="query_side",
     )(*in_hbm(query), gain, window, *(weights if gathered else in_hbm(*weights)))
 
 
-def project(place, heads, mine, near, far, group, mixed):
+CALLS = 2
+
+
+def tiles(features):
+    tile = 512 if features % 512 == 0 else 128
+    count = features // tile
+    middle = (count + 1) // CALLS
+    return tile, (range(middle), range(middle, count))
+
+
+def project(heads, mine, near, far, group, call, mixed):
     tokens, width = heads[0].shape
     count = len(heads)
-    features = near[0].shape[1] if near else mine.shape[1]
     part = width // 2
-    tile = 512 if features % 512 == 0 else 128
-
-    def kernel(place_ref, *refs):
+    features = mine.shape[1] // count
+    tile, shares = tiles(features)
+    share = shares[call]
+    blocks = len(share)
+
+    def kernel(*refs):
         head_refs, refs = refs[:count], refs[count:]
         mine_ref, refs = refs[0], refs[1:]
         near_refs, refs = refs[: count - 1], refs[count - 1 :]
         far_refs, refs = refs[: count - 1], refs[count - 1 :]
-        out_ref = refs[-1]
-        c = place_ref[0]
-        total = dot(head_refs[0][...], mine_ref[...], NN)
-        for head, one, two in zip(head_refs[1:], near_refs, far_refs):
-            total += dot(head[:, pl.ds(pl.multiple_of(c * part, 128), part)], one[...], NN)
-            total += dot(head[:, pl.ds(pl.multiple_of((1 - c) * part, 128), part)], two[...], NN)
-        out_ref[...] = total.astype(BF16)
-
-    blocks = features // tile
+        out_ref, w_ref, done_ref, sems, out_sems = refs[-5:]
+        c = lax.axis_index("ctx") & 1
+        start = lax.axis_index("head") * features
+        loads = fetch(
+            [
+                (mine_ref.at[:, pl.ds(pl.multiple_of(start + t * tile, 128), tile)], w_ref.at[n])
+                for n, t in enumerate(share)
+            ],
+            sems,
+        )
+        stores = []
+        for n, t in enumerate(share):
+            at = pl.ds(t * tile, tile)
+            total = None
+            for head, one, two in zip(head_refs[1:], near_refs, far_refs):
+                for source, half in ((one, c), (two, 1 - c)):
+                    rows = head[:, pl.ds(pl.multiple_of(half * part, 128), part)]
+                    term = dot(rows, source[:, at], NN)
+                    total = term if total is None else total + term
+            loads[n].wait()
+            term = dot(head_refs[0][...], w_ref[n], NN)
+            done_ref[n] = (term if total is None else total + term).astype(BF16)
+            stores += fetch([(done_ref.at[n], out_ref.at[group, :, at])], out_sems.at[pl.ds(n, 1)])
+        wait(stores)
+
     operands = [*heads, mine, *near, *far]
-    in_specs = [whole((tokens, width))] * count
-    in_specs += [pl.BlockSpec((width, tile), lambda i, at: (0, at[1] * blocks + i))]
-    in_specs += [pl.BlockSpec((part, tile), lambda i, at: (0, i))] * (2 * (count - 1))
+    in_specs = [VMEM] * count + [HBM] + [VMEM] * (2 * (count - 1))
+    operands[count] = in_hbm(mine)[0]
     aliases = {}
     if mixed is not None:
+        aliases = {len(operands): 0}
         operands.append(mixed)
         in_specs.append(HBM)
-        aliases = {len(operands): 0}
-    return pl.pallas_call(
-        kernel,
-        grid_spec=pltpu.PrefetchScalarGridSpec(
-            num_scalar_prefetch=1,
-            grid=(blocks,),
-            in_specs=in_specs,
-            out_specs=pl.BlockSpec((None, tokens, tile), lambda i, at: (group, 0, i)),
-        ),
+    return pl.pallas_call(
+        kernel,
+        in_specs=in_specs,
+        out_specs=HBM,
         out_shape=jax.ShapeDtypeStruct((GROUPS, tokens, features), BF16),
         input_output_aliases=aliases,
-        compiler_params=limit(20),
+        scratch_shapes=[
+            pltpu.VMEM((blocks, width, tile), BF16),
+            pltpu.VMEM((blocks, tokens, tile), BF16),
+            pltpu.SemaphoreType.DMA((blocks,)),
+            pltpu.SemaphoreType.DMA((blocks,)),
+        ],
+        compiler_params=limit(12),
         name="project",
-    )(place, *operands)
+    )(*operands)
 
 
 def matrices(mine, other):
@@ -325,22 +373,30 @@
 
 def orders(count):
     rest = list(range(1, count.bit_length() - 1))
-    return rest, rest[1:] + rest[:1]
+    return rest[1:] + rest[:1], rest
+
+
+def class_of(index):
+    return (index ^ (index >> 1)) & 1
 
 
 def swap_pairs(count):
     return [(i, i ^ 1) for i in range(count)]
 
 
+def mask(step_bit):
+    return 3 if step_bit == 1 else 1 << step_bit
+
+
 def exchange(value, count, step):
-    even, odd = orders(count)
-    pairs = [(i, i ^ (1 << (odd if i & 1 else even)[step])) for i in range(count)]
+    ones, others = orders(count)
+    pairs = [(i, i ^ mask((others if class_of(i) else ones)[step])) for i in range(count)]
     return lax.ppermute(value, "ctx", pairs)
 
 
 def own_bit(index, count, step):
-    even, odd = orders(count)
-    return jnp.where(index & 1, (index >> odd[step]) & 1, (index >> even[step]) & 1)
+    ones, others = orders(count)
+    return jnp.where(class_of(index) == 1, (index >> others[step]) & 1, (index >> ones[step]) & 1)
 
 
 def piece_rows(refs, index, count, steps, flip):
@@ -423,11 +479,38 @@
 
 def row_start(index, count, rows):
     rows //= 2
-    start = (index & 1) * rows
+    start = class_of(index) * rows
     for step in range(len(orders(count)[0])):
         rows //= 2
         start += own_bit(index, count, step) * rows
-    return start, rows
+    return start
+
+
+def own_rows(weights, count):
+    width, hidden = weights[0].shape[1:]
+    rows = 3 * hidden
+
+    def kernel(*refs):
+        w_in, (out_ref, w_ref, turned, sems) = refs[:3], refs[3:]
+        wait(fetch(weight_pairs(w_in, w_ref, width, False), sems))
+        for n in range(3):
+            turned[pl.ds(n * hidden, hidden)] = w_ref[pl.ds(n * width, width)].T
+        start = pl.multiple_of(row_start(lax.axis_index("ctx"), count, rows), 16)
+        out_ref[...] = turned[pl.ds(start, rows // count)].astype(F32)
+
+    return pl.pallas_call(
+        kernel,
+        in_specs=[HBM] * 3,
+        out_specs=VMEM,
+        out_shape=jax.ShapeDtypeStruct((rows // count, width), F32),
+        scratch_shapes=[
+            pltpu.VMEM((3 * width, hidden), BF16),
+            pltpu.VMEM((rows, width), BF16),
+            pltpu.SemaphoreType.DMA((3,)),
+        ],
+        compiler_params=limit(6),
+        name="own_rows",
+    )(*in_hbm(*weights))
 
 
 def layer(query, key_in, value, rates, w_in, w_gate, w_out, norm_gain, proj_weight):
@@ -441,16 +524,28 @@
     features = proj_weight.shape[1] // heads
     part = width // 2
 
-    natural = (w_in, w_gate, w_out)
-    send, keep, *stacks = key_side(key_in, value, rates, natural, 0, False)
-
-    up = [(i, i + 1) for i in range(count - 1)]
-    down = [(j, i) for i, j in up]
-    before = []
-    after = []
+    stacks = []
     for group in range(GROUPS):
-        before.append(lax.ppermute(stacks[group][:, tokens - reach :], "ctx", up))
-        after.append(lax.ppermute(stacks[group][:, :reach], "ctx", down))
+        kv, *natural = side_by_side(key_in, value, () if group else (w_in, w_gate, w_out), group)
+        stacks.append(kv)
+        if natural:
+            send, keep = key_side(kv, rates, natural, 0)
+
+    across = [(i, i + 1 if i & 1 else i - 1) for i in range(1, count - 1)]
+    near_pairs = [(i, j) for i, j in across if class_of(i)]
+    far_pairs = [(i, j) for i, j in across if not class_of(i)]
+    halos = []
+    for own in stacks:
+        to_chip = to_next = own
+        if tokens > reach:
+            at_end = (tokens - reach) * core
+            to_next = lax.dynamic_slice_in_dim(own, at_end, reach, 1)
+            to_chip = lax.dynamic_slice_in_dim(own, tokens - reach - at_end, reach, 1)
+        chip = lax.ppermute(to_chip, "ctx", swap_pairs(count))
+        near_halo = lax.ppermute(to_next, "ctx", near_pairs)
+        far_halo = lax.ppermute(to_next, "ctx", far_pairs)
+        halos.append((chip, near_halo, far_halo))
+
     near = []
     far = []
     for shift in range(1, heads):
@@ -459,26 +554,24 @@
         got = lax.ppermute(piece, "head", [(i, (i + shift) % heads) for i in range(heads)])
         near.append(got)
         far.append(lax.ppermute(got, "ctx", swap_pairs(count)))
-    place = jnp.stack([core, head.astype(jnp.int32)])
-
-    state_rows = jnp.concatenate([w_in[0].T, w_gate[0].T, w_out[0].T], axis=0)
-    offset, rows = row_start(index, count, state_rows.shape[0])
-    state = lax.dynamic_slice_in_dim(state_rows, offset, rows, 0).astype(F32)
-
-    weights = natural
+
+    state = own_rows((w_in, w_gate, w_out), count)
+
+    weights = (w_in, w_gate, w_out)
     mixed = None
     for group in range(GROUPS):
         gathered = group > 0
         if gathered:
-            send, keep = key_side(key_in, value, rates, weights, group, True)
-        window = window_side(query, stacks[group], before[group], after[group], group)
+            send, keep = key_side(stacks[group], rates, weights, group)
+        window = window_side(query, key_in, value, *halos[group], group)
         head_out = query_side(query, norm_gain, window, weights, group, gathered)
         outs = [head_out]
         for shift in range(1, heads):
             outs.append(
                 lax.ppermute(head_out, "head", [(i, (i + shift) % heads) for i in range(heads)])
             )
-        mixed = project(place, outs, proj_weight, near, far, group, mixed)
+        for call in range(CALLS):
+            mixed = project(outs, proj_weight, near, far, group, call, mixed)
         state, shard = next_state(state, send, keep, count)
         weights = gather_rows(shard, index, count)
     return (mixed, *matrices(*weights))

time: 186 us -> 158 us (0.85)
  the two profiles are of different devices: /device:TPU:14 before, /device:TPU:0 now
where the time goes in v3:
time: 158 us; the launch traced here: 157 us
  waiting for transfers between devices  83.3 us (53%)
  Pallas kernels  41.8 us (26%)
  starting transfers between devices  27.6 us (17%)
  local copies, waits for them, and re-layouts  2.2 us (1%)
    ppermute x12, waiting for transfers between devices, exchange(): return lax.ppermute(value, 'ctx', pairs)  69 us
    ppermute x12, starting transfers between devices, exchange(): return lax.ppermute(value, 'ctx', pairs)  18.6 us
    pallas_call x4, Pallas kernels, project(): pl.pallas_call(kernel, in_specs=in_specs, out_specs=HBM, out_shape=jax.Sh...  13 us
    ppermute x2, waiting for transfers between devices, layer(): lax.ppermute(head_out, 'head', [(i, (i + shift) % heads) for i in range(h...  9.74 us
    pallas_call x2, Pallas kernels, window_side(): pl.pallas_call(kernel, in_specs=[HBM] * 6, out_specs=VMEM, out_shape=jax....  7.86 us
    pallas_call x2, Pallas kernels, key_side(): pl.pallas_call(kernel, in_specs=in_specs, out_specs=[VMEM] * len(out_shap...  6.67 us
    pallas_call x2, Pallas kernels, query_side(): pl.pallas_call(kernel, in_specs=[HBM, VMEM, VMEM] + [VMEM if gathered els...  5.88 us
    ppermute x2, waiting for transfers between devices, next_state(): pieces = [keep, lax.ppermute(send, 'ctx', swap_pairs(count))]  3.82 us
  transfers between devices with their start and end apart: 26, of which 17 were waited for; matrix products, arithmetic and copies ran while one was open for 1% of the time, Pallas kernels for 20%

profile of v3, /device:TPU:0, one launch (start us, length us, event | category | flops | bytes accessed | tf_op | source)
XLA Modules:
  0.0 157.0 jit_solution(6620666218858655627)
XLA Ops:
  2.4 3.3 %key_side.2 = (bf16[768,512]{1,0:T(8,128)(2,1)S(1)}, f32[768,512]{1,0:T(8,128)S(1)}) custom-call(bf16[2,512,512]{2,1,0:T(8,128)(2,1)S(1)} %get-tuple-element.16.kv, f32[2,1,512]{2,1,0:T(1,128)S(1)} %copy-done.8, bf16[1536,512]{1,0:T(8,128)(2,1)S(1)} %get-tuple-element.17.refs_0_), custom_call_target="tpu_custom_call" | custom-call | tf_op jit(solution)/shard_map/key_side/pallas_call | solution.py:121
  8.2 3.0 %collective-permute-start.4 = (bf16[384,512]{1,0:T(8,128)(2,1)S(1)}, bf16[384,512]{1,0:T(8,128)(2,1)S(1)}, u32[]{:S(2)}, u32[]{:S(2)}) collective-permute-start(bf16[384,512]{1,0:T(8,128)(2,1)S(1)} %partial_sum.6), channel_id=1, source_target_pairs={{0,8},{2,4},{4,2},{6,14},{8,0},{10,12},{12,10},{14,6},{16,24},{18,... | collective-permute-start | bytes 1179656 | tf_op jit(solution)/shard_map/ppermute | solution.py:394
  11.2 5.8 %collective-permute-done.4.refs_2_ = bf16[384,512]{1,0:T(8,128)(2,1)S(1)} collective-permute-done((bf16[384,512]{1,0:T(8,128)(2,1)S(1)}, bf16[384,512]{1,0:T(8,128)(2,1)S(1)}, u32[]{:S(2)}, u32[]{:S(2)}) %collective-permute-start.4) | collective-permute-done | bytes 393248 | tf_op jit(solution)/shard_map/ppermute | solution.py:394
  17.0 3.1 %collective-permute-start.5 = (bf16[192,512]{1,0:T(8,128)(2,1)S(1)}, bf16[192,512]{1,0:T(8,128)(2,1)S(1)}, u32[]{:S(2)}, u32[]{:S(2)}) collective-permute-start(bf16[192,512]{1,0:T(8,128)(2,1)S(1)} %partial_sum.7), channel_id=1, source_target_pairs={{0,16},{2,10},{4,12},{6,22},{8,24},{10,2},{12,4},{14,30},{16,0},{1... | collective-permute-start | bytes 589832 | tf_op jit(solution)/shard_map/ppermute | solution.py:394
  20.1 4.5 %collective-permute-done.5.refs_3_ = bf16[192,512]{1,0:T(8,128)(2,1)S(1)} collective-permute-done((bf16[192,512]{1,0:T(8,128)(2,1)S(1)}, bf16[192,512]{1,0:T(8,128)(2,1)S(1)}, u32[]{:S(2)}, u32[]{:S(2)}) %collective-permute-start.5) | collective-permute-done | bytes 196640 | tf_op jit(solution)/shard_map/ppermute | solution.py:394
  30.5 3.2 %collective-permute-done.7 = bf16[96,512]{1,0:T(8,128)(2,1)S(1)} collective-permute-done((bf16[96,512]{1,0:T(8,128)(2,1)S(1)}, bf16[96,512]{1,0:T(8,128)(2,1)S(1)}, u32[]{:S(2)}, u32[]{:S(2)}) %collective-permute-start.7) | collective-permute-done | bytes 98336 | tf_op jit(solution)/shard_map/ppermute | solution.py:394
  36.0 4.5 %collective-permute-done.8 = bf16[192,512]{1,0:T(8,128)(2,1)S(1)} collective-permute-done((bf16[192,512]{1,0:T(8,128)(2,1)S(1)}, bf16[192,512]{1,0:T(8,128)(2,1)S(1)}, u32[]{:S(2)}, u32[]{:S(2)}) %collective-permute-start.8) | collective-permute-done | bytes 196640 | tf_op jit(solution)/shard_map/ppermute | solution.py:394
  40.6 3.0 %collective-permute-start.9 = (bf16[384,512]{1,0:T(8,128)(2,1)S(1)}, bf16[384,512]{1,0:T(8,128)(2,1)S(1)}, u32[]{:S(2)}, u32[]{:S(2)}) collective-permute-start(bf16[384,512]{1,0:T(8,128)(2,1)S(1)} %maximum_select_fusion.2), channel_id=1, source_target_pairs={{0,8},{2,4},{4,2},{6,14},{8,0},{10,12},{12,10},{14,6},{16,24},{18,... | collective-permute-start | bytes 1179656 | tf_op jit(solution)/shard_map/ppermute | solution.py:394
  43.6 5.8 %collective-permute-done.9 = bf16[384,512]{1,0:T(8,128)(2,1)S(1)} collective-permute-done((bf16[384,512]{1,0:T(8,128)(2,1)S(1)}, bf16[384,512]{1,0:T(8,128)(2,1)S(1)}, u32[]{:S(2)}, u32[]{:S(2)}) %collective-permute-start.9) | collective-permute-done | bytes 393248 | tf_op jit(solution)/shard_map/ppermute | solution.py:394
  52.2 3.4 %key_side.3 = (bf16[768,512]{1,0:T(8,128)(2,1)S(1)}, f32[768,512]{1,0:T(8,128)S(1)}) custom-call(bf16[2,512,512]{2,1,0:T(8,128)(2,1)S(1)} %side_by_side.2.kv, f32[2,1,512]{2,1,0:T(1,128)S(1)} %copy-done.8, bf16[768,512]{1,0:T(8,128)(2,1)S(1)} %maximum_select_fusion.refs_0_, bf16[768,512]{1,0:T(8,128)(2,1)S(1)} %collective-permute-done.10.refs_1_), custom_call_target="tpu_custom_call" | custom-call | tf_op jit(solution)/shard_map/key_side/pallas_call | solution.py:121
  66.9 3.2 %collective-permute-start.20 = (bf16[192,512]{1,0:T(8,128)(2,1)S(1)}, bf16[192,512]{1,0:T(8,128)(2,1)S(1)}, u32[]{:S(2)}, u32[]{:S(2)}) collective-permute-start(bf16[192,512]{1,0:T(8,128)(2,1)S(1)} %partial_sum.10), channel_id=1, source_target_pairs={{0,16},{2,10},{4,12},{6,22},{8,24},{10,2},{12,4},{14,30},{16,0},{1... | collective-permute-start | bytes 589832 | tf_op jit(solution)/shard_map/ppermute | solution.py:394
  70.1 20.1 %collective-permute-done.20.refs_3_ = bf16[192,512]{1,0:T(8,128)(2,1)S(1)} collective-permute-done((bf16[192,512]{1,0:T(8,128)(2,1)S(1)}, bf16[192,512]{1,0:T(8,128)(2,1)S(1)}, u32[]{:S(2)}, u32[]{:S(2)}) %collective-permute-start.20) | collective-permute-done | bytes 196640 | tf_op jit(solution)/shard_map/ppermute | solution.py:394
  90.3 4.0 %collective-permute-done.21.refs_4_ = bf16[96,512]{1,0:T(8,128)(2,1)S(1)} collective-permute-done((bf16[96,512]{1,0:T(8,128)(2,1)S(1)}, bf16[96,512]{1,0:T(8,128)(2,1)S(1)}, u32[]{:S(2)}, u32[]{:S(2)}) %collective-permute-start.21) | collective-permute-done | bytes 98336 | tf_op jit(solution)/shard_map/ppermute | solution.py:394
  95.5 3.7 %collective-permute-done.22 = bf16[96,512]{1,0:T(8,128)(2,1)S(1)} collective-permute-done((bf16[96,512]{1,0:T(8,128)(2,1)S(1)}, bf16[96,512]{1,0:T(8,128)(2,1)S(1)}, u32[]{:S(2)}, u32[]{:S(2)}) %collective-permute-start.22) | collective-permute-done | bytes 98336 | tf_op jit(solution)/shard_map/ppermute | solution.py:394
  99.4 8.4 %collective-permute-done.23 = bf16[192,512]{1,0:T(8,128)(2,1)S(1)} collective-permute-done((bf16[192,512]{1,0:T(8,128)(2,1)S(1)}, bf16[192,512]{1,0:T(8,128)(2,1)S(1)}, u32[]{:S(2)}, u32[]{:S(2)}) %collective-permute-start.23) | collective-permute-done | bytes 196640 | tf_op jit(solution)/shard_map/ppermute | solution.py:394
  109.6 6.2 %collective-permute-done.24 = bf16[384,512]{1,0:T(8,128)(2,1)S(1)} collective-permute-done((bf16[384,512]{1,0:T(8,128)(2,1)S(1)}, bf16[384,512]{1,0:T(8,128)(2,1)S(1)}, u32[]{:S(2)}, u32[]{:S(2)}) %collective-permute-start.24) | collective-permute-done | bytes 393248 | tf_op jit(solution)/shard_map/ppermute | solution.py:394
  116.7 3.8 %window_side.3.window_ref = f32[512,512]{1,0:T(8,128)S(1)} custom-call(bf16[2,512,512]{2,1,0:T(8,128)(2,1)} %q_in.7, bf16[2,512,512]{2,1,0:T(8,128)(2,1)} %k_in.7, bf16[2,512,512]{2,1,0:T(8,128)(2,1)} %v_in.7, bf16[2,512,512]{2,1,0:T(8,128)(2,1)S(1)} %collective-permute-done.14.chip_ref, bf16[2,512,512]{2,1,0:T(8,128)(2,1)S(1)} %collective-permute-done.15.near_ref, ...), custom_call_target="tpu_custom_call" | custom-call | tf_op jit(solution)/shard_map/window_side/pallas_call | solution.py:210
  120.5 3.2 %query_side.3.refs_0_ = bf16[512,512]{1,0:T(8,128)(2,1)S(1)} custom-call(bf16[2,512,512]{2,1,0:T(8,128)(2,1)} %q_in.7, f32[1,512]{1,0:T(1,128)S(1)} %copy-done.9, f32[512,512]{1,0:T(8,128)S(1)} %window_side.3.window_ref, bf16[1,512,512]{2,1,0:T(8,128)(2,1)} %refs_0_.5, bf16[1,512,512]{2,1,0:T(8,128)(2,1)} %refs_1_.5, bf16[1,512,512]{2,1,0:T(8,128)(2,1)} %refs_2_.9), custom_call_target="tpu_custom_call" | custom-call | tf_op jit(solution)/shard_map/query_side/pallas_call | solution.py:256
  123.8 4.0 %window_side.2.window_ref = f32[512,512]{1,0:T(8,128)S(1)} custom-call(bf16[2,512,512]{2,1,0:T(8,128)(2,1)} %q_in.7, bf16[2,512,512]{2,1,0:T(8,128)(2,1)} %k_in.7, bf16[2,512,512]{2,1,0:T(8,128)(2,1)} %v_in.7, bf16[2,512,512]{2,1,0:T(8,128)(2,1)S(1)} %collective-permute-done.chip_ref, bf16[2,512,512]{2,1,0:T(8,128)(2,1)S(1)} %collective-permute-done.1.near_ref, ...), custom_call_target="tpu_custom_call" | custom-call | tf_op jit(solution)/shard_map/window_side/pallas_call | solution.py:210
  132.6 5.6 %collective-permute-done.17.refs_1_ = bf16[512,512]{1,0:T(8,128)(2,1)S(1)} collective-permute-done((bf16[512,512]{1,0:T(8,128)(2,1)S(1)}, bf16[512,512]{1,0:T(8,128)(2,1)S(1)}, u32[]{:S(2)}, u32[]{:S(2)}) %collective-permute-start.17) | collective-permute-done | bytes 524320 | tf_op jit(solution)/shard_map/ppermute | solution.py:571
  138.3 3.5 %project.4.refs_5_ = bf16[2,512,2560]{2,1,0:T(8,128)(2,1)} custom-call(bf16[512,512]{1,0:T(8,128)(2,1)S(1)} %query_side.3.refs_0_, bf16[512,512]{1,0:T(8,128)(2,1)S(1)} %collective-permute-done.17.refs_1_, bf16[512,5120]{1,0:T(8,128)(2,1)} %refs_2_.13, bf16[256,2560]{1,0:T(8,128)(2,1)S(1)} %collective-permute-done.12.refs_3_, ...), custom_call_target="tpu_custom_call" | custom-call | tf_op jit(solution)/shard_map/project/pallas_call | solution.py:328
  141.8 2.9 %project.5.refs_5_ = bf16[2,512,2560]{2,1,0:T(8,128)(2,1)} custom-call(bf16[512,512]{1,0:T(8,128)(2,1)S(1)} %query_side.3.refs_0_, bf16[512,512]{1,0:T(8,128)(2,1)S(1)} %collective-permute-done.17.refs_1_, bf16[512,5120]{1,0:T(8,128)(2,1)} %refs_2_.13, bf16[256,2560]{1,0:T(8,128)(2,1)S(1)} %collective-permute-done.12.refs_3_, ...), custom_call_target="tpu_custom_call", output_to_operand_aliasing={{}: (5, {})} | custom-call | tf_op jit(solution)/shard_map/project/pallas_call | solution.py:328
  144.7 4.1 %collective-permute-done.11.refs_1_ = bf16[512,512]{1,0:T(8,128)(2,1)S(1)} collective-permute-done((bf16[512,512]{1,0:T(8,128)(2,1)S(1)}, bf16[512,512]{1,0:T(8,128)(2,1)S(1)}, u32[]{:S(2)}, u32[]{:S(2)}) %collective-permute-start.11) | collective-permute-done | bytes 524320 | tf_op jit(solution)/shard_map/ppermute | solution.py:571
  148.9 3.5 %project.6.refs_5_ = bf16[2,512,2560]{2,1,0:T(8,128)(2,1)} custom-call(bf16[512,512]{1,0:T(8,128)(2,1)S(1)} %query_side.2.refs_0_, bf16[512,512]{1,0:T(8,128)(2,1)S(1)} %collective-permute-done.11.refs_1_, bf16[512,5120]{1,0:T(8,128)(2,1)} %refs_2_.13, bf16[256,2560]{1,0:T(8,128)(2,1)S(1)} %collective-permute-done.12.refs_3_, ...), custom_call_target="tpu_custom_call", output_to_operand_aliasing={{}: (5, {})} | custom-call | tf_op jit(solution)/shard_map/project/pallas_call | solution.py:328
  (77 shorter events, 39.9 us)
Async XLA Ops:
  8.2 8.8 %collective-permute-start.4 = (bf16[384,512]{1,0:T(8,128)(2,1)S(1)}, bf16[384,512]{1,0:T(8,128)(2,1)S(1)}, u32[]{:S(2)}, u32[]{:S(2)}) collective-permute-start(bf16[384,512]{1,0:T(8,128)(2,1)S(1)} %partial_sum.6), channel_id=1, source_target_pairs={{0,8},{2,4},{4,2},{6,14},{8,0},{10,12},{12,10},{14,6},{16,24},{18,... | collective-permute-start | bytes 1179656 | tf_op jit(solution)/shard_map/ppermute | solution.py:394
  17.0 7.6 %collective-permute-start.5 = (bf16[192,512]{1,0:T(8,128)(2,1)S(1)}, bf16[192,512]{1,0:T(8,128)(2,1)S(1)}, u32[]{:S(2)}, u32[]{:S(2)}) collective-permute-start(bf16[192,512]{1,0:T(8,128)(2,1)S(1)} %partial_sum.7), channel_id=1, source_target_pairs={{0,16},{2,10},{4,12},{6,22},{8,24},{10,2},{12,4},{14,30},{16,0},{1... | collective-permute-start | bytes 589832 | tf_op jit(solution)/shard_map/ppermute | solution.py:394
  24.7 4.1 %collective-permute-start.6 = (bf16[96,512]{1,0:T(8,128)(2,1)S(1)}, bf16[96,512]{1,0:T(8,128)(2,1)S(1)}, u32[]{:S(2)}, u32[]{:S(2)}) collective-permute-start(bf16[96,512]{1,0:T(8,128)(2,1)S(1)} %partial_sum.8), channel_id=1, source_target_pairs={{0,6},{2,18},{4,20},{6,0},{8,14},{10,26},{12,28},{14,8},{16,22},{1... | collective-permute-start | bytes 294920 | tf_op jit(solution)/shard_map/ppermute | solution.py:394
  29.7 4.0 %collective-permute-start.7 = (bf16[96,512]{1,0:T(8,128)(2,1)S(1)}, bf16[96,512]{1,0:T(8,128)(2,1)S(1)}, u32[]{:S(2)}, u32[]{:S(2)}) collective-permute-start(bf16[96,512]{1,0:T(8,128)(2,1)S(1)} %get-tuple-element.20), channel_id=1, source_target_pairs={{0,6},{2,18},{4,20},{6,0},{8,14},{10,26},{12,28},{14,8},{16,22},{1... | collective-permute-start | bytes 294920 | tf_op jit(solution)/shard_map/ppermute | solution.py:394
  33.8 6.7 %collective-permute-start.8 = (bf16[192,512]{1,0:T(8,128)(2,1)S(1)}, bf16[192,512]{1,0:T(8,128)(2,1)S(1)}, u32[]{:S(2)}, u32[]{:S(2)}) collective-permute-start(bf16[192,512]{1,0:T(8,128)(2,1)S(1)} %maximum_select_fusion.4), channel_id=1, source_target_pairs={{0,16},{2,10},{4,12},{6,22},{8,24},{10,2},{12,4},{14,30},{16,0},{1... | collective-permute-start | bytes 589832 | tf_op jit(solution)/shard_map/ppermute | solution.py:394
  40.6 8.8 %collective-permute-start.9 = (bf16[384,512]{1,0:T(8,128)(2,1)S(1)}, bf16[384,512]{1,0:T(8,128)(2,1)S(1)}, u32[]{:S(2)}, u32[]{:S(2)}) collective-permute-start(bf16[384,512]{1,0:T(8,128)(2,1)S(1)} %maximum_select_fusion.2), channel_id=1, source_target_pairs={{0,8},{2,4},{4,2},{6,14},{8,0},{10,12},{12,10},{14,6},{16,24},{18,... | collective-permute-start | bytes 1179656 | tf_op jit(solution)/shard_map/ppermute | solution.py:394
  49.7 2.5 %collective-permute-start.10 = (bf16[768,512]{1,0:T(8,128)(2,1)S(1)}, bf16[768,512]{1,0:T(8,128)(2,1)S(1)}, u32[]{:S(2)}, u32[]{:S(2)}) collective-permute-start(bf16[768,512]{1,0:T(8,128)(2,1)S(1)} %maximum_select_fusion.refs_0_), channel_id=1, source_target_pairs={{0,2},{2,0},{4,6},{6,4},{8,10},{10,8},{12,14},{14,12},{16,18},{18,... | collective-permute-start | bytes 2359304 | tf_op jit(solution)/shard_map/ppermute | solution.py:477
  58.8 8.0 %collective-permute-start.19 = (bf16[384,512]{1,0:T(8,128)(2,1)}, bf16[384,512]{1,0:T(8,128)(2,1)S(1)}, u32[]{:S(2)}, u32[]{:S(2)}) collective-permute-start(bf16[384,512]{1,0:T(8,128)(2,1)} %partial_sum.9), channel_id=1, source_target_pairs={{0,8},{2,4},{4,2},{6,14},{8,0},{10,12},{12,10},{14,6},{16,24},{18,... | collective-permute-start | bytes 1179656 | tf_op jit(solution)/shard_map/ppermute | solution.py:394
  62.1 47.4 %collective-permute-start.12 = (bf16[256,2560]{1,0:T(8,128)(2,1)S(1)}, bf16[256,2560]{1,0:T(8,128)(2,1)S(1)}, u32[]{:S(2)}, u32[]{:S(2)}) collective-permute-start(bf16[256,2560]{1,0:T(8,128)(2,1)S(1)} %dynamic_slice.3), channel_id=1, source_target_pairs={{0,1},{1,0},{2,3},{3,2},{4,5},{5,4},{6,7},{7,6},{8,9},{9,8},{10,11... | collective-permute-start | bytes 3932168 | tf_op jit(solution)/shard_map/ppermute | solution.py:554
  63.8 44.2 %collective-permute-start.16 = (bf16[2,512,512]{2,1,0:T(8,128)(2,1)S(1)}, bf16[2,512,512]{2,1,0:T(8,128)(2,1)S(1)}, u32[]{:S(2)}, u32[]{:S(2)}) collective-permute-start(bf16[2,512,512]{2,1,0:T(8,128)(2,1)S(1)} %copy-done.5), channel_id=1, source_target_pairs={{6,8},{8,6},{14,16},{16,14},{22,24},{24,22},{7,9},{9,7},{15,17},{1... | collective-permute-start | bytes 3145736 | tf_op jit(solution)/shard_map/ppermute | solution.py:546
  64.6 44.2 %collective-permute-start.15 = (bf16[2,512,512]{2,1,0:T(8,128)(2,1)S(1)}, bf16[2,512,512]{2,1,0:T(8,128)(2,1)S(1)}, u32[]{:S(2)}, u32[]{:S(2)}) collective-permute-start(bf16[2,512,512]{2,1,0:T(8,128)(2,1)S(1)} %copy-done.5), channel_id=1, source_target_pairs={{2,4},{4,2},{10,12},{12,10},{18,20},{20,18},{26,28},{28,26},{3,5},... | collective-permute-start | bytes 3145736 | tf_op jit(solution)/shard_map/ppermute | solution.py:545
  66.9 23.3 %collective-permute-start.20 = (bf16[192,512]{1,0:T(8,128)(2,1)S(1)}, bf16[192,512]{1,0:T(8,128)(2,1)S(1)}, u32[]{:S(2)}, u32[]{:S(2)}) collective-permute-start(bf16[192,512]{1,0:T(8,128)(2,1)S(1)} %partial_sum.10), channel_id=1, source_target_pairs={{0,16},{2,10},{4,12},{6,22},{8,24},{10,2},{12,4},{14,30},{16,0},{1... | collective-permute-start | bytes 589832 | tf_op jit(solution)/shard_map/ppermute | solution.py:394
  90.2 4.1 %collective-permute-start.21 = (bf16[96,512]{1,0:T(8,128)(2,1)S(1)}, bf16[96,512]{1,0:T(8,128)(2,1)S(1)}, u32[]{:S(2)}, u32[]{:S(2)}) collective-permute-start(bf16[96,512]{1,0:T(8,128)(2,1)S(1)} %partial_sum.11), channel_id=1, source_target_pairs={{0,6},{2,18},{4,20},{6,0},{8,14},{10,26},{12,28},{14,8},{16,22},{1... | collective-permute-start | bytes 294920 | tf_op jit(solution)/shard_map/ppermute | solution.py:394
  95.2 4.0 %collective-permute-start.22 = (bf16[96,512]{1,0:T(8,128)(2,1)S(1)}, bf16[96,512]{1,0:T(8,128)(2,1)S(1)}, u32[]{:S(2)}, u32[]{:S(2)}) collective-permute-start(bf16[96,512]{1,0:T(8,128)(2,1)S(1)} %get-tuple-element.24), channel_id=1, source_target_pairs={{0,6},{2,18},{4,20},{6,0},{8,14},{10,26},{12,28},{14,8},{16,22},{1... | collective-permute-start | bytes 294920 | tf_op jit(solution)/shard_map/ppermute | solution.py:394
  99.3 8.5 %collective-permute-start.23 = (bf16[192,512]{1,0:T(8,128)(2,1)S(1)}, bf16[192,512]{1,0:T(8,128)(2,1)S(1)}, u32[]{:S(2)}, u32[]{:S(2)}) collective-permute-start(bf16[192,512]{1,0:T(8,128)(2,1)S(1)} %maximum_select_fusion.5), channel_id=1, source_target_pairs={{0,16},{2,10},{4,12},{6,22},{8,24},{10,2},{12,4},{14,30},{16,0},{1... | collective-permute-start | bytes 589832 | tf_op jit(solution)/shard_map/ppermute | solution.py:394
  99.4 16.8 %collective-permute-start.14 = (bf16[2,512,512]{2,1,0:T(8,128)(2,1)S(1)}, bf16[2,512,512]{2,1,0:T(8,128)(2,1)S(1)}, u32[]{:S(2)}, u32[]{:S(2)}) collective-permute-start(bf16[2,512,512]{2,1,0:T(8,128)(2,1)S(1)} %copy-done.5), channel_id=1, source_target_pairs={{0,2},{2,0},{4,6},{6,4},{8,10},{10,8},{12,14},{14,12},{16,18},{18,... | collective-permute-start | bytes 3145736 | tf_op jit(solution)/shard_map/ppermute | solution.py:544
  107.9 7.8 %collective-permute-start.24 = (bf16[384,512]{1,0:T(8,128)(2,1)S(1)}, bf16[384,512]{1,0:T(8,128)(2,1)S(1)}, u32[]{:S(2)}, u32[]{:S(2)}) collective-permute-start(bf16[384,512]{1,0:T(8,128)(2,1)S(1)} %maximum_select_fusion.3), channel_id=1, source_target_pairs={{0,8},{2,4},{4,2},{6,14},{8,0},{10,12},{12,10},{14,6},{16,24},{18,... | collective-permute-start | bytes 1179656 | tf_op jit(solution)/shard_map/ppermute | solution.py:394
  108.0 15.7 %collective-permute-start.2 = (bf16[2,512,512]{2,1,0:T(8,128)(2,1)S(1)}, bf16[2,512,512]{2,1,0:T(8,128)(2,1)S(1)}, u32[]{:S(2)}, u32[]{:S(2)}) collective-permute-start(bf16[2,512,512]{2,1,0:T(8,128)(2,1)S(1)} %copy-done.1), channel_id=1, source_target_pairs={{6,8},{8,6},{14,16},{16,14},{22,24},{24,22},{7,9},{9,7},{15,17},{1... | collective-permute-start | bytes 3145736 | tf_op jit(solution)/shard_map/ppermute | solution.py:546
  108.8 15.0 %collective-permute-start.1 = (bf16[2,512,512]{2,1,0:T(8,128)(2,1)S(1)}, bf16[2,512,512]{2,1,0:T(8,128)(2,1)S(1)}, u32[]{:S(2)}, u32[]{:S(2)}) collective-permute-start(bf16[2,512,512]{2,1,0:T(8,128)(2,1)S(1)} %copy-done.1), channel_id=1, source_target_pairs={{2,4},{4,2},{10,12},{12,10},{18,20},{20,18},{26,28},{28,26},{3,5},... | collective-permute-start | bytes 3145736 | tf_op jit(solution)/shard_map/ppermute | solution.py:545
  109.5 14.3 %collective-permute-start = (bf16[2,512,512]{2,1,0:T(8,128)(2,1)S(1)}, bf16[2,512,512]{2,1,0:T(8,128)(2,1)S(1)}, u32[]{:S(2)}, u32[]{:S(2)}) collective-permute-start(bf16[2,512,512]{2,1,0:T(8,128)(2,1)S(1)} %copy-done.1), channel_id=1, source_target_pairs={{0,2},{2,0},{4,6},{6,4},{8,10},{10,8},{12,14},{14,12},{16,18},{18,... | collective-permute-start | bytes 3145736 | tf_op jit(solution)/shard_map/ppermute | solution.py:544
  115.8 22.5 %collective-permute-start.13 = (bf16[256,2560]{1,0:T(8,128)(2,1)S(1)}, bf16[256,2560]{1,0:T(8,128)(2,1)S(1)}, u32[]{:S(2)}, u32[]{:S(2)}) collective-permute-start(bf16[256,2560]{1,0:T(8,128)(2,1)S(1)} %collective-permute-done.12.refs_3_), channel_id=1, source_target_pairs={{0,2},{2,0},{4,6},{6,4},{8,10},{10,8},{12,14},{14,12},{16,18},{18,... | collective-permute-start | bytes 3932168 | tf_op jit(solution)/shard_map/ppermute | solution.py:556
  116.1 39.3 %collective-permute-start.25 = (bf16[768,512]{1,0:T(8,128)(2,1)S(1)}, bf16[768,512]{1,0:T(8,128)(2,1)S(1)}, u32[]{:S(2)}, u32[]{:S(2)}) collective-permute-start(bf16[768,512]{1,0:T(8,128)(2,1)S(1)} %maximum_select_fusion.1.mine_ref), channel_id=1, source_target_pairs={{0,2},{2,0},{4,6},{6,4},{8,10},{10,8},{12,14},{14,12},{16,18},{18,... | collective-permute-start | bytes 2359304 | tf_op jit(solution)/shard_map/ppermute | solution.py:477
  123.7 14.5 %collective-permute-start.17 = (bf16[512,512]{1,0:T(8,128)(2,1)S(1)}, bf16[512,512]{1,0:T(8,128)(2,1)S(1)}, u32[]{:S(2)}, u32[]{:S(2)}) collective-permute-start(bf16[512,512]{1,0:T(8,128)(2,1)S(1)} %query_side.3.refs_0_), channel_id=1, source_target_pairs={{0,1},{1,0},{2,3},{3,2},{4,5},{5,4},{6,7},{7,6},{8,9},{9,8},{10,11... | collective-permute-start | bytes 1572872 | tf_op jit(solution)/shard_map/ppermute | solution.py:571
  130.6 18.3 %collective-permute-start.11 = (bf16[512,512]{1,0:T(8,128)(2,1)S(1)}, bf16[512,512]{1,0:T(8,128)(2,1)S(1)}, u32[]{:S(2)}, u32[]{:S(2)}) collective-permute-start(bf16[512,512]{1,0:T(8,128)(2,1)S(1)} %query_side.2.refs_0_), channel_id=1, source_target_pairs={{0,1},{1,0},{2,3},{3,2},{4,5},{5,4},{6,7},{7,6},{8,9},{9,8},{10,11... | collective-permute-start | bytes 1572872 | tf_op jit(solution)/shard_map/ppermute | solution.py:571
  (12 other events, 79.9 us)

commit v4 on v3

--- a/solution.py
+++ b/solution.py
@@ -129,16 +129,20 @@
     )(*operands)
 
 
-def side_by_side(keys, values, weights, group):
+def side_by_side(keys, values, weights, group, singles):
     tokens, width = keys.shape[1:]
     count = len(weights)
-
-    def kernel(k_in, v_in, *refs):
-        w_in, (kv, *w_ref, sems, w_sems) = refs[:count], refs[count:]
-        loads = fetch([(k_in.at[group], kv.at[0]), (v_in.at[group], kv.at[1])], sems)
+    sources = [(0, group), (1, group), *singles]
+
+    def kernel(*refs):
+        kv_in, w_in, refs = refs[:2], refs[2 : 2 + count], refs[2 + count :]
+        kv, targets, (*w_ref, sems, w_sems) = refs[0], refs[1 : 1 + len(singles)], refs[1 + len(singles) :]
+        targets = (kv.at[0], kv.at[1], *targets)
+        loads = fetch([(kv_in[n].at[g], to) for (n, g), to in zip(sources, targets)], sems)
         wait(loads + (fetch(weight_pairs(w_in, w_ref[0], width, False), w_sems) if count else []))
 
     out_shape = [jax.ShapeDtypeStruct((2, tokens, width), BF16)]
+    out_shape += [jax.ShapeDtypeStruct((tokens, width), BF16)] * len(singles)
     if count:
         out_shape.append(jax.ShapeDtypeStruct((count * width, weights[0].shape[2]), BF16))
     return pl.pallas_call(
@@ -146,7 +150,7 @@
         in_specs=[HBM] * (2 + count),
         out_specs=[VMEM] * len(out_shape),
         out_shape=out_shape,
-        scratch_shapes=[pltpu.SemaphoreType.DMA((2,)), pltpu.SemaphoreType.DMA((3,))],
+        scratch_shapes=[pltpu.SemaphoreType.DMA((len(sources),)), pltpu.SemaphoreType.DMA((3,))],
         compiler_params=limit(2),
         name="side_by_side",
     )(*in_hbm(keys, values, *weights))
@@ -160,7 +164,9 @@
     span = step + WINDOW
     scale = width ** (-0.5)
 
-    def kernel(q_in, k_in, v_in, chip_ref, near_ref, far_ref, out_ref, q_ref, k_all, v_all, sems, far_sems):
+    def kernel(q_in, k_in, v_in, chip_ref, near_ref, *refs):
+        far_refs, (out_ref, q_ref, k_all, v_all, sems, far_sems) = refs[:-6], refs[-6:]
+        far_parts = far_refs if len(far_refs) == 2 else (far_refs[0].at[0], far_refs[0].at[1])
         index = lax.axis_index("ctx")
         core = index & 1
         other = class_of(index)
@@ -178,7 +184,7 @@
 
             @pl.when(other == 0)
             def _():
-                pltpu.make_async_copy(far_ref.at[n], target.at[far_at], far_sems.at[n]).start()
+                pltpu.make_async_copy(far_parts[n], target.at[far_at], far_sems.at[n]).start()
 
             copies.append(pltpu.make_async_copy(near_ref.at[n], target.at[far_at], far_sems.at[n]))
         wait(fetch(pairs, sems) + copies)
@@ -209,7 +215,7 @@
 
     return pl.pallas_call(
         kernel,
-        in_specs=[HBM] * 6,
+        in_specs=[HBM] * (5 + len(far)),
         out_specs=VMEM,
         out_shape=jax.ShapeDtypeStruct((tokens, width), F32),
         scratch_shapes=[
@@ -221,7 +227,7 @@
         ],
         compiler_params=limit(12),
         name="window_side",
-    )(*in_hbm(query, keys, values), chip, near, far)
+    )(*in_hbm(query, keys, values), chip, near, *far)
 
 
 def query_side(query, gain, window, weights, group, gathered):
@@ -342,6 +348,29 @@
     )(*operands)
 
 
+def piece_for(weights, shift, heads):
+    width, features = weights.shape
+    part = width // 2
+    features //= heads
+
+    def kernel(in_ref, out_ref, sem):
+        c = lax.axis_index("ctx") & 1
+        target = (lax.axis_index("head") + shift) % heads
+        rows = pl.ds(pl.multiple_of(c * part, 16), part)
+        columns = pl.ds(pl.multiple_of(target * features, 128), features)
+        wait(fetch([(in_ref.at[rows, columns], out_ref)], sem))
+
+    return pl.pallas_call(
+        kernel,
+        in_specs=[HBM],
+        out_specs=VMEM,
+        out_shape=jax.ShapeDtypeStruct((part, features), weights.dtype),
+        scratch_shapes=[pltpu.SemaphoreType.DMA((1,))],
+        compiler_params=limit(2),
+        name="piece_for",
+    )(*in_hbm(weights))
+
+
 def matrices(mine, other):
     half, width = mine.shape
     rows = 2 * half
@@ -464,16 +493,29 @@
     return renormed(before, pieces, count, steps)
 
 
-def gather_rows(shard, index, count):
+def joined(shard, got, count, step):
+    rows, width = shard.shape
+
+    def kernel(shard_ref, got_ref, out_ref):
+        bit = own_bit(lax.axis_index("ctx"), count, step)
+        out_ref[pl.ds(pl.multiple_of(bit * rows, 16), rows)] = shard_ref[...]
+        out_ref[pl.ds(pl.multiple_of((1 - bit) * rows, 16), rows)] = got_ref[...]
+
+    return pl.pallas_call(
+        kernel,
+        in_specs=[VMEM] * 2,
+        out_specs=VMEM,
+        out_shape=jax.ShapeDtypeStruct((2 * rows, width), shard.dtype),
+        compiler_params=limit(4),
+        name="joined",
+    )(shard, got)
+
+
+def gather_rows(shard, count):
     steps = len(orders(count)[0])
     for step in reversed(range(steps)):
         got = exchange(shard, count, step)
-        bit = own_bit(index, count, step)
-        shard = jnp.where(
-            bit == 0,
-            jnp.concatenate([shard, got], axis=0),
-            jnp.concatenate([got, shard], axis=0),
-        )
+        shard = joined(shard, got, count, step)
     return shard, lax.ppermute(shard, "ctx", swap_pairs(count))
 
 
@@ -517,40 +559,37 @@
     count = lax.axis_size("ctx")
     heads = lax.axis_size("head")
     index = lax.axis_index("ctx").astype(jnp.int32)
-    head = lax.axis_index("head")
     core = (index & 1).astype(jnp.int32)
-    tokens, width = query.shape[1:]
+    tokens, _ = query.shape[1:]
     reach = WINDOW // 2
-    features = proj_weight.shape[1] // heads
-    part = width // 2
-
-    stacks = []
-    for group in range(GROUPS):
-        kv, *natural = side_by_side(key_in, value, () if group else (w_in, w_gate, w_out), group)
-        stacks.append(kv)
-        if natural:
-            send, keep = key_side(kv, rates, natural, 0)
+
+    kv, keys_only, natural = side_by_side(key_in, value, (w_in, w_gate, w_out), 0, [(0, 0)])
+    send, keep = key_side(kv, rates, [natural], 0)
+    later, values_only = side_by_side(key_in, value, (), 1, [(1, 0)])
 
     across = [(i, i + 1 if i & 1 else i - 1) for i in range(1, count - 1)]
     near_pairs = [(i, j) for i, j in across if class_of(i)]
     far_pairs = [(i, j) for i, j in across if not class_of(i)]
+
+    def edge(rows, at_end):
+        axis = rows.ndim - 2
+        if tokens == reach:
+            return rows
+        return lax.dynamic_slice_in_dim(rows, (tokens - reach) * at_end, reach, axis)
+
     halos = []
-    for own in stacks:
-        to_chip = to_next = own
-        if tokens > reach:
-            at_end = (tokens - reach) * core
-            to_next = lax.dynamic_slice_in_dim(own, at_end, reach, 1)
-            to_chip = lax.dynamic_slice_in_dim(own, tokens - reach - at_end, reach, 1)
-        chip = lax.ppermute(to_chip, "ctx", swap_pairs(count))
-        near_halo = lax.ppermute(to_next, "ctx", near_pairs)
-        far_halo = lax.ppermute(to_next, "ctx", far_pairs)
+    for own, alone in ((kv, (keys_only, values_only)), (later, (later,))):
+        chip = lax.ppermute(edge(own, 1 - core), "ctx", swap_pairs(count))
+        near_halo = lax.ppermute(edge(own, core), "ctx", near_pairs)
+        far_halo = []
+        for rows in alone:
+            far_halo.append(lax.ppermute(edge(rows, core), "ctx", far_pairs))
         halos.append((chip, near_halo, far_halo))
 
     near = []
     far = []
     for shift in range(1, heads):
-        target = (head + shift) % heads
-        piece = lax.dynamic_slice(proj_weight, (core * part, target * features), (part, features))
+        piece = piece_for(proj_weight, shift, heads)
         got = lax.ppermute(piece, "head", [(i, (i + shift) % heads) for i in range(heads)])
         near.append(got)
         far.append(lax.ppermute(got, "ctx", swap_pairs(count)))
@@ -562,7 +601,7 @@
     for group in range(GROUPS):
         gathered = group > 0
         if gathered:
-            send, keep = key_side(stacks[group], rates, weights, group)
+            send, keep = key_side(later, rates, weights, group)
         window = window_side(query, key_in, value, *halos[group], group)
         head_out = query_side(query, norm_gain, window, weights, group, gathered)
         outs = [head_out]
@@ -573,7 +612,7 @@
         for call in range(CALLS):
             mixed = project(outs, proj_weight, near, far, group, call, mixed)
         state, shard = next_state(state, send, keep, count)
-        weights = gather_rows(shard, index, count)
+        weights = gather_rows(shard, count)
     return (mixed, *matrices(*weights))
 
 

time: 158 us -> 160 us (1.013)
  the two profiles are of different devices: /device:TPU:0 before, /device:TPU:14 now
where the time goes in v4:
time: 160 us; the launch traced here: 158 us
  waiting for transfers between devices  80 us (50%)
  Pallas kernels  43.1 us (27%)
  starting transfers between devices  33.3 us (21%)
    ppermute x12, waiting for transfers between devices, exchange(): return lax.ppermute(value, 'ctx', pairs)  67.4 us
    ppermute x12, starting transfers between devices, exchange(): return lax.ppermute(value, 'ctx', pairs)  15.9 us
    pallas_call x4, Pallas kernels, project(): pl.pallas_call(kernel, in_specs=in_specs, out_specs=HBM, out_shape=jax.Sh...  12.9 us
    pallas_call x2, Pallas kernels, window_side(): pl.pallas_call(kernel, in_specs=[HBM] * (5 + len(far)), out_specs=VMEM, o...  7.84 us
    ppermute x2, waiting for transfers between devices, layer(): lax.ppermute(head_out, 'head', [(i, (i + shift) % heads) for i in range(h...  7.02 us
    pallas_call x2, Pallas kernels, key_side(): pl.pallas_call(kernel, in_specs=in_specs, out_specs=[VMEM] * len(out_shap...  6.73 us
    ppermute x2, starting transfers between devices, layer(): near_halo = lax.ppermute(edge(own, core), 'ctx', near_pairs)  6.26 us
    pallas_call x2, Pallas kernels, query_side(): pl.pallas_call(kernel, in_specs=[HBM, VMEM, VMEM] + [VMEM if gathered els...  5.87 us
  transfers between devices with their start and end apart: 27, of which 18 were waited for; matrix products, arithmetic and copies ran while one was open for 0% of the time, Pallas kernels for 21%

profile of v4, /device:TPU:14, one launch (start us, length us, event | category | flops | bytes accessed | tf_op | source)
XLA Modules:
  0.0 157.6 jit_solution(12643182906214349310)
XLA Ops:
  2.5 3.3 %key_side.2 = (bf16[768,512]{1,0:T(8,128)(2,1)S(1)}, f32[768,512]{1,0:T(8,128)S(1)}) custom-call(bf16[2,512,512]{2,1,0:T(8,128)(2,1)S(1)} %get-tuple-element.20.kv, f32[2,1,512]{2,1,0:T(1,128)S(1)} %copy-done, bf16[1536,512]{1,0:T(8,128)(2,1)S(1)} %get-tuple-element.21.refs_0_), custom_call_target="tpu_custom_call" | custom-call | tf_op jit(solution)/shard_map/key_side/pallas_call | solution.py:121
  8.6 6.9 %collective-permute-done.4.refs_2_ = bf16[384,512]{1,0:T(8,128)(2,1)S(1)} collective-permute-done((bf16[384,512]{1,0:T(8,128)(2,1)S(1)}, bf16[384,512]{1,0:T(8,128)(2,1)S(1)}, u32[]{:S(2)}, u32[]{:S(2)}) %collective-permute-start.4) | collective-permute-done | bytes 393248 | tf_op jit(solution)/shard_map/ppermute | solution.py:423
  16.1 7.2 %collective-permute-done.5.refs_3_ = bf16[192,512]{1,0:T(8,128)(2,1)S(1)} collective-permute-done((bf16[192,512]{1,0:T(8,128)(2,1)S(1)}, bf16[192,512]{1,0:T(8,128)(2,1)S(1)}, u32[]{:S(2)}, u32[]{:S(2)}) %collective-permute-start.5) | collective-permute-done | bytes 196640 | tf_op jit(solution)/shard_map/ppermute | solution.py:423
  31.9 3.0 %collective-permute-done.7.got_ref = bf16[96,512]{1,0:T(8,128)(2,1)S(1)} collective-permute-done((bf16[96,512]{1,0:T(8,128)(2,1)S(1)}, bf16[96,512]{1,0:T(8,128)(2,1)S(1)}, u32[]{:S(2)}, u32[]{:S(2)}) %collective-permute-start.7) | collective-permute-done | bytes 98336 | tf_op jit(solution)/shard_map/ppermute | solution.py:423
  35.1 5.5 %collective-permute-done.8.got_ref = bf16[192,512]{1,0:T(8,128)(2,1)S(1)} collective-permute-done((bf16[192,512]{1,0:T(8,128)(2,1)S(1)}, bf16[192,512]{1,0:T(8,128)(2,1)S(1)}, u32[]{:S(2)}, u32[]{:S(2)}) %collective-permute-start.8) | collective-permute-done | bytes 196640 | tf_op jit(solution)/shard_map/ppermute | solution.py:423
  40.7 7.2 %collective-permute-done.9.got_ref = bf16[384,512]{1,0:T(8,128)(2,1)S(1)} collective-permute-done((bf16[384,512]{1,0:T(8,128)(2,1)S(1)}, bf16[384,512]{1,0:T(8,128)(2,1)S(1)}, u32[]{:S(2)}, u32[]{:S(2)}) %collective-permute-start.9) | collective-permute-done | bytes 393248 | tf_op jit(solution)/shard_map/ppermute | solution.py:423
  50.4 3.4 %key_side.3 = (bf16[768,512]{1,0:T(8,128)(2,1)S(1)}, f32[768,512]{1,0:T(8,128)S(1)}) custom-call(bf16[2,512,512]{2,1,0:T(8,128)(2,1)S(1)} %get-tuple-element.19.kv, f32[2,1,512]{2,1,0:T(1,128)S(1)} %copy-done, bf16[768,512]{1,0:T(8,128)(2,1)S(1)} %joined.8.refs_0_, bf16[768,512]{1,0:T(8,128)(2,1)S(1)} %collective-permute-done.10.refs_1_), custom_call_target="tpu_custom_call" | custom-call | tf_op jit(solution)/shard_map/key_side/pallas_call | solution.py:121
  56.6 3.3 %collective-permute-start.15 = (bf16[2,512,512]{2,1,0:T(8,128)(2,1)S(1)}, bf16[2,512,512]{2,1,0:T(8,128)(2,1)S(1)}, u32[]{:S(2)}, u32[]{:S(2)}) collective-permute-start(bf16[2,512,512]{2,1,0:T(8,128)(2,1)S(1)} %get-tuple-element.20.kv), channel_id=1, source_target_pairs={{2,4},{4,2},{10,12},{12,10},{18,20},{20,18},{26,28},{28,26},{3,5},... | collective-permute-start | bytes 3145736 | tf_op jit(solution)/shard_map/ppermute | solution.py:583
  59.9 3.6 %collective-permute-done.20.refs_2_ = bf16[384,512]{1,0:T(8,128)(2,1)S(1)} collective-permute-done((bf16[384,512]{1,0:T(8,128)(2,1)S(1)}, bf16[384,512]{1,0:T(8,128)(2,1)S(1)}, u32[]{:S(2)}, u32[]{:S(2)}) %collective-permute-start.20) | collective-permute-done | bytes 393248 | tf_op jit(solution)/shard_map/ppermute | solution.py:423
  64.3 6.5 %collective-permute-done.21.refs_3_ = bf16[192,512]{1,0:T(8,128)(2,1)S(1)} collective-permute-done((bf16[192,512]{1,0:T(8,128)(2,1)S(1)}, bf16[192,512]{1,0:T(8,128)(2,1)S(1)}, u32[]{:S(2)}, u32[]{:S(2)}) %collective-permute-start.21) | collective-permute-done | bytes 196640 | tf_op jit(solution)/shard_map/ppermute | solution.py:423
  70.8 4.1 %collective-permute-start.22 = (bf16[96,512]{1,0:T(8,128)(2,1)S(1)}, bf16[96,512]{1,0:T(8,128)(2,1)S(1)}, u32[]{:S(2)}, u32[]{:S(2)}) collective-permute-start(bf16[96,512]{1,0:T(8,128)(2,1)S(1)} %partial_sum.11), channel_id=1, source_target_pairs={{0,6},{2,18},{4,20},{6,0},{8,14},{10,26},{12,28},{14,8},{16,22},{1... | collective-permute-start | bytes 294920 | tf_op jit(solution)/shard_map/ppermute | solution.py:423
  78.6 3.4 %collective-permute-start.23 = (bf16[96,512]{1,0:T(8,128)(2,1)S(1)}, bf16[96,512]{1,0:T(8,128)(2,1)S(1)}, u32[]{:S(2)}, u32[]{:S(2)}) collective-permute-start(bf16[96,512]{1,0:T(8,128)(2,1)S(1)} %get-tuple-element.30.shard_ref), channel_id=1, source_target_pairs={{0,6},{2,18},{4,20},{6,0},{8,14},{10,26},{12,28},{14,8},{16,22},{1... | collective-permute-start | bytes 294920 | tf_op jit(solution)/shard_map/ppermute | solution.py:423
  85.4 7.8 %collective-permute-done.24.got_ref = bf16[192,512]{1,0:T(8,128)(2,1)S(1)} collective-permute-done((bf16[192,512]{1,0:T(8,128)(2,1)S(1)}, bf16[192,512]{1,0:T(8,128)(2,1)S(1)}, u32[]{:S(2)}, u32[]{:S(2)}) %collective-permute-start.24) | collective-permute-done | bytes 196640 | tf_op jit(solution)/shard_map/ppermute | solution.py:423
  93.1 4.9 %collective-permute-start.14 = (bf16[2,512,512]{2,1,0:T(8,128)(2,1)S(1)}, bf16[2,512,512]{2,1,0:T(8,128)(2,1)S(1)}, u32[]{:S(2)}, u32[]{:S(2)}) collective-permute-start(bf16[2,512,512]{2,1,0:T(8,128)(2,1)S(1)} %get-tuple-element.20.kv), channel_id=1, source_target_pairs={{0,2},{2,0},{4,6},{6,4},{8,10},{10,8},{12,14},{14,12},{16,18},{18,... | collective-permute-start | bytes 3145736 | tf_op jit(solution)/shard_map/ppermute | solution.py:582
  102.6 13.9 %collective-permute-done.25.got_ref = bf16[384,512]{1,0:T(8,128)(2,1)S(1)} collective-permute-done((bf16[384,512]{1,0:T(8,128)(2,1)S(1)}, bf16[384,512]{1,0:T(8,128)(2,1)S(1)}, u32[]{:S(2)}, u32[]{:S(2)}) %collective-permute-start.25) | collective-permute-done | bytes 393248 | tf_op jit(solution)/shard_map/ppermute | solution.py:423
  117.3 3.8 %window_side.3.window_ref = f32[512,512]{1,0:T(8,128)S(1)} custom-call(bf16[2,512,512]{2,1,0:T(8,128)(2,1)} %q_in.7, bf16[2,512,512]{2,1,0:T(8,128)(2,1)} %k_in.3, bf16[2,512,512]{2,1,0:T(8,128)(2,1)} %v_in.3, bf16[2,512,512]{2,1,0:T(8,128)(2,1)S(1)} %collective-permute-done.14.chip_ref, bf16[2,512,512]{2,1,0:T(8,128)(2,1)S(1)} %collective-permute-done.15.near_ref, ...), custom_call_target="tpu_custom_call" | custom-call | tf_op jit(solution)/shard_map/window_side/pallas_call | solution.py:216
  121.1 3.1 %query_side.3.refs_0_ = bf16[512,512]{1,0:T(8,128)(2,1)S(1)} custom-call(bf16[2,512,512]{2,1,0:T(8,128)(2,1)} %q_in.7, f32[1,512]{1,0:T(1,128)S(1)} %copy-done.1, f32[512,512]{1,0:T(8,128)S(1)} %window_side.3.window_ref, bf16[1,512,512]{2,1,0:T(8,128)(2,1)} %refs_0_.7, bf16[1,512,512]{2,1,0:T(8,128)(2,1)} %refs_1_.7, bf16[1,512,512]{2,1,0:T(8,128)(2,1)} %refs_2_.9), custom_call_target="tpu_custom_call" | custom-call | tf_op jit(solution)/shard_map/query_side/pallas_call | solution.py:262
  127.8 4.0 %window_side.2.window_ref = f32[512,512]{1,0:T(8,128)S(1)} custom-call(bf16[2,512,512]{2,1,0:T(8,128)(2,1)} %q_in.7, bf16[2,512,512]{2,1,0:T(8,128)(2,1)} %k_in.3, bf16[2,512,512]{2,1,0:T(8,128)(2,1)} %v_in.3, bf16[2,512,512]{2,1,0:T(8,128)(2,1)S(1)} %collective-permute-done.chip_ref, bf16[2,512,512]{2,1,0:T(8,128)(2,1)S(1)} %collective-permute-done.1.near_ref, ...), custom_call_target="tpu_custom_call" | custom-call | tf_op jit(solution)/shard_map/window_side/pallas_call | solution.py:216
  135.9 3.2 %collective-permute-done.18.refs_1_ = bf16[512,512]{1,0:T(8,128)(2,1)S(1)} collective-permute-done((bf16[512,512]{1,0:T(8,128)(2,1)S(1)}, bf16[512,512]{1,0:T(8,128)(2,1)S(1)}, u32[]{:S(2)}, u32[]{:S(2)}) %collective-permute-start.18) | collective-permute-done | bytes 524320 | tf_op jit(solution)/shard_map/ppermute | solution.py:610
  139.1 3.5 %project.4.refs_5_ = bf16[2,512,2560]{2,1,0:T(8,128)(2,1)} custom-call(bf16[512,512]{1,0:T(8,128)(2,1)S(1)} %query_side.3.refs_0_, bf16[512,512]{1,0:T(8,128)(2,1)S(1)} %collective-permute-done.18.refs_1_, bf16[512,5120]{1,0:T(8,128)(2,1)} %refs_2_.13, bf16[256,2560]{1,0:T(8,128)(2,1)S(1)} %collective-permute-done.12.refs_3_, ...), custom_call_target="tpu_custom_call" | custom-call | tf_op jit(solution)/shard_map/project/pallas_call | solution.py:334
  142.7 2.9 %project.5.refs_5_ = bf16[2,512,2560]{2,1,0:T(8,128)(2,1)} custom-call(bf16[512,512]{1,0:T(8,128)(2,1)S(1)} %query_side.3.refs_0_, bf16[512,512]{1,0:T(8,128)(2,1)S(1)} %collective-permute-done.18.refs_1_, bf16[512,5120]{1,0:T(8,128)(2,1)} %refs_2_.13, bf16[256,2560]{1,0:T(8,128)(2,1)S(1)} %collective-permute-done.12.refs_3_, ...), custom_call_target="tpu_custom_call", output_to_operand_aliasing={{}: (5, {})} | custom-call | tf_op jit(solution)/shard_map/project/pallas_call | solution.py:334
  145.6 3.8 %collective-permute-done.11.refs_1_ = bf16[512,512]{1,0:T(8,128)(2,1)S(1)} collective-permute-done((bf16[512,512]{1,0:T(8,128)(2,1)S(1)}, bf16[512,512]{1,0:T(8,128)(2,1)S(1)}, u32[]{:S(2)}, u32[]{:S(2)}) %collective-permute-start.11) | collective-permute-done | bytes 524320 | tf_op jit(solution)/shard_map/ppermute | solution.py:610
  149.4 3.5 %project.6.refs_5_ = bf16[2,512,2560]{2,1,0:T(8,128)(2,1)} custom-call(bf16[512,512]{1,0:T(8,128)(2,1)S(1)} %query_side.2.refs_0_, bf16[512,512]{1,0:T(8,128)(2,1)S(1)} %collective-permute-done.11.refs_1_, bf16[512,5120]{1,0:T(8,128)(2,1)} %refs_2_.13, bf16[256,2560]{1,0:T(8,128)(2,1)S(1)} %collective-permute-done.12.refs_3_, ...), custom_call_target="tpu_custom_call", output_to_operand_aliasing={{}: (5, {})} | custom-call | tf_op jit(solution)/shard_map/project/pallas_call | solution.py:334
  153.0 2.9 %project.7 = bf16[2,512,2560]{2,1,0:T(8,128)(2,1)} custom-call(bf16[512,512]{1,0:T(8,128)(2,1)S(1)} %query_side.2.refs_0_, bf16[512,512]{1,0:T(8,128)(2,1)S(1)} %collective-permute-done.11.refs_1_, bf16[512,5120]{1,0:T(8,128)(2,1)} %refs_2_.13, bf16[256,2560]{1,0:T(8,128)(2,1)S(1)} %collective-permute-done.12.refs_3_, ...), custom_call_target="tpu_custom_call", output_to_operand_aliasing={{}: (5, {})} | custom-call | tf_op jit(solution)/shard_map/project/pallas_call | solution.py:334
  (63 shorter events, 41.5 us)
Async XLA Ops:
  8.3 7.3 %collective-permute-start.4 = (bf16[384,512]{1,0:T(8,128)(2,1)S(1)}, bf16[384,512]{1,0:T(8,128)(2,1)S(1)}, u32[]{:S(2)}, u32[]{:S(2)}) collective-permute-start(bf16[384,512]{1,0:T(8,128)(2,1)S(1)} %partial_sum.6), channel_id=1, source_target_pairs={{0,8},{2,4},{4,2},{6,14},{8,0},{10,12},{12,10},{14,6},{16,24},{18,... | collective-permute-start | bytes 1179656 | tf_op jit(solution)/shard_map/ppermute | solution.py:423
  15.6 7.7 %collective-permute-start.5 = (bf16[192,512]{1,0:T(8,128)(2,1)S(1)}, bf16[192,512]{1,0:T(8,128)(2,1)S(1)}, u32[]{:S(2)}, u32[]{:S(2)}) collective-permute-start(bf16[192,512]{1,0:T(8,128)(2,1)S(1)} %partial_sum.7), channel_id=1, source_target_pairs={{0,16},{2,10},{4,12},{6,22},{8,24},{10,2},{12,4},{14,30},{16,0},{1... | collective-permute-start | bytes 589832 | tf_op jit(solution)/shard_map/ppermute | solution.py:423
  23.4 5.6 %collective-permute-start.6 = (bf16[96,512]{1,0:T(8,128)(2,1)S(1)}, bf16[96,512]{1,0:T(8,128)(2,1)S(1)}, u32[]{:S(2)}, u32[]{:S(2)}) collective-permute-start(bf16[96,512]{1,0:T(8,128)(2,1)S(1)} %partial_sum.8), channel_id=1, source_target_pairs={{0,6},{2,18},{4,20},{6,0},{8,14},{10,26},{12,28},{14,8},{16,22},{1... | collective-permute-start | bytes 294920 | tf_op jit(solution)/shard_map/ppermute | solution.py:423
  29.2 5.6 %collective-permute-start.7 = (bf16[96,512]{1,0:T(8,128)(2,1)S(1)}, bf16[96,512]{1,0:T(8,128)(2,1)S(1)}, u32[]{:S(2)}, u32[]{:S(2)}) collective-permute-start(bf16[96,512]{1,0:T(8,128)(2,1)S(1)} %get-tuple-element.24.shard_ref), channel_id=1, source_target_pairs={{0,6},{2,18},{4,20},{6,0},{8,14},{10,26},{12,28},{14,8},{16,22},{1... | collective-permute-start | bytes 294920 | tf_op jit(solution)/shard_map/ppermute | solution.py:423
  34.9 5.7 %collective-permute-start.8 = (bf16[192,512]{1,0:T(8,128)(2,1)S(1)}, bf16[192,512]{1,0:T(8,128)(2,1)S(1)}, u32[]{:S(2)}, u32[]{:S(2)}) collective-permute-start(bf16[192,512]{1,0:T(8,128)(2,1)S(1)} %joined.6.shard_ref), channel_id=1, source_target_pairs={{0,16},{2,10},{4,12},{6,22},{8,24},{10,2},{12,4},{14,30},{16,0},{1... | collective-permute-start | bytes 589832 | tf_op jit(solution)/shard_map/ppermute | solution.py:423
  40.7 7.3 %collective-permute-start.9 = (bf16[384,512]{1,0:T(8,128)(2,1)S(1)}, bf16[384,512]{1,0:T(8,128)(2,1)S(1)}, u32[]{:S(2)}, u32[]{:S(2)}) collective-permute-start(bf16[384,512]{1,0:T(8,128)(2,1)S(1)} %joined.7.shard_ref), channel_id=1, source_target_pairs={{0,8},{2,4},{4,2},{6,14},{8,0},{10,12},{12,10},{14,6},{16,24},{18,... | collective-permute-start | bytes 1179656 | tf_op jit(solution)/shard_map/ppermute | solution.py:423
  55.3 47.2 %collective-permute-start.12 = (bf16[256,2560]{1,0:T(8,128)(2,1)S(1)}, bf16[256,2560]{1,0:T(8,128)(2,1)S(1)}, u32[]{:S(2)}, u32[]{:S(2)}) collective-permute-start(bf16[256,2560]{1,0:T(8,128)(2,1)S(1)} %piece_for.1), channel_id=1, source_target_pairs={{0,1},{1,0},{2,3},{3,2},{4,5},{5,4},{6,7},{7,6},{8,9},{9,8},{10,11... | collective-permute-start | bytes 3932168 | tf_op jit(solution)/shard_map/ppermute | solution.py:593
  56.2 7.3 %collective-permute-start.20 = (bf16[384,512]{1,0:T(8,128)(2,1)S(1)}, bf16[384,512]{1,0:T(8,128)(2,1)S(1)}, u32[]{:S(2)}, u32[]{:S(2)}) collective-permute-start(bf16[384,512]{1,0:T(8,128)(2,1)S(1)} %partial_sum.9), channel_id=1, source_target_pairs={{0,8},{2,4},{4,2},{6,14},{8,0},{10,12},{12,10},{14,6},{16,24},{18,... | collective-permute-start | bytes 1179656 | tf_op jit(solution)/shard_map/ppermute | solution.py:423
  56.6 43.0 %collective-permute-start.15 = (bf16[2,512,512]{2,1,0:T(8,128)(2,1)S(1)}, bf16[2,512,512]{2,1,0:T(8,128)(2,1)S(1)}, u32[]{:S(2)}, u32[]{:S(2)}) collective-permute-start(bf16[2,512,512]{2,1,0:T(8,128)(2,1)S(1)} %get-tuple-element.20.kv), channel_id=1, source_target_pairs={{2,4},{4,2},{10,12},{12,10},{18,20},{20,18},{26,28},{28,26},{3,5},... | collective-permute-start | bytes 3145736 | tf_op jit(solution)/shard_map/ppermute | solution.py:583
  63.6 7.2 %collective-permute-start.21 = (bf16[192,512]{1,0:T(8,128)(2,1)S(1)}, bf16[192,512]{1,0:T(8,128)(2,1)S(1)}, u32[]{:S(2)}, u32[]{:S(2)}) collective-permute-start(bf16[192,512]{1,0:T(8,128)(2,1)S(1)} %partial_sum.10), channel_id=1, source_target_pairs={{0,16},{2,10},{4,12},{6,22},{8,24},{10,2},{12,4},{14,30},{16,0},{1... | collective-permute-start | bytes 589832 | tf_op jit(solution)/shard_map/ppermute | solution.py:423
  70.8 7.0 %collective-permute-start.22 = (bf16[96,512]{1,0:T(8,128)(2,1)S(1)}, bf16[96,512]{1,0:T(8,128)(2,1)S(1)}, u32[]{:S(2)}, u32[]{:S(2)}) collective-permute-start(bf16[96,512]{1,0:T(8,128)(2,1)S(1)} %partial_sum.11), channel_id=1, source_target_pairs={{0,6},{2,18},{4,20},{6,0},{8,14},{10,26},{12,28},{14,8},{16,22},{1... | collective-permute-start | bytes 294920 | tf_op jit(solution)/shard_map/ppermute | solution.py:423
  74.9 23.1 %collective-permute-start.17 = (bf16[512,512]{1,0:T(8,128)(2,1)S(1)}, bf16[512,512]{1,0:T(8,128)(2,1)S(1)}, u32[]{:S(2)}, u32[]{:S(2)}) collective-permute-start(bf16[512,512]{1,0:T(8,128)(2,1)S(1)} %get-tuple-element.26), channel_id=1, source_target_pairs={{6,8},{8,6},{14,16},{16,14},{22,24},{24,22},{7,9},{9,7},{15,17},{1... | collective-permute-start | bytes 1572872 | tf_op jit(solution)/shard_map/ppermute | solution.py:586
  78.6 6.6 %collective-permute-start.23 = (bf16[96,512]{1,0:T(8,128)(2,1)S(1)}, bf16[96,512]{1,0:T(8,128)(2,1)S(1)}, u32[]{:S(2)}, u32[]{:S(2)}) collective-permute-start(bf16[96,512]{1,0:T(8,128)(2,1)S(1)} %get-tuple-element.30.shard_ref), channel_id=1, source_target_pairs={{0,6},{2,18},{4,20},{6,0},{8,14},{10,26},{12,28},{14,8},{16,22},{1... | collective-permute-start | bytes 294920 | tf_op jit(solution)/shard_map/ppermute | solution.py:423
  82.0 16.9 %collective-permute-start.16 = (bf16[512,512]{1,0:T(8,128)(2,1)S(1)}, bf16[512,512]{1,0:T(8,128)(2,1)S(1)}, u32[]{:S(2)}, u32[]{:S(2)}) collective-permute-start(bf16[512,512]{1,0:T(8,128)(2,1)S(1)} %get-tuple-element.25), channel_id=1, source_target_pairs={{6,8},{8,6},{14,16},{16,14},{22,24},{24,22},{7,9},{9,7},{15,17},{1... | collective-permute-start | bytes 1572872 | tf_op jit(solution)/shard_map/ppermute | solution.py:586
  85.3 7.8 %collective-permute-start.24 = (bf16[192,512]{1,0:T(8,128)(2,1)S(1)}, bf16[192,512]{1,0:T(8,128)(2,1)S(1)}, u32[]{:S(2)}, u32[]{:S(2)}) collective-permute-start(bf16[192,512]{1,0:T(8,128)(2,1)S(1)} %joined.9.shard_ref), channel_id=1, source_target_pairs={{0,16},{2,10},{4,12},{6,22},{8,24},{10,2},{12,4},{14,30},{16,0},{1... | collective-permute-start | bytes 589832 | tf_op jit(solution)/shard_map/ppermute | solution.py:423
  93.1 23.5 %collective-permute-start.14 = (bf16[2,512,512]{2,1,0:T(8,128)(2,1)S(1)}, bf16[2,512,512]{2,1,0:T(8,128)(2,1)S(1)}, u32[]{:S(2)}, u32[]{:S(2)}) collective-permute-start(bf16[2,512,512]{2,1,0:T(8,128)(2,1)S(1)} %get-tuple-element.20.kv), channel_id=1, source_target_pairs={{0,2},{2,0},{4,6},{6,4},{8,10},{10,8},{12,14},{14,12},{16,18},{18,... | collective-permute-start | bytes 3145736 | tf_op jit(solution)/shard_map/ppermute | solution.py:582
  98.1 18.5 %collective-permute-start.25 = (bf16[384,512]{1,0:T(8,128)(2,1)S(1)}, bf16[384,512]{1,0:T(8,128)(2,1)S(1)}, u32[]{:S(2)}, u32[]{:S(2)}) collective-permute-start(bf16[384,512]{1,0:T(8,128)(2,1)S(1)} %joined.10.shard_ref), channel_id=1, source_target_pairs={{0,8},{2,4},{4,2},{6,14},{8,0},{10,12},{12,10},{14,6},{16,24},{18,... | collective-permute-start | bytes 1179656 | tf_op jit(solution)/shard_map/ppermute | solution.py:423
  98.9 25.4 %collective-permute-start.2 = (bf16[2,512,512]{2,1,0:T(8,128)(2,1)S(1)}, bf16[2,512,512]{2,1,0:T(8,128)(2,1)S(1)}, u32[]{:S(2)}, u32[]{:S(2)}) collective-permute-start(bf16[2,512,512]{2,1,0:T(8,128)(2,1)S(1)} %get-tuple-element.19.kv), channel_id=1, source_target_pairs={{6,8},{8,6},{14,16},{16,14},{22,24},{24,22},{7,9},{9,7},{15,17},{1... | collective-permute-start | bytes 3145736 | tf_op jit(solution)/shard_map/ppermute | solution.py:586
  99.6 28.2 %collective-permute-start.1 = (bf16[2,512,512]{2,1,0:T(8,128)(2,1)S(1)}, bf16[2,512,512]{2,1,0:T(8,128)(2,1)S(1)}, u32[]{:S(2)}, u32[]{:S(2)}) collective-permute-start(bf16[2,512,512]{2,1,0:T(8,128)(2,1)S(1)} %get-tuple-element.19.kv), channel_id=1, source_target_pairs={{2,4},{4,2},{10,12},{12,10},{18,20},{20,18},{26,28},{28,26},{3,5},... | collective-permute-start | bytes 3145736 | tf_op jit(solution)/shard_map/ppermute | solution.py:583
  102.6 25.3 %collective-permute-start = (bf16[2,512,512]{2,1,0:T(8,128)(2,1)S(1)}, bf16[2,512,512]{2,1,0:T(8,128)(2,1)S(1)}, u32[]{:S(2)}, u32[]{:S(2)}) collective-permute-start(bf16[2,512,512]{2,1,0:T(8,128)(2,1)S(1)} %get-tuple-element.19.kv), channel_id=1, source_target_pairs={{0,2},{2,0},{4,6},{6,4},{8,10},{10,8},{12,14},{14,12},{16,18},{18,... | collective-permute-start | bytes 3145736 | tf_op jit(solution)/shard_map/ppermute | solution.py:582
  116.6 22.5 %collective-permute-start.13 = (bf16[256,2560]{1,0:T(8,128)(2,1)S(1)}, bf16[256,2560]{1,0:T(8,128)(2,1)S(1)}, u32[]{:S(2)}, u32[]{:S(2)}) collective-permute-start(bf16[256,2560]{1,0:T(8,128)(2,1)S(1)} %collective-permute-done.12.refs_3_), channel_id=1, source_target_pairs={{0,2},{2,0},{4,6},{6,4},{8,10},{10,8},{12,14},{14,12},{16,18},{18,... | collective-permute-start | bytes 3932168 | tf_op jit(solution)/shard_map/ppermute | solution.py:595
  116.7 39.2 %collective-permute-start.26 = (bf16[768,512]{1,0:T(8,128)(2,1)S(1)}, bf16[768,512]{1,0:T(8,128)(2,1)S(1)}, u32[]{:S(2)}, u32[]{:S(2)}) collective-permute-start(bf16[768,512]{1,0:T(8,128)(2,1)S(1)} %joined.11.mine_ref), channel_id=1, source_target_pairs={{0,2},{2,0},{4,6},{6,4},{8,10},{10,8},{12,14},{14,12},{16,18},{18,... | collective-permute-start | bytes 2359304 | tf_op jit(solution)/shard_map/ppermute | solution.py:519
  124.3 14.9 %collective-permute-start.18 = (bf16[512,512]{1,0:T(8,128)(2,1)S(1)}, bf16[512,512]{1,0:T(8,128)(2,1)S(1)}, u32[]{:S(2)}, u32[]{:S(2)}) collective-permute-start(bf16[512,512]{1,0:T(8,128)(2,1)S(1)} %query_side.3.refs_0_), channel_id=1, source_target_pairs={{0,1},{1,0},{2,3},{3,2},{4,5},{5,4},{6,7},{7,6},{8,9},{9,8},{10,11... | collective-permute-start | bytes 1572872 | tf_op jit(solution)/shard_map/ppermute | solution.py:610
  134.6 14.8 %collective-permute-start.11 = (bf16[512,512]{1,0:T(8,128)(2,1)S(1)}, bf16[512,512]{1,0:T(8,128)(2,1)S(1)}, u32[]{:S(2)}, u32[]{:S(2)}) collective-permute-start(bf16[512,512]{1,0:T(8,128)(2,1)S(1)} %query_side.2.refs_0_), channel_id=1, source_target_pairs={{0,1},{1,0},{2,3},{3,2},{4,5},{5,4},{6,7},{7,6},{8,9},{9,8},{10,11... | collective-permute-start | bytes 1572872 | tf_op jit(solution)/shard_map/ppermute | solution.py:610
  (5 other events, 13.4 us)

commit v5 on v4

--- a/solution.py
+++ b/solution.py
@@ -60,7 +60,7 @@
     hidden = width
     rows = 3 * hidden
     half = rows // 2
-    step = min(256, tokens)
+    step = min(512, tokens)
     scale = width ** (-0.5)
     first = NN if first_group else NT
     second = NT if first_group else NN
@@ -234,7 +234,7 @@
     tokens, width = query.shape[1:]
     hidden = width
     rows = 3 * hidden
-    step = min(256, tokens)
+    step = min(512, tokens)
     scale = width ** (-0.5)
     first = NT if gathered else NN
     count = len(weights)
@@ -371,33 +371,41 @@
     )(*in_hbm(weights))
 
 
-def matrices(mine, other):
-    half, width = mine.shape
-    rows = 2 * half
-    hidden = rows // 3
-
-    def kernel(mine_ref, other_ref, a, b, c, w_ref, out_ref, sems, out_sems):
-        wait(fetch(weight_pairs((mine_ref, other_ref), w_ref, hidden, True), sems))
+def turned_half(rows_half, flip, outs):
+    half, width = rows_half.shape
+    part = half // 3
+    hidden = 2 * part
+
+    def kernel(*refs):
+        in_ref, targets, (block_ref, sems) = refs[0], refs[-5:-2], refs[-2:]
+        h = class_of(lax.axis_index("ctx"))
+        if flip:
+            h = 1 - h
         copies = []
-        for n, out in enumerate((a, b, c)):
-            out_ref[n] = w_ref[pl.ds(n * hidden, hidden)].T
-            copies += fetch([(out_ref.at[n], out.at[0])], out_sems.at[pl.ds(n, 1)])
+        for j in range(3):
+            block_ref[j] = in_ref[pl.ds(j * part, part)].T
+            for value in range(2):
+                matrix, side = divmod(3 * value + j, 2)
+                place = targets[matrix].at[0, :, pl.ds(side * part, part)]
+                copy = pltpu.make_async_copy(block_ref.at[j], place, sems.at[j])
+
+                @pl.when(h == value)
+                def _():
+                    copy.start()
+
+            copies.append(copy)
         wait(copies)
 
     return pl.pallas_call(
         kernel,
-        in_specs=[VMEM] * 2,
+        in_specs=[VMEM] + [HBM] * len(outs),
         out_specs=[HBM] * 3,
         out_shape=[jax.ShapeDtypeStruct((1, width, hidden), BF16)] * 3,
-        scratch_shapes=[
-            pltpu.VMEM((rows, width), BF16),
-            pltpu.VMEM((3, width, hidden), BF16),
-            pltpu.SemaphoreType.DMA((2,)),
-            pltpu.SemaphoreType.DMA((3,)),
-        ],
-        compiler_params=limit(10),
-        name="matrices",
-    )(mine, other)
+        input_output_aliases={n + 1: n for n in range(len(outs))},
+        scratch_shapes=[pltpu.VMEM((3, width, part), BF16), pltpu.SemaphoreType.DMA((3,))],
+        compiler_params=limit(4),
+        name="turned_half",
+    )(rows_half, *outs)
 
 
 def orders(count):
@@ -613,7 +621,10 @@
             mixed = project(outs, proj_weight, near, far, group, call, mixed)
         state, shard = next_state(state, send, keep, count)
         weights = gather_rows(shard, count)
-    return (mixed, *matrices(*weights))
+    outs = ()
+    for flip, rows_half in enumerate(weights):
+        outs = turned_half(rows_half, flip, outs)
+    return (mixed, *outs)
 
 
 def solution(mesh):

time: 160 us -> 157 us (0.981)
    ppermute x12, starting transfers between devices: 15.9 us -> 20.3 us  [exchange(): return lax.ppermute(value, 'ctx', pairs)]
    ppermute x2, starting transfers between devices: 4.95 us -> 0.55 us  [layer(): chip = lax.ppermute(edge(own, 1 - core), 'ctx', swap_pairs(count))]
where the time goes in v5:
time: 157 us; the launch traced here: 155 us
  waiting for transfers between devices  79.5 us (51%)
  Pallas kernels  42.2 us (27%)
  starting transfers between devices  32.3 us (21%)
    ppermute x12, waiting for transfers between devices, exchange(): return lax.ppermute(value, 'ctx', pairs)  66.4 us
    ppermute x12, starting transfers between devices, exchange(): return lax.ppermute(value, 'ctx', pairs)  20.3 us
    pallas_call x4, Pallas kernels, project(): pl.pallas_call(kernel, in_specs=in_specs, out_specs=HBM, out_shape=jax.Sh...  12.9 us
    pallas_call x2, Pallas kernels, window_side(): pl.pallas_call(kernel, in_specs=[HBM] * (5 + len(far)), out_specs=VMEM, o...  7.84 us
    ppermute x2, waiting for transfers between devices, layer(): lax.ppermute(head_out, 'head', [(i, (i + shift) % heads) for i in range(h...  7.08 us
    pallas_call x2, Pallas kernels, key_side(): pl.pallas_call(kernel, in_specs=in_specs, out_specs=[VMEM] * len(out_shap...  5.95 us
    ppermute x2, starting transfers between devices, layer(): near_halo = lax.ppermute(edge(own, core), 'ctx', near_pairs)  5.28 us
    pallas_call x2, Pallas kernels, query_side(): pl.pallas_call(kernel, in_specs=[HBM, VMEM, VMEM] + [VMEM if gathered els...  5.17 us
  transfers between devices with their start and end apart: 27, of which 18 were waited for; matrix products, arithmetic and copies ran while one was open for 0% of the time, Pallas kernels for 21%

profile of v5, /device:TPU:14, one launch (start us, length us, event | category | flops | bytes accessed | tf_op | source)
XLA Modules:
  0.0 155.1 jit_solution(18431310398988381747)
XLA Ops:
  2.5 2.9 %key_side.2 = (bf16[768,512]{1,0:T(8,128)(2,1)S(1)}, f32[768,512]{1,0:T(8,128)S(1)}) custom-call(bf16[2,512,512]{2,1,0:T(8,128)(2,1)S(1)} %get-tuple-element.23.kv, f32[2,1,512]{2,1,0:T(1,128)S(1)} %copy-done, bf16[1536,512]{1,0:T(8,128)(2,1)S(1)} %get-tuple-element.24.refs_0_), custom_call_target="tpu_custom_call" | custom-call | tf_op jit(solution)/shard_map/key_side/pallas_call | solution.py:121
  8.2 6.9 %collective-permute-done.4.refs_2_ = bf16[384,512]{1,0:T(8,128)(2,1)S(1)} collective-permute-done((bf16[384,512]{1,0:T(8,128)(2,1)S(1)}, bf16[384,512]{1,0:T(8,128)(2,1)S(1)}, u32[]{:S(2)}, u32[]{:S(2)}) %collective-permute-start.4) | collective-permute-done | bytes 393248 | tf_op jit(solution)/shard_map/ppermute | solution.py:431
  15.7 7.2 %collective-permute-done.5.refs_3_ = bf16[192,512]{1,0:T(8,128)(2,1)S(1)} collective-permute-done((bf16[192,512]{1,0:T(8,128)(2,1)S(1)}, bf16[192,512]{1,0:T(8,128)(2,1)S(1)}, u32[]{:S(2)}, u32[]{:S(2)}) %collective-permute-start.5) | collective-permute-done | bytes 196640 | tf_op jit(solution)/shard_map/ppermute | solution.py:431
  31.4 3.0 %collective-permute-done.7.got_ref = bf16[96,512]{1,0:T(8,128)(2,1)S(1)} collective-permute-done((bf16[96,512]{1,0:T(8,128)(2,1)S(1)}, bf16[96,512]{1,0:T(8,128)(2,1)S(1)}, u32[]{:S(2)}, u32[]{:S(2)}) %collective-permute-start.7) | collective-permute-done | bytes 98336 | tf_op jit(solution)/shard_map/ppermute | solution.py:431
  34.7 5.5 %collective-permute-done.8.got_ref = bf16[192,512]{1,0:T(8,128)(2,1)S(1)} collective-permute-done((bf16[192,512]{1,0:T(8,128)(2,1)S(1)}, bf16[192,512]{1,0:T(8,128)(2,1)S(1)}, u32[]{:S(2)}, u32[]{:S(2)}) %collective-permute-start.8) | collective-permute-done | bytes 196640 | tf_op jit(solution)/shard_map/ppermute | solution.py:431
  40.3 7.2 %collective-permute-done.9.got_ref = bf16[384,512]{1,0:T(8,128)(2,1)S(1)} collective-permute-done((bf16[384,512]{1,0:T(8,128)(2,1)S(1)}, bf16[384,512]{1,0:T(8,128)(2,1)S(1)}, u32[]{:S(2)}, u32[]{:S(2)}) %collective-permute-start.9) | collective-permute-done | bytes 393248 | tf_op jit(solution)/shard_map/ppermute | solution.py:431
  49.9 3.1 %key_side.3 = (bf16[768,512]{1,0:T(8,128)(2,1)S(1)}, f32[768,512]{1,0:T(8,128)S(1)}) custom-call(bf16[2,512,512]{2,1,0:T(8,128)(2,1)S(1)} %get-tuple-element.22.kv, f32[2,1,512]{2,1,0:T(1,128)S(1)} %copy-done, bf16[768,512]{1,0:T(8,128)(2,1)S(1)} %joined.8.refs_0_, bf16[768,512]{1,0:T(8,128)(2,1)S(1)} %collective-permute-done.10.refs_1_), custom_call_target="tpu_custom_call" | custom-call | tf_op jit(solution)/shard_map/key_side/pallas_call | solution.py:121
  55.8 3.3 %collective-permute-start.15 = (bf16[2,512,512]{2,1,0:T(8,128)(2,1)S(1)}, bf16[2,512,512]{2,1,0:T(8,128)(2,1)S(1)}, u32[]{:S(2)}, u32[]{:S(2)}) collective-permute-start(bf16[2,512,512]{2,1,0:T(8,128)(2,1)S(1)} %get-tuple-element.23.kv), channel_id=1, source_target_pairs={{2,4},{4,2},{10,12},{12,10},{18,20},{20,18},{26,28},{28,26},{3,5},... | collective-permute-start | bytes 3145736 | tf_op jit(solution)/shard_map/ppermute | solution.py:591
  59.2 3.6 %collective-permute-done.20.refs_2_ = bf16[384,512]{1,0:T(8,128)(2,1)S(1)} collective-permute-done((bf16[384,512]{1,0:T(8,128)(2,1)S(1)}, bf16[384,512]{1,0:T(8,128)(2,1)S(1)}, u32[]{:S(2)}, u32[]{:S(2)}) %collective-permute-start.20) | collective-permute-done | bytes 393248 | tf_op jit(solution)/shard_map/ppermute | solution.py:431
  64.2 5.8 %collective-permute-done.21.refs_3_ = bf16[192,512]{1,0:T(8,128)(2,1)S(1)} collective-permute-done((bf16[192,512]{1,0:T(8,128)(2,1)S(1)}, bf16[192,512]{1,0:T(8,128)(2,1)S(1)}, u32[]{:S(2)}, u32[]{:S(2)}) %collective-permute-start.21) | collective-permute-done | bytes 196640 | tf_op jit(solution)/shard_map/ppermute | solution.py:431
  70.0 5.5 %collective-permute-start.22 = (bf16[96,512]{1,0:T(8,128)(2,1)S(1)}, bf16[96,512]{1,0:T(8,128)(2,1)S(1)}, u32[]{:S(2)}, u32[]{:S(2)}) collective-permute-start(bf16[96,512]{1,0:T(8,128)(2,1)S(1)} %partial_sum.11), channel_id=1, source_target_pairs={{0,6},{2,18},{4,20},{6,0},{8,14},{10,26},{12,28},{14,8},{16,22},{1... | collective-permute-start | bytes 294920 | tf_op jit(solution)/shard_map/ppermute | solution.py:431
  79.1 3.4 %collective-permute-start.23 = (bf16[96,512]{1,0:T(8,128)(2,1)S(1)}, bf16[96,512]{1,0:T(8,128)(2,1)S(1)}, u32[]{:S(2)}, u32[]{:S(2)}) collective-permute-start(bf16[96,512]{1,0:T(8,128)(2,1)S(1)} %get-tuple-element.33.shard_ref), channel_id=1, source_target_pairs={{0,6},{2,18},{4,20},{6,0},{8,14},{10,26},{12,28},{14,8},{16,22},{1... | collective-permute-start | bytes 294920 | tf_op jit(solution)/shard_map/ppermute | solution.py:431
  85.2 7.8 %collective-permute-done.24.got_ref = bf16[192,512]{1,0:T(8,128)(2,1)S(1)} collective-permute-done((bf16[192,512]{1,0:T(8,128)(2,1)S(1)}, bf16[192,512]{1,0:T(8,128)(2,1)S(1)}, u32[]{:S(2)}, u32[]{:S(2)}) %collective-permute-start.24) | collective-permute-done | bytes 196640 | tf_op jit(solution)/shard_map/ppermute | solution.py:431
  93.3 3.9 %collective-permute-start.25 = (bf16[384,512]{1,0:T(8,128)(2,1)S(1)}, bf16[384,512]{1,0:T(8,128)(2,1)S(1)}, u32[]{:S(2)}, u32[]{:S(2)}) collective-permute-start(bf16[384,512]{1,0:T(8,128)(2,1)S(1)} %joined.10.shard_ref), channel_id=1, source_target_pairs={{0,8},{2,4},{4,2},{6,14},{8,0},{10,12},{12,10},{14,6},{16,24},{18,... | collective-permute-start | bytes 1179656 | tf_op jit(solution)/shard_map/ppermute | solution.py:431
  100.1 13.8 %collective-permute-done.25.got_ref = bf16[384,512]{1,0:T(8,128)(2,1)S(1)} collective-permute-done((bf16[384,512]{1,0:T(8,128)(2,1)S(1)}, bf16[384,512]{1,0:T(8,128)(2,1)S(1)}, u32[]{:S(2)}, u32[]{:S(2)}) %collective-permute-start.25) | collective-permute-done | bytes 393248 | tf_op jit(solution)/shard_map/ppermute | solution.py:431
  114.6 3.8 %window_side.3.window_ref = f32[512,512]{1,0:T(8,128)S(1)} custom-call(bf16[2,512,512]{2,1,0:T(8,128)(2,1)} %q_in.7, bf16[2,512,512]{2,1,0:T(8,128)(2,1)} %k_in.3, bf16[2,512,512]{2,1,0:T(8,128)(2,1)} %v_in.3, bf16[2,512,512]{2,1,0:T(8,128)(2,1)S(1)} %collective-permute-done.14.chip_ref, bf16[2,512,512]{2,1,0:T(8,128)(2,1)S(1)} %collective-permute-done.15.near_ref, ...), custom_call_target="tpu_custom_call" | custom-call | tf_op jit(solution)/shard_map/window_side/pallas_call | solution.py:216
  118.4 2.8 %query_side.3.refs_0_ = bf16[512,512]{1,0:T(8,128)(2,1)S(1)} custom-call(bf16[2,512,512]{2,1,0:T(8,128)(2,1)} %q_in.7, f32[1,512]{1,0:T(1,128)S(1)} %copy-done.1, f32[512,512]{1,0:T(8,128)S(1)} %window_side.3.window_ref, bf16[1,512,512]{2,1,0:T(8,128)(2,1)} %refs_0_.7, bf16[1,512,512]{2,1,0:T(8,128)(2,1)} %refs_1_.7, bf16[1,512,512]{2,1,0:T(8,128)(2,1)} %refs_2_.9), custom_call_target="tpu_custom_call" | custom-call | tf_op jit(solution)/shard_map/query_side/pallas_call | solution.py:262
  125.1 4.0 %window_side.2.window_ref = f32[512,512]{1,0:T(8,128)S(1)} custom-call(bf16[2,512,512]{2,1,0:T(8,128)(2,1)} %q_in.7, bf16[2,512,512]{2,1,0:T(8,128)(2,1)} %k_in.3, bf16[2,512,512]{2,1,0:T(8,128)(2,1)} %v_in.3, bf16[2,512,512]{2,1,0:T(8,128)(2,1)S(1)} %collective-permute-done.chip_ref, bf16[2,512,512]{2,1,0:T(8,128)(2,1)S(1)} %collective-permute-done.1.near_ref, ...), custom_call_target="tpu_custom_call" | custom-call | tf_op jit(solution)/shard_map/window_side/pallas_call | solution.py:216
  132.8 3.3 %collective-permute-done.18.refs_1_ = bf16[512,512]{1,0:T(8,128)(2,1)S(1)} collective-permute-done((bf16[512,512]{1,0:T(8,128)(2,1)S(1)}, bf16[512,512]{1,0:T(8,128)(2,1)S(1)}, u32[]{:S(2)}, u32[]{:S(2)}) %collective-permute-start.18) | collective-permute-done | bytes 524320 | tf_op jit(solution)/shard_map/ppermute | solution.py:618
  136.1 3.5 %project.4.refs_5_ = bf16[2,512,2560]{2,1,0:T(8,128)(2,1)} custom-call(bf16[512,512]{1,0:T(8,128)(2,1)S(1)} %query_side.3.refs_0_, bf16[512,512]{1,0:T(8,128)(2,1)S(1)} %collective-permute-done.18.refs_1_, bf16[512,5120]{1,0:T(8,128)(2,1)} %refs_2_.13, bf16[256,2560]{1,0:T(8,128)(2,1)S(1)} %collective-permute-done.12.refs_3_, ...), custom_call_target="tpu_custom_call" | custom-call | tf_op jit(solution)/shard_map/project/pallas_call | solution.py:334
  139.6 2.9 %project.5.refs_5_ = bf16[2,512,2560]{2,1,0:T(8,128)(2,1)} custom-call(bf16[512,512]{1,0:T(8,128)(2,1)S(1)} %query_side.3.refs_0_, bf16[512,512]{1,0:T(8,128)(2,1)S(1)} %collective-permute-done.18.refs_1_, bf16[512,5120]{1,0:T(8,128)(2,1)} %refs_2_.13, bf16[256,2560]{1,0:T(8,128)(2,1)S(1)} %collective-permute-done.12.refs_3_, ...), custom_call_target="tpu_custom_call", output_to_operand_aliasing={{}: (5, {})} | custom-call | tf_op jit(solution)/shard_map/project/pallas_call | solution.py:334
  142.6 3.8 %collective-permute-done.11.refs_1_ = bf16[512,512]{1,0:T(8,128)(2,1)S(1)} collective-permute-done((bf16[512,512]{1,0:T(8,128)(2,1)S(1)}, bf16[512,512]{1,0:T(8,128)(2,1)S(1)}, u32[]{:S(2)}, u32[]{:S(2)}) %collective-permute-start.11) | collective-permute-done | bytes 524320 | tf_op jit(solution)/shard_map/ppermute | solution.py:618
  146.4 3.5 %project.6.refs_5_ = bf16[2,512,2560]{2,1,0:T(8,128)(2,1)} custom-call(bf16[512,512]{1,0:T(8,128)(2,1)S(1)} %query_side.2.refs_0_, bf16[512,512]{1,0:T(8,128)(2,1)S(1)} %collective-permute-done.11.refs_1_, bf16[512,5120]{1,0:T(8,128)(2,1)} %refs_2_.13, bf16[256,2560]{1,0:T(8,128)(2,1)S(1)} %collective-permute-done.12.refs_3_, ...), custom_call_target="tpu_custom_call", output_to_operand_aliasing={{}: (5, {})} | custom-call | tf_op jit(solution)/shard_map/project/pallas_call | solution.py:334
  149.9 2.9 %project.7 = bf16[2,512,2560]{2,1,0:T(8,128)(2,1)} custom-call(bf16[512,512]{1,0:T(8,128)(2,1)S(1)} %query_side.2.refs_0_, bf16[512,512]{1,0:T(8,128)(2,1)S(1)} %collective-permute-done.11.refs_1_, bf16[512,5120]{1,0:T(8,128)(2,1)} %refs_2_.13, bf16[256,2560]{1,0:T(8,128)(2,1)S(1)} %collective-permute-done.12.refs_3_, ...), custom_call_target="tpu_custom_call", output_to_operand_aliasing={{}: (5, {})} | custom-call | tf_op jit(solution)/shard_map/project/pallas_call | solution.py:334
  (64 shorter events, 40.6 us)
Async XLA Ops:
  7.9 7.3 %collective-permute-start.4 = (bf16[384,512]{1,0:T(8,128)(2,1)S(1)}, bf16[384,512]{1,0:T(8,128)(2,1)S(1)}, u32[]{:S(2)}, u32[]{:S(2)}) collective-permute-start(bf16[384,512]{1,0:T(8,128)(2,1)S(1)} %partial_sum.6), channel_id=1, source_target_pairs={{0,8},{2,4},{4,2},{6,14},{8,0},{10,12},{12,10},{14,6},{16,24},{18,... | collective-permute-start | bytes 1179656 | tf_op jit(solution)/shard_map/ppermute | solution.py:431
  15.2 7.7 %collective-permute-start.5 = (bf16[192,512]{1,0:T(8,128)(2,1)S(1)}, bf16[192,512]{1,0:T(8,128)(2,1)S(1)}, u32[]{:S(2)}, u32[]{:S(2)}) collective-permute-start(bf16[192,512]{1,0:T(8,128)(2,1)S(1)} %partial_sum.7), channel_id=1, source_target_pairs={{0,16},{2,10},{4,12},{6,22},{8,24},{10,2},{12,4},{14,30},{16,0},{1... | collective-permute-start | bytes 589832 | tf_op jit(solution)/shard_map/ppermute | solution.py:431
  23.0 5.6 %collective-permute-start.6 = (bf16[96,512]{1,0:T(8,128)(2,1)S(1)}, bf16[96,512]{1,0:T(8,128)(2,1)S(1)}, u32[]{:S(2)}, u32[]{:S(2)}) collective-permute-start(bf16[96,512]{1,0:T(8,128)(2,1)S(1)} %partial_sum.8), channel_id=1, source_target_pairs={{0,6},{2,18},{4,20},{6,0},{8,14},{10,26},{12,28},{14,8},{16,22},{1... | collective-permute-start | bytes 294920 | tf_op jit(solution)/shard_map/ppermute | solution.py:431
  28.8 5.6 %collective-permute-start.7 = (bf16[96,512]{1,0:T(8,128)(2,1)S(1)}, bf16[96,512]{1,0:T(8,128)(2,1)S(1)}, u32[]{:S(2)}, u32[]{:S(2)}) collective-permute-start(bf16[96,512]{1,0:T(8,128)(2,1)S(1)} %get-tuple-element.27.shard_ref), channel_id=1, source_target_pairs={{0,6},{2,18},{4,20},{6,0},{8,14},{10,26},{12,28},{14,8},{16,22},{1... | collective-permute-start | bytes 294920 | tf_op jit(solution)/shard_map/ppermute | solution.py:431
  34.5 5.7 %collective-permute-start.8 = (bf16[192,512]{1,0:T(8,128)(2,1)S(1)}, bf16[192,512]{1,0:T(8,128)(2,1)S(1)}, u32[]{:S(2)}, u32[]{:S(2)}) collective-permute-start(bf16[192,512]{1,0:T(8,128)(2,1)S(1)} %joined.6.shard_ref), channel_id=1, source_target_pairs={{0,16},{2,10},{4,12},{6,22},{8,24},{10,2},{12,4},{14,30},{16,0},{1... | collective-permute-start | bytes 589832 | tf_op jit(solution)/shard_map/ppermute | solution.py:431
  40.2 7.3 %collective-permute-start.9 = (bf16[384,512]{1,0:T(8,128)(2,1)S(1)}, bf16[384,512]{1,0:T(8,128)(2,1)S(1)}, u32[]{:S(2)}, u32[]{:S(2)}) collective-permute-start(bf16[384,512]{1,0:T(8,128)(2,1)S(1)} %joined.7.shard_ref), channel_id=1, source_target_pairs={{0,8},{2,4},{4,2},{6,14},{8,0},{10,12},{12,10},{14,6},{16,24},{18,... | collective-permute-start | bytes 1179656 | tf_op jit(solution)/shard_map/ppermute | solution.py:431
  54.5 45.3 %collective-permute-start.12 = (bf16[256,2560]{1,0:T(8,128)(2,1)S(1)}, bf16[256,2560]{1,0:T(8,128)(2,1)S(1)}, u32[]{:S(2)}, u32[]{:S(2)}) collective-permute-start(bf16[256,2560]{1,0:T(8,128)(2,1)S(1)} %piece_for.1), channel_id=1, source_target_pairs={{0,1},{1,0},{2,3},{3,2},{4,5},{5,4},{6,7},{7,6},{8,9},{9,8},{10,11... | collective-permute-start | bytes 3932168 | tf_op jit(solution)/shard_map/ppermute | solution.py:601
  55.5 7.3 %collective-permute-start.20 = (bf16[384,512]{1,0:T(8,128)(2,1)S(1)}, bf16[384,512]{1,0:T(8,128)(2,1)S(1)}, u32[]{:S(2)}, u32[]{:S(2)}) collective-permute-start(bf16[384,512]{1,0:T(8,128)(2,1)S(1)} %partial_sum.9), channel_id=1, source_target_pairs={{0,8},{2,4},{4,2},{6,14},{8,0},{10,12},{12,10},{14,6},{16,24},{18,... | collective-permute-start | bytes 1179656 | tf_op jit(solution)/shard_map/ppermute | solution.py:431
  55.8 42.1 %collective-permute-start.15 = (bf16[2,512,512]{2,1,0:T(8,128)(2,1)S(1)}, bf16[2,512,512]{2,1,0:T(8,128)(2,1)S(1)}, u32[]{:S(2)}, u32[]{:S(2)}) collective-permute-start(bf16[2,512,512]{2,1,0:T(8,128)(2,1)S(1)} %get-tuple-element.23.kv), channel_id=1, source_target_pairs={{2,4},{4,2},{10,12},{12,10},{18,20},{20,18},{26,28},{28,26},{3,5},... | collective-permute-start | bytes 3145736 | tf_op jit(solution)/shard_map/ppermute | solution.py:591
  62.8 7.2 %collective-permute-start.21 = (bf16[192,512]{1,0:T(8,128)(2,1)S(1)}, bf16[192,512]{1,0:T(8,128)(2,1)S(1)}, u32[]{:S(2)}, u32[]{:S(2)}) collective-permute-start(bf16[192,512]{1,0:T(8,128)(2,1)S(1)} %partial_sum.10), channel_id=1, source_target_pairs={{0,16},{2,10},{4,12},{6,22},{8,24},{10,2},{12,4},{14,30},{16,0},{1... | collective-permute-start | bytes 589832 | tf_op jit(solution)/shard_map/ppermute | solution.py:431
  63.5 29.8 %collective-permute-start.17 = (bf16[512,512]{1,0:T(8,128)(2,1)S(1)}, bf16[512,512]{1,0:T(8,128)(2,1)S(1)}, u32[]{:S(2)}, u32[]{:S(2)}) collective-permute-start(bf16[512,512]{1,0:T(8,128)(2,1)S(1)} %get-tuple-element.29), channel_id=1, source_target_pairs={{6,8},{8,6},{14,16},{16,14},{22,24},{24,22},{7,9},{9,7},{15,17},{1... | collective-permute-start | bytes 1572872 | tf_op jit(solution)/shard_map/ppermute | solution.py:594
  70.0 8.2 %collective-permute-start.22 = (bf16[96,512]{1,0:T(8,128)(2,1)S(1)}, bf16[96,512]{1,0:T(8,128)(2,1)S(1)}, u32[]{:S(2)}, u32[]{:S(2)}) collective-permute-start(bf16[96,512]{1,0:T(8,128)(2,1)S(1)} %partial_sum.11), channel_id=1, source_target_pairs={{0,6},{2,18},{4,20},{6,0},{8,14},{10,26},{12,28},{14,8},{16,22},{1... | collective-permute-start | bytes 294920 | tf_op jit(solution)/shard_map/ppermute | solution.py:431
  79.1 6.0 %collective-permute-start.23 = (bf16[96,512]{1,0:T(8,128)(2,1)S(1)}, bf16[96,512]{1,0:T(8,128)(2,1)S(1)}, u32[]{:S(2)}, u32[]{:S(2)}) collective-permute-start(bf16[96,512]{1,0:T(8,128)(2,1)S(1)} %get-tuple-element.33.shard_ref), channel_id=1, source_target_pairs={{0,6},{2,18},{4,20},{6,0},{8,14},{10,26},{12,28},{14,8},{16,22},{1... | collective-permute-start | bytes 294920 | tf_op jit(solution)/shard_map/ppermute | solution.py:431
  82.4 14.7 %collective-permute-start.16 = (bf16[512,512]{1,0:T(8,128)(2,1)S(1)}, bf16[512,512]{1,0:T(8,128)(2,1)S(1)}, u32[]{:S(2)}, u32[]{:S(2)}) collective-permute-start(bf16[512,512]{1,0:T(8,128)(2,1)S(1)} %get-tuple-element.28), channel_id=1, source_target_pairs={{6,8},{8,6},{14,16},{16,14},{22,24},{24,22},{7,9},{9,7},{15,17},{1... | collective-permute-start | bytes 1572872 | tf_op jit(solution)/shard_map/ppermute | solution.py:594
  85.1 7.8 %collective-permute-start.24 = (bf16[192,512]{1,0:T(8,128)(2,1)S(1)}, bf16[192,512]{1,0:T(8,128)(2,1)S(1)}, u32[]{:S(2)}, u32[]{:S(2)}) collective-permute-start(bf16[192,512]{1,0:T(8,128)(2,1)S(1)} %joined.9.shard_ref), channel_id=1, source_target_pairs={{0,16},{2,10},{4,12},{6,22},{8,24},{10,2},{12,4},{14,30},{16,0},{1... | collective-permute-start | bytes 589832 | tf_op jit(solution)/shard_map/ppermute | solution.py:431
  92.9 21.1 %collective-permute-start.14 = (bf16[2,512,512]{2,1,0:T(8,128)(2,1)S(1)}, bf16[2,512,512]{2,1,0:T(8,128)(2,1)S(1)}, u32[]{:S(2)}, u32[]{:S(2)}) collective-permute-start(bf16[2,512,512]{2,1,0:T(8,128)(2,1)S(1)} %get-tuple-element.23.kv), channel_id=1, source_target_pairs={{0,2},{2,0},{4,6},{6,4},{8,10},{10,8},{12,14},{14,12},{16,18},{18,... | collective-permute-start | bytes 3145736 | tf_op jit(solution)/shard_map/ppermute | solution.py:590
  93.3 20.6 %collective-permute-start.25 = (bf16[384,512]{1,0:T(8,128)(2,1)S(1)}, bf16[384,512]{1,0:T(8,128)(2,1)S(1)}, u32[]{:S(2)}, u32[]{:S(2)}) collective-permute-start(bf16[384,512]{1,0:T(8,128)(2,1)S(1)} %joined.10.shard_ref), channel_id=1, source_target_pairs={{0,8},{2,4},{4,2},{6,14},{8,0},{10,12},{12,10},{14,6},{16,24},{18,... | collective-permute-start | bytes 1179656 | tf_op jit(solution)/shard_map/ppermute | solution.py:431
  97.2 24.0 %collective-permute-start.2 = (bf16[2,512,512]{2,1,0:T(8,128)(2,1)S(1)}, bf16[2,512,512]{2,1,0:T(8,128)(2,1)S(1)}, u32[]{:S(2)}, u32[]{:S(2)}) collective-permute-start(bf16[2,512,512]{2,1,0:T(8,128)(2,1)S(1)} %get-tuple-element.22.kv), channel_id=1, source_target_pairs={{6,8},{8,6},{14,16},{16,14},{22,24},{24,22},{7,9},{9,7},{15,17},{1... | collective-permute-start | bytes 3145736 | tf_op jit(solution)/shard_map/ppermute | solution.py:594
  97.9 27.2 %collective-permute-start.1 = (bf16[2,512,512]{2,1,0:T(8,128)(2,1)S(1)}, bf16[2,512,512]{2,1,0:T(8,128)(2,1)S(1)}, u32[]{:S(2)}, u32[]{:S(2)}) collective-permute-start(bf16[2,512,512]{2,1,0:T(8,128)(2,1)S(1)} %get-tuple-element.22.kv), channel_id=1, source_target_pairs={{2,4},{4,2},{10,12},{12,10},{18,20},{20,18},{26,28},{28,26},{3,5},... | collective-permute-start | bytes 3145736 | tf_op jit(solution)/shard_map/ppermute | solution.py:591
  99.9 25.2 %collective-permute-start = (bf16[2,512,512]{2,1,0:T(8,128)(2,1)S(1)}, bf16[2,512,512]{2,1,0:T(8,128)(2,1)S(1)}, u32[]{:S(2)}, u32[]{:S(2)}) collective-permute-start(bf16[2,512,512]{2,1,0:T(8,128)(2,1)S(1)} %get-tuple-element.22.kv), channel_id=1, source_target_pairs={{0,2},{2,0},{4,6},{6,4},{8,10},{10,8},{12,14},{14,12},{16,18},{18,... | collective-permute-start | bytes 3145736 | tf_op jit(solution)/shard_map/ppermute | solution.py:590
  113.9 22.2 %collective-permute-start.13 = (bf16[256,2560]{1,0:T(8,128)(2,1)S(1)}, bf16[256,2560]{1,0:T(8,128)(2,1)S(1)}, u32[]{:S(2)}, u32[]{:S(2)}) collective-permute-start(bf16[256,2560]{1,0:T(8,128)(2,1)S(1)} %collective-permute-done.12.refs_3_), channel_id=1, source_target_pairs={{0,2},{2,0},{4,6},{6,4},{8,10},{10,8},{12,14},{14,12},{16,18},{18,... | collective-permute-start | bytes 3932168 | tf_op jit(solution)/shard_map/ppermute | solution.py:603
  114.0 39.9 %collective-permute-start.26 = (bf16[768,512]{1,0:T(8,128)(2,1)S(1)}, bf16[768,512]{1,0:T(8,128)(2,1)S(1)}, u32[]{:S(2)}, u32[]{:S(2)}) collective-permute-start(bf16[768,512]{1,0:T(8,128)(2,1)S(1)} %joined.11.refs_0_), channel_id=1, source_target_pairs={{0,2},{2,0},{4,6},{6,4},{8,10},{10,8},{12,14},{14,12},{16,18},{18,... | collective-permute-start | bytes 2359304 | tf_op jit(solution)/shard_map/ppermute | solution.py:527
  121.2 14.9 %collective-permute-start.18 = (bf16[512,512]{1,0:T(8,128)(2,1)S(1)}, bf16[512,512]{1,0:T(8,128)(2,1)S(1)}, u32[]{:S(2)}, u32[]{:S(2)}) collective-permute-start(bf16[512,512]{1,0:T(8,128)(2,1)S(1)} %query_side.3.refs_0_), channel_id=1, source_target_pairs={{0,1},{1,0},{2,3},{3,2},{4,5},{5,4},{6,7},{7,6},{8,9},{9,8},{10,11... | collective-permute-start | bytes 1572872 | tf_op jit(solution)/shard_map/ppermute | solution.py:618
  131.5 14.9 %collective-permute-start.11 = (bf16[512,512]{1,0:T(8,128)(2,1)S(1)}, bf16[512,512]{1,0:T(8,128)(2,1)S(1)}, u32[]{:S(2)}, u32[]{:S(2)}) collective-permute-start(bf16[512,512]{1,0:T(8,128)(2,1)S(1)} %query_side.2.refs_0_), channel_id=1, source_target_pairs={{0,1},{1,0},{2,3},{3,2},{4,5},{5,4},{6,7},{7,6},{8,9},{9,8},{10,11... | collective-permute-start | bytes 1572872 | tf_op jit(solution)/shard_map/ppermute | solution.py:618
  (5 other events, 13.4 us)
